TPU v7x, 32 devices: a whole 2x2x4 slice. The times are simulated.
32 devices in a mesh: groups: 2 (over y), tile: 4 (over z), chan: 2 (over x), sub: 2 (over core).
Axes of the slice: x: 2, y: 2, z: 4, core: 2. Of those that a mesh axis runs over, the one named last changes fastest.
Arguments:
- cycle_maps: bfloat16 [8, 3, 65536], P(('groups', 'chan', 'sub'), None, 'tile'), parts along dimension 0, may hold values from -6 to 6
- send_pick: int32 [98304], P('tile'), may hold values from 0 to 16384, as said below
- recv_pick: int32 [65536], P('tile'), may hold values from 0 to 24575, as said below
- neighbour: int32 [4, 4], replicated, may hold values from -1 to 3, as said below
- facing: int32 [4, 4], replicated, may hold values from 0 to 3, as said below
- conv_first: bfloat16 [9, 64, 3], replicated, may hold values from -1.25 to 1.25
- conv_second: bfloat16 [9, 64, 64], replicated, may hold values from -0.25 to 0.25
- cotangent: bfloat16 [8, 64, 65536], P(('groups', 'chan', 'sub'), None, 'tile'), parts along dimension 0, may hold values from -6 to 6
Outputs:
- output_maps: bfloat16 [8, 64, 65536], P(('groups', 'chan', 'sub'), None, 'tile'), parts along dimension 0
- grad_hidden: bfloat16 [8, 64, 65536], P(('groups', 'chan', 'sub'), None, 'tile'), parts along dimension 0
- grad_first: float32 [18, 64, 3], P('groups'), parts along dimension 0
- grad_second: float32 [18, 64, 64], P('groups'), parts along dimension 0
There are 2 independent parts, one for each index of `groups`. A program takes and returns all parts, laid end to end along the dimension named above; an argument that names none is the same for every part. Nothing has to cross between parts.
Inputs may be any that keep to these rules, and one draw needn't show every extreme that they name: `send_pick`: entry ((i * 4) + d) * 6144 + s names the cycle pixel (0 to 16383, local to owner i) that owner i puts into slot s of its block for tile d, or 16384 for an empty slot; the used slots of each block are 0 to n - 1 with n at most 6144, and some block is full. Every cycle pixel is named exactly once. `recv_pick`: entry d * 16384 + q is i * 6144 + s: pixel q of tile d is carried in slot s of owner i's block for tile d, a used slot. With send_pick it maps cycle pixels one to one onto tile pixels; each tile receives from every owner. `neighbour`: the tiles form a band four tiles tall, closed east to west; each tile is turned by a multiple of a right angle. Row t lists the tile across sides north, east, south, west of tile t in its own orientation, -1 beyond the band's rim. Adjacency is mutual: if side k of t touches side j of p, side j of p touches side k of t. A tile meets one tile on at most 2 sides, and some tile on exactly that many. `facing`: the side of the neighbouring tile that touches side k of tile t; 0 where there is no neighbour.
All inputs are finite; a program needn't handle non-finite values.
Results may differ from a plain program's by a relative error of at most 0.005.
Values may be sent and summed in bfloat16 or wider, within the bound.
No kernel may reach another device: no remote copies, remote signals or barrier semaphores. Data moves between devices by JAX's collectives and lax.ppermute only.
A program may use at most 192 MiB of HBM per device.

v0:
```python
import math

import jax
import jax.numpy as jnp
from jax import lax
from jax.sharding import PartitionSpec as P

SIDE = 128
CH = 64


def border(field):
    return jnp.stack([field[:, :, 0, :], field[:, :, :, -1], field[:, :, -1, :], field[:, :, :, 0]])


def frame_rim(frame):
    return jnp.stack(
        [frame[:, :, 0, 1:-1], frame[:, :, 1:-1, -1], frame[:, :, -1, 1:-1], frame[:, :, 1:-1, 0]]
    )


def outgoing(strips):
    return jnp.stack([strips[0], strips[1], strips[2][..., ::-1], strips[3][..., ::-1]])


def orient(strips):
    return jnp.stack([strips[0][..., ::-1], strips[1][..., ::-1], strips[2], strips[3]])


def with_rims(field, incoming):
    padded = jnp.pad(field, ((0, 0), (0, 0), (1, 1), (1, 1)))
    padded = padded.at[:, :, 0, 1:-1].set(incoming[0])
    padded = padded.at[:, :, 1:-1, -1].set(incoming[1])
    padded = padded.at[:, :, -1, 1:-1].set(incoming[2])
    padded = padded.at[:, :, 1:-1, 0].set(incoming[3])
    return padded


def add_rims(interior, incoming):
    interior = interior.at[:, :, 0, :].add(incoming[0])
    interior = interior.at[:, :, :, -1].add(incoming[1])
    interior = interior.at[:, :, -1, :].add(incoming[2])
    interior = interior.at[:, :, :, 0].add(incoming[3])
    return interior


def windows(padded, width, anchor):
    stacked = []
    for position in range(9):
        row_shift, col_shift = divmod(position, 3)
        row_start = (
            anchor + (2 - 2 * anchor) * row_shift // 2 if anchor == 0 else anchor - row_shift
        )
        col_start = (
            anchor + (2 - 2 * anchor) * col_shift // 2 if anchor == 0 else anchor - col_shift
        )
        stacked.append(padded[:, :, row_start : row_start + width, col_start : col_start + width])
    return jnp.stack(stacked, axis=1)


def weight_terms(columns, grad_out):
    return jnp.einsum("boij,bpcij->poc", grad_out, columns, preferred_element_type=jnp.float32)


def spread(grad_out, weights):
    wide = jnp.pad(grad_out, ((0, 0), (0, 0), (2, 2), (2, 2)))
    return jnp.einsum(
        "poc,bpoij->bcij", weights, windows(wide, SIDE + 2, 2), preferred_element_type=jnp.float32
    )


def pick_gathered(gathered, pick_table):
    return jnp.einsum(
        "kq,qbcs->kbcs", pick_table, gathered, preferred_element_type=jnp.float32
    ).astype(gathered.dtype)


def body(cycle_maps, send_pick, recv_pick, neighbour, facing, conv_first, conv_second, cotangent):
    map_count, input_count, pixel_count = cycle_maps.shape
    tile_count = lax.axis_size("tile")
    block_slots = send_pick.shape[0] // tile_count
    my_index = lax.axis_index("tile")
    devices = jnp.arange(tile_count, dtype=jnp.int32)
    sides = jnp.arange(4, dtype=jnp.int32)
    mine = (devices == my_index)[:, None]
    my_nbr = jnp.sum(jnp.where(mine, neighbour, 0), axis=0)
    my_face = jnp.sum(jnp.where(mine, facing, 0), axis=0)
    partner = my_nbr[:, None] == devices[None, :]
    facing_hot = my_face[:, None] == sides[None, :]
    pick_table = (
        (partner[:, :, None] & facing_hot[:, None, :])
        .reshape(4, 4 * tile_count)
        .astype(jnp.bfloat16)
    )
    extended = jnp.concatenate(
        [cycle_maps, jnp.zeros((map_count, input_count, 1), cycle_maps.dtype)], axis=2
    )
    blocks_out = jnp.take(extended, send_pick, axis=2).reshape(
        map_count, input_count, tile_count, block_slots
    )
    arrived = lax.all_to_all(blocks_out, "tile", split_axis=2, concat_axis=2, tiled=True)
    tiles = jnp.take(
        arrived.reshape(map_count, input_count, tile_count * block_slots), recv_pick, axis=2
    )
    tiles = tiles.reshape(map_count, input_count, SIDE, SIDE)
    incoming = pick_gathered(
        lax.all_gather(outgoing(border(tiles)), "tile", axis=0, tiled=True), pick_table
    )
    padded_in = with_rims(tiles, orient(incoming))
    input_columns = windows(padded_in, SIDE, 0)
    pre = jnp.einsum(
        "poc,bpcij->boij", conv_first, input_columns, preferred_element_type=jnp.float32
    )
    hidden = jax.nn.silu(pre).astype(jnp.bfloat16)
    incoming = pick_gathered(
        lax.all_gather(outgoing(border(hidden)), "tile", axis=0, tiled=True), pick_table
    )
    padded_hidden = with_rims(hidden, orient(incoming))
    hidden_columns = windows(padded_hidden, SIDE, 0)
    output_maps = jnp.einsum(
        "poc,bpcij->boij", conv_second, hidden_columns, preferred_element_type=jnp.float32
    ).astype(jnp.bfloat16)
    count = map_count * lax.axis_size("chan") * lax.axis_size("sub") * tile_count * SIDE * SIDE
    scale = 1.0 / math.sqrt(count)
    grad_out = cotangent.reshape(map_count, CH, SIDE, SIDE)
    second_term = weight_terms(hidden_columns, grad_out) * scale
    grad_frame = spread(grad_out, conv_second)
    rim_strips = outgoing(frame_rim(grad_frame)).astype(jnp.bfloat16)
    incoming = pick_gathered(lax.all_gather(rim_strips, "tile", axis=0, tiled=True), pick_table)
    hidden_grad = add_rims(grad_frame[:, :, 1:-1, 1:-1], orient(incoming).astype(jnp.float32))
    sigma = jax.nn.sigmoid(pre)
    pre_grad = (hidden_grad * sigma * (1.0 + pre * (1.0 - sigma))).astype(jnp.bfloat16)
    first_term = weight_terms(input_columns, pre_grad) * scale
    grad_first, grad_second = lax.psum((first_term, second_term), ("tile", "chan", "sub"))
    output_flat = output_maps.reshape(map_count, CH, pixel_count)
    grad_flat = hidden_grad.astype(jnp.bfloat16).reshape(map_count, CH, pixel_count)
    return (output_flat, grad_flat, grad_first, grad_second)


def solution(mesh):
    in_specs = (
        P(("groups", "chan", "sub"), None, "tile"),
        P("tile"),
        P("tile"),
        P(),
        P(),
        P(),
        P(),
        P(("groups", "chan", "sub"), None, "tile"),
    )
    out_specs = (
        P(("groups", "chan", "sub"), None, "tile"),
        P(("groups", "chan", "sub"), None, "tile"),
        P("groups", None, None),
        P("groups", None, None),
    )
    return jax.shard_map(body, mesh=mesh, in_specs=in_specs, out_specs=out_specs, check_vma=False)
```

profile of v0, /device:TPU:0, one launch (start us, length us, event | category | flops | bytes accessed | tf_op | source)
XLA Modules:
  0.0 564.2 jit_solution(10738026590723426309)
XLA Ops:
  13.1 5.4 pad_bitcast_fusion
  18.5 85.3 %gather_fusion = bf16[24576,3]{1,0:T(8,128)(2,1)} fusion(bf16[3,16385]{0,1:T(8,128)(2,1)} %pad_bitcast_fusion, s32[24576]{0:T(1024)S(1)} %fusion.91), kind=kCustom, calls=%fused_computation | custom fusion | bytes 393216 | tf_op jit(solution)/shard_map/jit(_take)/gather | solution.py:98
  103.8 5.3 copy.632
  110.0 6.3 %all-to-all-start = ((bf16[1,3,4,6144]{3,1,0,2:T(4,128)(2,1)}), bf16[1,3,4,6144]{3,1,0,2:T(4,128)(2,1)S(1)}, u32[]{:S(2)}, u32[]{:S(2)}) async-start(bf16[1,3,4,6144]{3,1,0,2:T(4,128)(2,1)} %broadcast_select_fusion), calls=%async_computation | async-start | bytes 393216 | tf_op jit(solution)/shard_map/all_to_all | solution.py:101
  147.1 19.4 %fusion = f32[130,130,64,1]{1,2,3,0:T(8,128)} fusion(bf16[1,9,64,130,130]{4,2,1,3,0:T(8,128)(2,1)} %fusion.23, bf16[9,64,64]{2,1,0:T(8,128)(2,1)S(1)} %copy-done), kind=kOutput, calls=%fused_computation.2 | convolution fusion | flops 1246003200 | bytes 23868928 | tf_op jit(solution)/shard_map/poc,bpoij->bcij/dot_general | solution.py:67
  166.5 10.8 %copy.667 = f32[130,130,64]{0,2,1:T(8,128)} copy(f32[130,130,64]{1,2,0:T(8,128)} %bitcast.344) | data formatting | bytes 8652800 | tf_op jit(solution)/shard_map/poc,bpoij->bcij/dot_general | solution.py:67
  189.0 14.4 %all_gather.11 = bf16[16,1,64,128]{3,2,1,0:T(8,128)(2,1)S(1)} all-gather(bf16[4,1,64,128]{3,2,1,0:T(8,128)(2,1)S(1)} %pad_maximum_fusion.1), channel_id=1, replica_groups=mesh['groups'=2,'tile'=4,'chan'=2,'sub'=2] {'tile'}, dimensions={0}, use_global_device_ids=true | all-gather | bytes 327680 | tf_op jit(solution)/shard_map/all_gather | solution.py:129
  204.1 6.5 %slice.631 = f32[1,64,128,128]{2,1,3,0:T(8,128)} slice(f32[1,64,130,130]{2,1,3,0:T(8,128)} %bitcast.342), slice={[0:1], [0:64], [1:129], [1:129]} | slice | bytes 8388608 | tf_op jit(solution)/shard_map/slice | solution.py:130
  210.8 4.8 copy.672
  215.7 6.7 %slice_add_fusion.1 = f32[1,64,1,128]{2,1,3,0:T(8,128)} fusion(f32[1,64,1,128]{2,1,3,0:T(8,128)} %copy.672, f32[1,64,130,130]{2,1,3,0:T(8,128)} %bitcast.343), kind=kLoop, calls=%fused_computation.37 | loop fusion | flops 8192 | bytes 98304 | tf_op jit(solution)/shard_map/add | solution.py:40
  222.4 11.3 %scatter-add.14 = f32[1,64,128,128]{2,1,3,0:T(8,128)} dynamic-update-slice(f32[1,64,128,128]{2,1,3,0:T(8,128)} %slice.631, f32[1,64,1,128]{2,1,3,0:T(8,128)} %slice_add_fusion.1, s32[]{:T(128)} %constant.343.clone.1, s32[]{:T(128)} %constant.343.clone.1, s32[]{:T(128)} %constant.343.clone.1, s32[]{:T(128)} %constant.343.clone.1) | dynamic-update-slice | bytes 65540 | tf_op jit(solution)/shard_map/scatter-add | solution.py:40
  235.0 5.3 slice.643
  240.3 5.5 copy.674
  254.6 6.8 %slice_add_fusion = f32[1,64,128,1]{3,1,2,0:T(8,128)} fusion(f32[1,64,128,1]{3,1,2,0:T(8,128)} %copy.675, f32[1,64,128,128]{3,1,2,0:T(8,128)} %fusion.94), kind=kLoop, calls=%fused_computation.36 | loop fusion | flops 8192 | bytes 98304 | tf_op jit(solution)/shard_map/add | solution.py:43
  261.3 11.3 %scatter-add.19 = f32[1,64,128,128]{3,1,2,0:T(8,128)} dynamic-update-slice(f32[1,64,128,128]{3,1,2,0:T(8,128)} %fusion.94, f32[1,64,128,1]{3,1,2,0:T(8,128)} %slice_add_fusion, s32[]{:T(128)} %constant.343.clone.1, s32[]{:T(128)} %constant.343.clone.1, s32[]{:T(128)} %constant.343.clone.1, s32[]{:T(128)} %constant.343.clone.1) | dynamic-update-slice | bytes 65540 | tf_op jit(solution)/shard_map/scatter-add | solution.py:43
  283.7 58.5 %gather_fusion.1 = bf16[16384,3]{1,0:T(8,128)(2,1)} fusion(bf16[3,24576]{0,1:T(8,128)(2,1)} %bitcast.346, s32[16384]{0:T(1024)S(1)} %fusion.92), kind=kCustom, calls=%fused_computation.1 | custom fusion | bytes 262144 | tf_op jit(solution)/shard_map/jit(_take)/gather | solution.py:102
  346.4 13.2 %all_gather.9 = bf16[16,1,3,128]{3,2,1,0:T(4,128)(2,1)S(1)} all-gather(bf16[4,1,3,128]{3,2,1,0:T(4,128)(2,1)S(1)} %pad_maximum_fusion.2), channel_id=1, replica_groups=mesh['groups'=2,'tile'=4,'chan'=2,'sub'=2] {'tile'}, dimensions={0}, use_global_device_ids=true | all-gather | bytes 15360 | tf_op jit(solution)/shard_map/all_gather | solution.py:107
  385.8 13.9 %all_gather.10 = bf16[16,1,64,128]{3,2,1,0:T(8,128)(2,1)S(1)} all-gather(bf16[4,1,64,128]{3,2,1,0:T(8,128)(2,1)S(1)} %pad_maximum_fusion), channel_id=1, replica_groups=mesh['groups'=2,'tile'=4,'chan'=2,'sub'=2] {'tile'}, dimensions={0}, use_global_device_ids=true | all-gather | bytes 327680 | tf_op jit(solution)/shard_map/all_gather | solution.py:116
  410.3 16.5 %scatter.35 = bf16[1,64,130,130]{3,1,2,0:T(8,128)(2,1)} dynamic-update-slice(bf16[1,64,130,130]{3,1,2,0:T(8,128)(2,1)} %scatter.34, bf16[1,64,128,1]{3,1,2,0:T(8,128)(2,1)} %copy.654, s32[]{:T(128)} %constant.343.clone.1, s32[]{:T(128)} %constant.343.clone.1, s32[]{:T(128)} %constant.352.clone.1, s32[]{:T(128)} %constant.353.clone.1) | dynamic-update-slice | bytes 32772 | tf_op jit(solution)/shard_map/scatter | solution.py:33
  428.3 10.6 %scatter.39 = bf16[1,64,130,130]{3,1,2,0:T(8,128)(2,1)} dynamic-update-slice(bf16[1,64,130,130]{3,1,2,0:T(8,128)(2,1)} %scatter.36, bf16[1,64,128,1]{3,1,2,0:T(8,128)(2,1)S(1)} %copy.655, s32[]{:T(128)} %constant.343.clone.1, s32[]{:T(128)} %constant.343.clone.1, s32[]{:T(128)} %constant.352.clone.1, s32[]{:T(128)} %constant.343.clone.1) | dynamic-update-slice | bytes 32772 | tf_op jit(solution)/shard_map/scatter | solution.py:35
  456.8 5.8 %fusion.63 = f32[9,64,64]{1,2,0:T(8,128)} fusion(bf16[64,128,128]{2,1,0:T(8,128)(2,1)S(1)} %bitcast.350, bf16[1,9,64,128,128]{4,2,3,1,0:T(8,128)(2,1)S(1)} %fusion.33), kind=kOutput, calls=%fused_computation.81 | convolution fusion | flops 1207996416 | bytes 21118976 | tf_op jit(solution)/shard_map/boij,bpcij->poc/dot_general | solution.py:62
  462.6 5.9 %fusion.78 = f32[9,64,3]{1,0,2:T(8,128)S(1)} fusion(f32[1,64,128,128]{3,1,2,0:T(8,128)} %scatter-add.19, f32[128,128,64,1]{1,2,3,0:T(8,128)} %get-tuple-element.234, bf16[1,9,3,128,128]{4,1,2,3,0:T(8,128)(2,1)} %copy-done.4), kind=kOutput, calls=%fused_computation.84 | convolution fusion | flops 66062016 | bytes 9280256 | tf_op jit(solution)/shard_map/boij,bpcij->poc/dot_general | solution.py:62
  468.6 58.0 %psum.14 = f32[9,64,3]{1,0,2:T(8,128)S(1)} all-reduce(f32[9,64,3]{1,0,2:T(8,128)S(1)} %fusion.78), channel_id=1, replica_groups=mesh['groups'=2,'tile'=4,'chan'=2,'sub'=2] {'tile','chan','sub'}, use_global_device_ids=true, to_apply=%region_2.3 | all-reduce | flops 1728 | bytes 13824 | tf_op jit(solution)/shard_map/psum | solution.py:134
  528.9 26.4 %all-reduce.6.cloned.1.call-done = f32[9,64,64]{1,2,0:T(8,128)} async-done(((f32[9,64,64]{1,2,0:T(8,128)}), f32[9,64,64]{1,2,0:T(8,128)}) %all-reduce.6.cloned.1.call-update) | async-done | bytes 147472 | tf_op jit(solution)/shard_map/psum | solution.py:134
  (132 shorter events, 135.4 us)
Async XLA Ops:
  7.2 139.9 %copy-start = (bf16[9,64,64]{2,1,0:T(8,128)(2,1)S(1)}, bf16[9,64,64]{2,1,0:T(8,128)(2,1)}, u32[]{:S(2)}) copy-start(bf16[9,64,64]{2,1,0:T(8,128)(2,1)} %param.38) | copy-start | bytes 221188
  18.5 98.0 %copy-start.2 = (bf16[1,64,16384]{2,1,0:T(8,128)(2,1)S(1)}, bf16[1,64,16384]{2,1,0:T(8,128)(2,1)}, u32[]{:S(2)}) copy-start(bf16[1,64,16384]{2,1,0:T(8,128)(2,1)} %param.39) | copy-start | bytes 6291460
  110.0 168.9 %all-to-all-start = ((bf16[1,3,4,6144]{3,1,0,2:T(4,128)(2,1)}), bf16[1,3,4,6144]{3,1,0,2:T(4,128)(2,1)S(1)}, u32[]{:S(2)}, u32[]{:S(2)}) async-start(bf16[1,3,4,6144]{3,1,0,2:T(4,128)(2,1)} %broadcast_select_fusion), calls=%async_computation | async-start | bytes 393216 | tf_op jit(solution)/shard_map/all_to_all | solution.py:101
  116.3 439.0 %all-reduce.6.cloned.1.call-start = ((), (), s32[]{:S(2)}) async-start(), calls=%async_computation.1 | async-start | bytes 589824 | tf_op jit(solution)/shard_map/psum | solution.py:134
  181.4 22.1 %copy-start.6 = (s32[4,4]{1,0:T(4,128)S(1)}, s32[4,4]{1,0:T(4,128)}, u32[]{:S(2)}) copy-start(s32[4,4]{1,0:T(4,128)} %param.35) | copy-start | bytes 196
  181.4 22.0 %copy-start.7 = (s32[4,4]{1,0:T(4,128)S(1)}, s32[4,4]{1,0:T(4,128)}, u32[]{:S(2)}) copy-start(s32[4,4]{1,0:T(4,128)} %param.36) | copy-start | bytes 196
  261.3 11.3 %copy-start.5 = (s32[16384]{0:T(1024)S(1)}, s32[16384]{0:T(1024)}, u32[]{:S(2)}) copy-start(s32[16384]{0:T(1024)} %param.34) | copy-start | bytes 196612
  360.2 10.3 %copy-start.8 = (bf16[9,64,3]{1,2,0:T(4,128)(2,1)S(1)}, bf16[9,64,3]{1,2,0:T(4,128)(2,1)}, u32[]{:S(2)}) copy-start(bf16[9,64,3]{1,2,0:T(4,128)(2,1)} %param.37) | copy-start | bytes 10372
  370.5 3.4 copy-start.4
  438.9 5.5 copy-start.1
  452.6 4.2 copy-start.3
Sparse Core Ops, SparseCore 0:
  462.8 92.4 all-reduce.5
where the time goes:
time: 569 us; the launch traced here: 564 us
  local copies, waits for them, and re-layouts  351 us (62%)
  blocking collectives  99.6 us (18%)
  matrix products  39.4 us (7%)
  other arithmetic  26.4 us (5%)
  waiting for transfers between devices  26.4 us (5%)
  between operations  14.8 us (3%)
  starting transfers between devices  6.45 us (1%)
    gather x2, local copies, waits for them, and re-layouts, body(): jnp.take(extended, send_pick, axis=2)  90.6 us
    gather x2, local copies, waits for them, and re-layouts, body(): jnp.take(arrived.reshape(map_count, input_count, tile_count * block_slots...  62.2 us
    psum x1, blocking collectives, body(): lax.psum((first_term, second_term), ('tile', 'chan', 'sub'))  58 us
    unnamed x41, local copies, waits for them, and re-layouts  49.3 us
    another operation x18, local copies, waits for them, and re-layouts  26.9 us
    psum x1, waiting for transfers between devices, body(): lax.psum((first_term, second_term), ('tile', 'chan', 'sub'))  26.4 us
    dot_general x1, matrix products, spread(): jnp.einsum('poc,bpoij->bcij', weights, windows(wide, SIDE + 2, 2), prefer...  19.4 us
    scatter x2, local copies, waits for them, and re-layouts, with_rims(): padded = padded.at[:, :, 1:-1, -1].set(incoming[1])  17.6 us
  transfers between devices with their start and end apart: 2, of which 1 were waited for; matrix products, arithmetic and copies ran while one was open for 28% of the time, Pallas kernels for 0%

commit v1 on v0

v1 whole, which is shorter than its diff:
```python
import functools
import math

import jax
import jax.numpy as jnp
from jax import lax
from jax.experimental import pallas as pl
from jax.experimental.pallas import tpu as pltpu
from jax.sharding import PartitionSpec as P

SIDE = 128
PIX = SIDE * SIDE
CH = 64
CIN = 3
LOW = 256
COMB = 80
ROWS = 16
STEPS = SIDE // ROWS
F32 = jnp.float32
BF16 = jnp.bfloat16
SMEM = pl.BlockSpec(memory_space=pltpu.SMEM)
VMEM = pl.BlockSpec(memory_space=pltpu.VMEM)


def iota(shape, dim):
    return lax.broadcasted_iota(jnp.int32, shape, dim)


def hot(a, b):
    return jnp.where(a == b, 1.0, 0.0).astype(BF16)


def dot(a, b):
    return jnp.dot(a, b, preferred_element_type=F32)


def dot_nt(a, b):
    return lax.dot_general(a, b, (((1,), (1,)), ((), ())), preferred_element_type=F32)


def reverse(strip):
    swap = hot(iota((SIDE, SIDE), 0) + iota((SIDE, SIDE), 1), SIDE - 1)
    return dot(strip.astype(BF16), swap)


def from_left(x):
    return jnp.where(iota(x.shape, 1) == 0, 0.0, pltpu.roll(x, 1, 1))


def from_right(x):
    return jnp.where(iota(x.shape, 1) == SIDE - 1, 0.0, pltpu.roll(x, SIDE - 1, 1))


def ends_table(shift, east):
    src = iota((SIDE, 2 * SIDE), 0)
    lane = iota((SIDE, 2 * SIDE), 1)
    return hot(lane, 2 * (src - shift) + (0 if east else 1))


def row_ends(pairs, row):
    half = row // (SIDE // 2)
    back = lax.rem(4 * SIDE - 2 * row - 1, SIDE)
    return pltpu.roll(pairs[half], back, 1)


def is_end(shape):
    lane = iota(shape, 1)
    return (lane == 0) | (lane == SIDE - 1)


def pick_rows(low_rows, high_rows, groups, source):
    found = dot(source, hot(iota((LOW, LOW), 0), low_rows))
    here = iota((groups, LOW), 0) == high_rows
    picked = []
    for c in range(CIN):
        part = jnp.where(here, found[c * groups : (c + 1) * groups], 0.0)
        picked.append(jnp.sum(part, axis=0, keepdims=True))
    return picked


def split_index(index):
    return index & (LOW - 1), index >> 8


def tile_params(limit_mib):
    return pltpu.CompilerParams(vmem_limit_bytes=limit_mib << 20)


def send_kernel(tile_count, direct, scal, cyc, index, *rest):
    outs, (stage, source, found) = rest[:-3], rest[-3:]
    groups = PIX // LOW
    per_dest = index.shape[0] // 2 // tile_count
    whole = cyc[...].astype(F32)
    for h in range(groups):
        piece = whole[:, h * LOW : (h + 1) * LOW]
        for c in range(CIN):
            stage[pl.ds(c * groups + h, 1), :] = piece[c : c + 1]
    source[...] = stage[...].astype(BF16)
    data = source[...]
    me = scal[0]

    def chunk(m, carry):
        if direct:
            dest = lax.rem(me + m // per_dest, tile_count)
            at = dest * per_dest + lax.rem(m, per_dest)
        else:
            at = m
        row = jnp.concatenate([index[pl.ds(2 * at, 1), :], index[pl.ds(2 * at + 1, 1), :]], axis=1)
        low, high = split_index(row)
        picked = pick_rows(low, high, groups, data)
        for c in range(CIN):
            found[c, pl.ds(m, 1), :] = picked[c]
        return carry

    lax.fori_loop(0, tile_count * per_dest, chunk, 0, unroll=4)
    for d in range(tile_count):
        for c in range(CIN):
            block = found[c, d * per_dest : (d + 1) * per_dest, :].astype(BF16)
            if direct:
                outs[d][c] = block
            else:
                outs[0][d, c] = block


def side_towards(nbr, me, dest):
    side = jnp.int32(0)
    for k in range(4):
        side = jnp.where(nbr[me, k] == dest, k, side)
    return side


def send_strips(tile_count, direct, nbr, me, strips, outs):
    if direct:
        for s in range(1, tile_count):
            dest = lax.rem(me + s, tile_count)
            outs[s - 1][...] = strips[side_towards(nbr, me, dest)]
    else:
        for dest in range(tile_count):
            outs[0][dest] = strips[side_towards(nbr, me, dest)]


def take_strips(tile_count, direct, nbr, fac, me, own, arrived, table):
    for k in range(4):
        table[k] = own[k]
    if direct:
        for s in range(1, tile_count):
            table[4 + lax.rem(me + tile_count - s, tile_count)] = arrived[s - 1][...]
    else:
        for d in range(tile_count):
            table[4 + d] = arrived[0][d]
    table[4 + tile_count] = jnp.zeros(table.shape[1:], table.dtype)
    got = []
    for k in range(4):
        other = nbr[me, k]
        at = jnp.where(other == me, fac[me, k], 4 + other)
        at = jnp.where(other < 0, 4 + tile_count, at)
        got.append(table[at])
    return got


def strip_kernel(tile_count, direct, scal, nbr, index, rims, *rest):
    n_in = tile_count if direct else 1
    n_out = tile_count - 1 if direct else 1
    blocks, rest = rest[:n_in], rest[n_in:]
    sends, rest = rest[:n_out], rest[n_out:]
    source, strips, comb, stage = rest
    me = scal[0]
    per_src = blocks[0].shape[-2]
    groups = tile_count * per_src
    for s in range(tile_count):
        for c in range(CIN):
            if direct:
                src = lax.rem(me + tile_count - s, tile_count)
                at = c * groups + src * per_src
                if per_src % 8 == 0:
                    at = pl.multiple_of(at, 8)
                stage[pl.ds(at, per_src), :] = blocks[s][c].astype(F32)
            else:
                at = c * groups + s * per_src
                stage[at : at + per_src, :] = blocks[0][s, c].astype(F32)
    source[...] = stage[...].astype(BF16)
    data = source[...]
    flipped = index[...].astype(F32).T
    col = lambda j: flipped[j : j + 1, :].astype(jnp.int32)
    row = lambda i: index[i : i + 1, :]
    pairs = [(row(0), row(1)), (row(126), row(127)), (col(0), col(1)), (col(126), col(127))]
    for n, pair in enumerate(pairs):
        low, high = split_index(jnp.concatenate(pair, axis=1))
        picked = pick_rows(low, high, groups, data)
        for c in range(CIN):
            strips[2 * n, c : c + 1, :] = picked[c][:, :SIDE]
            strips[2 * n + 1, c : c + 1, :] = picked[c][:, SIDE:]
    for n in range(8):
        strips[n, CIN:, :] = jnp.zeros((8 - CIN, SIDE), F32)
    edge = [strips[0], strips[7], reverse(strips[3]), reverse(strips[4])]
    blank = jnp.zeros((COMB - CH - 8, SIDE), F32)
    for k in range(4):
        comb[k, :CH, :] = rims[k]
        comb[k, CH:, :] = jnp.concatenate([edge[k], blank], axis=0).astype(BF16)
    send_strips(tile_count, direct, nbr, me, comb, sends)


def main_pick_kernel(groups, index, source, out):
    data = source[...]

    def chunk(m, carry):
        row = jnp.concatenate([index[pl.ds(2 * m, 1), :], index[pl.ds(2 * m + 1, 1), :]], axis=1)
        low, high = split_index(row)
        picked = pick_rows(low, high, groups, data)
        lanes = pl.ds(pl.multiple_of(m * LOW, LOW), LOW)
        for c in range(CIN):
            out[c : c + 1, lanes] = picked[c]
        return carry

    lax.fori_loop(0, PIX // LOW, chunk, 0, unroll=4)
    out[CIN:, :] = jnp.zeros((8 - CIN, PIX), F32)


def three_rows_down(before, here, after):
    up = jnp.concatenate([here[:, SIDE:], after], axis=1)
    down = jnp.concatenate([before, here[:, :-SIDE]], axis=1)
    return jnp.concatenate([up, here, down], axis=0)


def frame_kernel(cot, prev, nxt, conv_second, hg, rims, ends, fwd_w, back_w, columns):
    step = pl.program_id(0)

    @pl.when(step == 0)
    def _():
        for a in range(3):
            for b in range(3):
                w = conv_second[3 * a + b]
                rows = slice(b * CH, (b + 1) * CH)
                lanes = slice(a * CH, (a + 1) * CH)
                fwd_w[rows, lanes] = w
                back_w[rows, lanes] = w.astype(F32).T.astype(BF16)
        columns[...] = jnp.zeros_like(columns)

    weights = back_w[...]
    here = cot[...]
    before = jnp.where(step > 0, prev[...], jnp.zeros_like(prev))
    after = jnp.where(step < STEPS - 1, nxt[...], jnp.zeros_like(nxt))
    stacked = three_rows_down(before, here, after)
    for p in range(ROWS // 2):
        lanes = slice(2 * p * SIDE, (2 * p + 2) * SIDE)
        z = dot(weights, stacked[:, lanes])
        for r in range(2):
            zr = z[:, r * SIDE : (r + 1) * SIDE]
            hg[:, (2 * p + r) * SIDE : (2 * p + r + 1) * SIDE] = (
                zr[CH : 2 * CH] + from_right(zr[:CH]) + from_left(zr[2 * CH :])
            )
    half = step // (STEPS // 2)
    acc = columns[half]
    pair = iota((CH, SIDE), 1) // 2
    for t in range(ROWS):
        r = step * ROWS + t
        line = here[:, t * SIDE : (t + 1) * SIDE].astype(F32)
        turned = pltpu.roll(line, lax.rem(2 * r + 1, SIDE), 1)
        acc = jnp.where(pair == lax.rem(r, SIDE // 2), turned, acc)
    columns[half] = acc

    def rim_row(line, a):
        z = dot(weights[:, a * CH : (a + 1) * CH], line)
        return z[CH : 2 * CH] + from_right(z[:CH]) + from_left(z[2 * CH :])

    @pl.when(step == 0)
    def _():
        rims[0] = rim_row(here[:, :SIDE], 0).astype(BF16)

    @pl.when(step == STEPS - 1)
    def _():
        rims[2] = reverse(rim_row(here[:, -SIDE:], 2)).astype(BF16)
        k = iota((2 * SIDE, 2 * SIDE), 0)
        n = iota((2 * SIDE, 2 * SIDE), 1)
        sort = hot(k, jnp.where(n < SIDE, 2 * n + 1, 2 * (n - SIDE)))
        both = jnp.concatenate([columns[0], columns[1]], axis=1).astype(BF16)
        both = dot(both, sort)
        for e in range(2):
            line = both[:, e * SIDE : (e + 1) * SIDE]
            three = jnp.concatenate([from_right(line), line, from_left(line)], axis=0).astype(BF16)
            ends[e] = three
            rim = dot(weights[2 * CH * e : 2 * CH * e + CH], three)
            if e == 0:
                rims[3] = reverse(rim).astype(BF16)
            else:
                rims[1] = rim.astype(BF16)


def first_weights(conv_first, table):
    table[...] = jnp.zeros_like(table)
    for a in range(3):
        for b in range(3):
            w = conv_first[3 * a + b].astype(F32)
            table[:, 32 * a + 8 * b : 32 * a + 8 * b + CIN] = w


def border_kernel(tile_count, direct, scal, nbr, fac, strips, comb, conv_first, *rest):
    n = tile_count - 1 if direct else 1
    arrived, rest = rest[:n], rest[n:]
    pads, rims_in, own, w_out, rest = rest[0], rest[1], rest[2], rest[3], rest[4:]
    sends, rest = rest[:n], rest[n:]
    table, w_table, lines = rest
    me = scal[0]
    first_weights(conv_first, w_table)
    w1 = w_table[...].astype(BF16)
    w_out[...] = w1
    got = take_strips(tile_count, direct, nbr, fac, me, comb, arrived, table)
    north = [reverse(got[0]), reverse(got[1]), got[2].astype(F32), got[3].astype(F32)]
    pad = [x[CH : CH + 8] for x in north]
    rims_in[0] = north[0][:CH]
    rims_in[1] = north[2][:CH]
    cols = dot(north[3][:CH].astype(BF16), ends_table(0, False))
    cols = cols + dot(north[1][:CH].astype(BF16), ends_table(0, True))
    rims_in[2] = cols[:, :SIDE]
    rims_in[3] = cols[:, SIDE:]
    pads[0] = pad[0]
    pads[1] = pad[2]
    cols = dot(pad[3].astype(BF16), ends_table(0, False)) + dot(pad[1].astype(BF16), ends_table(0, True))
    pads[2] = cols[:, :SIDE]
    pads[3] = cols[:, SIDE:]

    lane = iota((8, SIDE), 1)

    def shifted(line, first, last):
        left = jnp.where(lane == 0, first, pltpu.roll(line, 1, 1))
        right = jnp.where(lane == SIDE - 1, last, pltpu.roll(line, SIDE - 1, 1))
        return [left, line, right]

    zero = jnp.zeros((8, 1), F32)
    at = lambda x, i: x[:, i : i + 1]
    n0, e0, s0, w0 = pad
    st = [strips[i] for i in range(8)]
    across = [
        (0, [(n0, zero, zero), (st[0], at(w0, 0), at(e0, 0)), (st[1], at(w0, 1), at(e0, 1))]),
        (2, [(st[2], at(w0, 126), at(e0, 126)), (st[3], at(w0, 127), at(e0, 127)), (s0, zero, zero)]),
    ]
    along = [
        (3, [(w0, zero, zero), (st[4], at(n0, 0), at(s0, 0)), (st[5], at(n0, 1), at(s0, 1))]),
        (1, [(st[6], at(n0, 126), at(s0, 126)), (st[7], at(n0, 127), at(s0, 127)), (e0, zero, zero)]),
    ]
    lines[...] = jnp.zeros_like(lines)
    for side, three in across:
        for a, line in enumerate(three):
            for b, value in enumerate(shifted(*line)):
                lines[32 * a + 8 * b : 32 * a + 8 * b + 8, side * SIDE : (side + 1) * SIDE] = value
    for side, three in along:
        for b, line in enumerate(three):
            for a, value in enumerate(shifted(*line)):
                lines[32 * a + 8 * b : 32 * a + 8 * b + 8, side * SIDE : (side + 1) * SIDE] = value
    pre = dot(w1, lines[...].astype(BF16))
    hid = (pre * jax.nn.sigmoid(pre)).astype(BF16)
    side = lambda k: hid[:, k * SIDE : (k + 1) * SIDE]
    own[0] = side(0)
    own[1] = side(1)
    own[2] = reverse(side(2)).astype(BF16)
    own[3] = reverse(side(3)).astype(BF16)
    send_strips(tile_count, direct, nbr, me, own, sends)


def middle_kernel(tiles, pads, rims_in, w1_ref, hg, cot, prev, nxt, hidden, grad, g1, g2, planes):
    step = pl.program_id(0)

    @pl.when(step == 0)
    def _():
        g1[...] = jnp.zeros_like(g1)
        g2[...] = jnp.zeros_like(g2)
        lane = iota((8, SIDE), 1)
        rest = jnp.zeros((8, SIDE), F32)

        def put(row, line):
            planes[:, row * SIDE : (row + 1) * SIDE] = line

        def frame(line, ends):
            left = jnp.where(lane == 0, ends, pltpu.roll(line, 1, 1))
            right = jnp.where(lane == SIDE - 1, ends, pltpu.roll(line, SIDE - 1, 1))
            return jnp.concatenate([left, line, right, rest], axis=0).astype(BF16)

        put(0, frame(pads[0], rest))
        put(SIDE + 1, frame(pads[1], rest))
        for i in range(SIDE):
            back = (4 * SIDE - 2 * i - 1) % SIDE
            ends = pltpu.roll(pads[2 + i // (SIDE // 2)], back, 1)
            put(i + 1, frame(tiles[:, i * SIDE : (i + 1) * SIDE], ends))

    w1 = w1_ref[...]
    here = cot[...]
    before = jnp.where(step > 0, prev[...], jnp.zeros_like(prev))
    after = jnp.where(step < STEPS - 1, nxt[...], jnp.zeros_like(nxt))
    stacked = three_rows_down(before, here, after)
    end = is_end((CH, SIDE))
    acc1 = g1[...]
    acc2 = g2[...]
    n_rows = 4
    for p in range(ROWS // n_rows):
        base = step * ROWS + p * n_rows
        cols = []
        for a in range(3):
            lanes = pl.ds(pl.multiple_of((base + a) * SIDE, SIDE), n_rows * SIDE)
            cols.append(planes[:, lanes])
        cols = jnp.concatenate(cols, axis=0)
        pre = dot(w1, cols)
        sigma = jax.nn.sigmoid(pre)
        hid = pre * sigma
        slope = sigma * (1.0 + pre * (1.0 - sigma))
        kept, shifted, slopes = [], [], []
        for r in range(n_rows):
            row = base + r
            lanes = slice((p * n_rows + r) * SIDE, (p * n_rows + r + 1) * SIDE)
            piece = slice(r * SIDE, (r + 1) * SIDE)
            line = hg[:, lanes]
            line = line + jnp.where(end, row_ends(rims_in.at[2:4], row), 0.0)
            if p == 0 and r == 0:
                line = line + jnp.where(step == 0, rims_in[0], 0.0)
            if p == ROWS // n_rows - 1 and r == n_rows - 1:
                line = line + jnp.where(step == STEPS - 1, rims_in[1], 0.0)
            grad[:, lanes] = line.astype(BF16)
            slopes.append((line * slope[:, piece]).astype(BF16))
            h = hid[:, piece]
            hb = h.astype(BF16)
            hidden[:, lanes] = hb
            kept.append(hb)
            shifted.append((from_left(h).astype(BF16), from_right(h).astype(BF16)))
        back = jnp.concatenate(slopes, axis=1)
        acc1 = acc1 + dot_nt(back, cols)
        three = jnp.concatenate(
            [
                jnp.concatenate([x[0] for x in shifted], axis=1),
                jnp.concatenate(kept, axis=1),
                jnp.concatenate([x[1] for x in shifted], axis=1),
            ],
            axis=0,
        )
        lanes = slice(p * n_rows * SIDE, (p + 1) * n_rows * SIDE)
        acc2 = acc2 + dot_nt(stacked[:, lanes], three)
    g1[...] = acc1
    g2[...] = acc2


def close_kernel(tile_count, direct, scale, scal, nbr, fac, own, ends, top, bottom, g1, g2, fwd_w, *rest):
    n = tile_count - 1 if direct else 1
    arrived, rest = rest[:n], rest[n:]
    pads, fringe, keep, send, table, total = rest
    me = scal[0]
    got = take_strips(tile_count, direct, nbr, fac, me, own, arrived, table)
    north = reverse(got[0])
    east = reverse(got[1]).astype(BF16)
    south = got[2].astype(F32)
    west = got[3]
    pads[0] = north.astype(BF16)
    pads[1] = got[2]
    side = jnp.zeros((CH, 2 * SIDE), F32)
    for e, strip in ((0, west), (1, east)):
        three = []
        for a in range(3):
            three.append(dot(strip, ends_table(a - 1, e == 1)))
        three = jnp.concatenate(three, axis=0).astype(BF16)
        side = side + dot(fwd_w[2 * CH * e : 2 * CH * e + CH, :], three)
    fringe[0] = side[:, :SIDE]
    fringe[1] = side[:, SIDE:]
    total[:, : 3 * CH] = g2[...] * scale
    total[:, 3 * CH :] = jnp.zeros((3 * CH, CH), F32)

    def wide(line):
        return jnp.concatenate([from_left(line), line, from_right(line)], axis=0).astype(BF16)

    total[:CH, : 3 * CH] += dot_nt(top[...], wide(north)) * scale
    total[2 * CH :, : 3 * CH] += dot_nt(bottom[...], wide(south)) * scale
    total[:, :CH] += dot_nt(ends[0], west) * scale
    total[:, 2 * CH : 3 * CH] += dot_nt(ends[1], east) * scale
    first = g1[...] * scale
    for a in range(3):
        total[a * CH : (a + 1) * CH, 3 * CH : 3 * CH + 32] = first[:, 32 * a : 32 * a + 32]
    core = scal[2]
    half = keep.shape[0]
    if half == 3 * CH:
        keep[...] = total[...]
        send[...] = jnp.zeros_like(send)
    else:
        keep[...] = total[pl.ds(pl.multiple_of(core * half, 8), half), :]
        send[...] = total[pl.ds(pl.multiple_of((1 - core) * half, 8), half), :]


def pair_kernel(scal, kept, got, keep, send, total):
    total[...] = kept[...] + got[...]
    half = keep.shape[0]
    here = scal[1]
    keep[...] = total[pl.ds(pl.multiple_of(here * half, 8), half), :]
    send[...] = total[pl.ds(pl.multiple_of((1 - here) * half, 8), half), :]


def ring_kernel(tile_count, scal, mine, *rest):
    got, (out, table) = rest[:-2], rest[-2:]
    me = scal[0]
    table[me] = mine[...]
    for s in range(1, tile_count):
        table[lax.rem(me + tile_count - s, tile_count)] = got[s - 1][...]
    total = table[0]
    for t in range(1, tile_count):
        total = total + table[t]
    out[...] = total


def join_kernel(scal, mine, got, out):
    half = mine.shape[0]
    here = scal[1]
    out[pl.ds(pl.multiple_of(here * half, 8), half), :] = mine[...]
    out[pl.ds(pl.multiple_of((1 - here) * half, 8), half), :] = got[...]


def unpack(total, first, second):
    for a in range(3):
        for b in range(3):
            rows = slice(a * CH, (a + 1) * CH)
            second[3 * a + b] = total[rows, b * CH : (b + 1) * CH]
            lane = 3 * CH + 8 * b
            first[3 * a + b] = total[rows, lane : lane + CIN]


def last_kernel(scal, mine, got, first, second, total):
    half = mine.shape[0]
    here = scal[2]
    total[pl.ds(pl.multiple_of(here * half, 8), half), :] = mine[...]
    total[pl.ds(pl.multiple_of((1 - here) * half, 8), half), :] = got[...]
    unpack(total, first, second)


def output_kernel(start, hid, prev, nxt, pads, fringe, fwd_w, *rest):
    out = rest[-1]
    step = pl.program_id(0) + start
    weights = fwd_w[...]
    here = hid[...]
    before = jnp.where(step > 0, prev[...], pads[0])
    after = jnp.where(step < STEPS - 1, nxt[...], pads[1])
    up = jnp.concatenate([here[:, SIDE:], after], axis=1)
    down = jnp.concatenate([before, here[:, :-SIDE]], axis=1)
    stacked = jnp.concatenate([down, here, up], axis=0)
    end = is_end((CH, SIDE))
    for p in range(ROWS // 2):
        z = dot(weights, stacked[:, 2 * p * SIDE : (2 * p + 2) * SIDE])
        for r in range(2):
            zr = z[:, r * SIDE : (r + 1) * SIDE]
            line = zr[CH : 2 * CH] + from_left(zr[:CH]) + from_right(zr[2 * CH :])
            line = line + jnp.where(end, row_ends(fringe, step * ROWS + 2 * p + r), 0.0)
            lanes = slice((2 * p + r) * SIDE, (2 * p + r + 1) * SIDE)
            out[:, lanes] = line.astype(BF16)


def shape(dims, kind):
    return jax.ShapeDtypeStruct(dims, kind)


def row_block(offset=0):
    return pl.BlockSpec((CH, ROWS * SIDE), lambda i: (0, i + offset))


def row_before(offset=0):
    return pl.BlockSpec((CH, SIDE), lambda i: (0, jnp.maximum((i + offset) * ROWS - 1, 0)))


def row_after(offset=0):
    return pl.BlockSpec((CH, SIDE), lambda i: (0, jnp.minimum((i + offset + 1) * ROWS, SIDE - 1)))


def cost(flops, moved):
    return pl.CostEstimate(flops=int(flops), bytes_accessed=int(moved), transcendentals=0)


def whole(dims):
    return pl.BlockSpec(dims, lambda i: (0,) * len(dims))


def body(cycle_maps, send_pick, recv_pick, neighbour, facing, conv_first, conv_second, cotangent):
    map_count, _, pixel_count = cycle_maps.shape
    tile_count = lax.axis_size("tile")
    chans = lax.axis_size("chan")
    cores = lax.axis_size("sub")
    direct = tile_count == 4
    assert map_count == 1 and pixel_count == PIX and tile_count != 8
    slots = send_pick.shape[0]
    per_pair = slots // tile_count // LOW
    groups = slots // LOW
    scal = jnp.stack([lax.axis_index(n).astype(jnp.int32) for n in ("tile", "chan", "sub")])
    cyc = cycle_maps.reshape(CIN, PIX)
    cot = cotangent.reshape(CH, PIX)
    n_send = tile_count - 1 if direct else 1

    def exchange(sends):
        if direct:
            return [
                lax.ppermute(x, "tile", [(i, (i + s) % tile_count) for i in range(tile_count)])
                for s, x in zip(range(1, tile_count), sends)
            ]
        return [lax.all_to_all(sends[0], "tile", 0, 0, tiled=True)]

    def sent(dims, kind):
        if direct:
            return [shape(dims, kind)] * n_send
        return [shape((tile_count,) + dims, kind)]

    if direct:
        block_shapes = [shape((CIN, per_pair, LOW), BF16)] * tile_count
    else:
        block_shapes = [shape((tile_count, CIN, per_pair, LOW), BF16)]
    blocks = pl.pallas_call(
        functools.partial(send_kernel, tile_count, direct),
        in_specs=[SMEM, VMEM, VMEM],
        out_specs=[VMEM] * len(block_shapes),
        out_shape=block_shapes,
        scratch_shapes=[
            pltpu.VMEM((CIN * PIX // LOW, LOW), F32),
            pltpu.VMEM((CIN * PIX // LOW, LOW), BF16),
            pltpu.VMEM((CIN, groups, LOW), F32),
        ],
        compiler_params=tile_params(16),
        name="send_pick",
    )(scal, cyc, send_pick.reshape(slots // SIDE, SIDE))
    if direct:
        blocks = [blocks[0]] + exchange(blocks[1:])
    else:
        blocks = exchange(blocks)

    hg, rims, ends, fwd_w = pl.pallas_call(
        frame_kernel,
        grid=(STEPS,),
        in_specs=[row_block(), row_before(), row_after(), whole((9, CH, CH))],
        out_specs=[row_block(), whole((4, CH, SIDE)), whole((2, 3 * CH, SIDE)), whole((3 * CH, 3 * CH))],
        out_shape=[
            shape((CH, PIX), F32),
            shape((4, CH, SIDE), BF16),
            shape((2, 3 * CH, SIDE), BF16),
            shape((3 * CH, 3 * CH), BF16),
        ],
        scratch_shapes=[pltpu.VMEM((3 * CH, 3 * CH), BF16), pltpu.VMEM((2, CH, SIDE), F32)],
        compiler_params=tile_params(32),
        cost_estimate=cost(2 * 9 * CH * CH * PIX, 6 * CH * PIX),
        name="frame",
    )(cot, cot, cot, conv_second)

    index = recv_pick.reshape(SIDE, SIDE)
    *sends, source, strips, comb = pl.pallas_call(
        functools.partial(strip_kernel, tile_count, direct),
        in_specs=[SMEM, SMEM] + [VMEM] * (2 + len(blocks)),
        out_specs=[VMEM] * (n_send + 3),
        out_shape=sent((COMB, SIDE), BF16)
        + [shape((CIN * groups, LOW), BF16), shape((8, 8, SIDE), F32), shape((4, COMB, SIDE), BF16)],
        scratch_shapes=[pltpu.VMEM((CIN * groups, LOW), F32)],
        compiler_params=tile_params(16),
        name="strips",
    )(scal, neighbour, index, rims, *blocks)
    arrived = exchange(sends)

    tiles = pl.pallas_call(
        functools.partial(main_pick_kernel, groups),
        in_specs=[VMEM] * 2,
        out_specs=VMEM,
        out_shape=shape((8, PIX), F32),
        compiler_params=tile_params(16),
        cost_estimate=cost(2 * CIN * groups * LOW * PIX, 2 * 8 * PIX),
        name="recv_pick",
    )(index, source)

    pads, rims_in, own, w1, *sends = pl.pallas_call(
        functools.partial(border_kernel, tile_count, direct),
        in_specs=[SMEM] * 3 + [VMEM] * (3 + n_send),
        out_specs=[VMEM] * (4 + n_send),
        out_shape=[
            shape((4, 8, SIDE), F32),
            shape((4, CH, SIDE), F32),
            shape((4, CH, SIDE), BF16),
            shape((CH, 96), BF16),
        ]
        + sent((CH, SIDE), BF16),
        scratch_shapes=[
            pltpu.VMEM((5 + tile_count, COMB, SIDE), BF16),
            pltpu.VMEM((CH, 96), F32),
            pltpu.VMEM((96, 4 * SIDE), F32),
        ],
        compiler_params=tile_params(16),
        name="border",
    )(scal, neighbour, facing, strips, comb, conv_first, *arrived)
    arrived = exchange(sends)

    hidden, grad, g1, g2 = pl.pallas_call(
        middle_kernel,
        grid=(STEPS,),
        in_specs=[
            whole((8, PIX)),
            whole((4, 8, SIDE)),
            whole((4, CH, SIDE)),
            whole((CH, 96)),
            row_block(),
            row_block(),
            row_before(),
            row_after(),
        ],
        out_specs=[row_block(), row_block(), whole((CH, 96)), whole((3 * CH, 3 * CH))],
        out_shape=[
            shape((CH, PIX), BF16),
            shape((CH, PIX), BF16),
            shape((CH, 96), F32),
            shape((3 * CH, 3 * CH), F32),
        ],
        scratch_shapes=[pltpu.VMEM((32, (SIDE + 2) * SIDE), BF16)],
        compiler_params=tile_params(40),
        cost_estimate=cost(2 * 9 * CH * CH * PIX, 12 * CH * PIX),
        name="middle",
    )(tiles, pads, rims_in, w1, hg, cot, cot, cot)

    scale = 1.0 / math.sqrt(map_count * chans * cores * tile_count * PIX)
    fast_sum = direct and chans == 2 and cores == 2
    half = 3 * CH // 2 if fast_sum else 3 * CH
    top = pl.BlockSpec((CH, SIDE), lambda i: (0, 0))
    bottom = pl.BlockSpec((CH, SIDE), lambda i: (0, SIDE - 1))
    smem = pl.BlockSpec(memory_space=pltpu.SMEM)
    pads2, fringe, keep, send = pl.pallas_call(
        functools.partial(close_kernel, tile_count, direct, scale),
        grid=(1,),
        in_specs=[smem, smem, smem, whole((4, CH, SIDE)), whole((2, 3 * CH, SIDE)), top, bottom]
        + [whole((CH, 96)), whole((3 * CH, 3 * CH)), whole((3 * CH, 3 * CH))]
        + [whole(x.shape) for x in arrived],
        out_specs=[whole((2, CH, SIDE)), whole((2, CH, SIDE)), whole((half, LOW)), whole((half, LOW))],
        out_shape=[
            shape((2, CH, SIDE), BF16),
            shape((2, CH, SIDE), F32),
            shape((half, LOW), F32),
            shape((half, LOW), F32),
        ],
        scratch_shapes=[pltpu.VMEM((5 + tile_count, CH, SIDE), BF16), pltpu.VMEM((3 * CH, LOW), F32)],
        compiler_params=tile_params(16),
        name="close",
    )(scal, neighbour, facing, own, ends, cot, cot, g1, g2, fwd_w, *arrived)

    def convolve(start, count, out):
        steps = [] if out is None else [out]
        return pl.pallas_call(
            functools.partial(output_kernel, start),
            grid=(count,),
            in_specs=[
                row_block(start),
                row_before(start),
                row_after(start),
                whole((2, CH, SIDE)),
                whole((2, CH, SIDE)),
                whole((3 * CH, 3 * CH)),
            ]
            + [pl.BlockSpec(memory_space=pl.ANY)] * len(steps),
            out_specs=row_block(start),
            out_shape=shape((CH, PIX), BF16),
            input_output_aliases={6: 0} if steps else {},
            compiler_params=tile_params(32),
            cost_estimate=cost(2 * 9 * CH * CH * PIX * count // STEPS, 4 * CH * PIX * count // STEPS),
            name="output",
        )(hidden, hidden, hidden, pads2, fringe, fwd_w, *steps)

    finals = [shape((9, CH, CIN), F32), shape((9, CH, CH), F32)]
    if fast_sum:
        swap = lambda x, name: lax.ppermute(x, name, [(0, 1), (1, 0)])
        quarter = half // 2
        got = swap(send, "sub")
        out = convolve(0, 2, None)
        keep2, send2 = pl.pallas_call(
            pair_kernel,
            in_specs=[SMEM, VMEM, VMEM],
            out_specs=[VMEM, VMEM],
            out_shape=[shape((quarter, LOW), F32)] * 2,
            scratch_shapes=[pltpu.VMEM((half, LOW), F32)],
            name="pair",
        )(scal, keep, got)
        got = swap(send2, "chan")
        out = convolve(2, 2, out)
        mine = keep2 + got
        got = exchange([mine] * n_send)
        out = convolve(4, 4, out)
        mine = pl.pallas_call(
            functools.partial(ring_kernel, tile_count),
            in_specs=[SMEM] + [VMEM] * tile_count,
            out_specs=VMEM,
            out_shape=shape((quarter, LOW), F32),
            scratch_shapes=[pltpu.VMEM((tile_count, quarter, LOW), F32)],
            name="ring",
        )(scal, mine, *got)
        got = swap(mine, "chan")
        mine = pl.pallas_call(
            join_kernel,
            in_specs=[SMEM, VMEM, VMEM],
            out_specs=VMEM,
            out_shape=shape((half, LOW), F32),
            name="join",
        )(scal, mine, got)
        got = swap(mine, "sub")
        first, second = pl.pallas_call(
            last_kernel,
            in_specs=[SMEM, VMEM, VMEM],
            out_specs=[VMEM, VMEM],
            out_shape=finals,
            scratch_shapes=[pltpu.VMEM((3 * CH, LOW), F32)],
            name="last",
        )(scal, mine, got)
    else:
        out = convolve(0, STEPS, None)
        total = lax.psum(keep, ("tile", "chan", "sub"))
        first, second = pl.pallas_call(
            unpack, in_specs=[VMEM], out_specs=[VMEM, VMEM], out_shape=finals, name="unpack"
        )(total)
    return (out.reshape(1, CH, PIX), grad.reshape(1, CH, PIX), first, second)


def solution(mesh):
    in_specs = (
        P(("groups", "chan", "sub"), None, "tile"),
        P("tile"),
        P("tile"),
        P(),
        P(),
        P(),
        P(),
        P(("groups", "chan", "sub"), None, "tile"),
    )
    out_specs = (
        P(("groups", "chan", "sub"), None, "tile"),
        P(("groups", "chan", "sub"), None, "tile"),
        P("groups", None, None),
        P("groups", None, None),
    )
    return jax.shard_map(body, mesh=mesh, in_specs=in_specs, out_specs=out_specs, check_vma=False)
```

time: 569 us -> 94.6 us (0.17)
  local copies, waits for them, and re-layouts: 351 us -> 11.3 us
  blocking collectives: 99.6 us -> 0 us
  Pallas kernels: 0 us -> 48.2 us
  matrix products: 39.4 us -> 0 us
  other arithmetic: 26.4 us -> 0.88 us
  waiting for transfers between devices: 26.4 us -> 11 us
  starting transfers between devices: 6.45 us -> 21.8 us
  between operations: 14.8 us -> 0.81 us
    gather x4 -> x0, local copies, waits for them, and re-layouts: 153 us -> none  [the longest x2 90.6 us: body(): jnp.take(extended, send_pick, axis=2)]
    psum x1 -> x0, blocking collectives: 58 us -> none  [body(): lax.psum((first_term, second_term), ('tile', 'chan', 'sub'))]
    pallas_call x0 -> x14, Pallas kernels: none -> 48.2 us  [the longest x1 11.6 us: body(): pl.pallas_call(middle_kernel, grid=(STEPS,), in_specs=[whole((8, PIX)), w...]
    all_gather x3 -> x0, blocking collectives: 41.6 us -> none  [the longest x1 14.4 us: body(): lax.all_gather(rim_strips, 'tile', axis=0, tiled=True)]
    another operation x36 -> x0, local copies, waits for them, and re-layouts: 39.6 us -> none
    dot_general x8 -> x0, matrix products: 39.4 us -> none  [the longest x1 19.4 us: spread(): jnp.einsum('poc,bpoij->bcij', weights, windows(wide, SIDE + 2, 2), prefer...]
    unnamed x41 -> x42, local copies, waits for them, and re-layouts: 49.3 us -> 11.3 us
    scatter x8 -> x0, local copies, waits for them, and re-layouts: 35.7 us -> none  [the longest x2 17.6 us: with_rims(): padded = padded.at[:, :, 1:-1, -1].set(incoming[1])]
  transfers between devices with their start and end apart: 2 -> 16, of which waited for: 1 -> 6; matrix products, arithmetic and copies ran while one was open for 28% -> 0% of each run, Pallas kernels for 0% -> 32%
where the time goes in v1:
time: 94.6 us; the launch traced here: 94.1 us
  Pallas kernels  48.2 us (51%)
  starting transfers between devices  21.8 us (23%)
  local copies, waits for them, and re-layouts  11.3 us (12%)
  waiting for transfers between devices  11 us (12%)
    ppermute x12, starting transfers between devices, exchange(): lax.ppermute(x, 'tile', [(i, (i + s) % tile_count) for i in range(tile_co...  18.8 us
    pallas_call x1, Pallas kernels, body(): pl.pallas_call(middle_kernel, grid=(STEPS,), in_specs=[whole((8, PIX)), w...  11.6 us
    unnamed x42, local copies, waits for them, and re-layouts  11.3 us
    pallas_call x1, Pallas kernels, body(): pl.pallas_call(functools.partial(send_kernel, tile_count, direct), in_spe...  8.07 us
    pallas_call x3, Pallas kernels, convolve(): pl.pallas_call(functools.partial(output_kernel, start), grid=(count,), in...  7.15 us
    ppermute x4, waiting for transfers between devices, body(): swap = lambda x, name: lax.ppermute(x, name, [(0, 1), (1, 0)])  6.92 us
    pallas_call x1, Pallas kernels, body(): pl.pallas_call(frame_kernel, grid=(STEPS,), in_specs=[row_block(), row_be...  5.97 us
    pallas_call x1, Pallas kernels, body(): pl.pallas_call(functools.partial(main_pick_kernel, groups), in_specs=[VME...  5.58 us
  transfers between devices with their start and end apart: 16, of which 6 were waited for; matrix products, arithmetic and copies ran while one was open for 0% of the time, Pallas kernels for 32%

profile of v1, /device:TPU:0, one launch (start us, length us, event | category | flops | bytes accessed | tf_op | source)
XLA Modules:
  0.0 94.1 jit_solution(12343283253475521234)
XLA Ops:
  2.5 8.1 %send_pick.1 = (bf16[3,24,256]{2,1,0:T(8,128)(2,1)S(1)}, bf16[3,24,256]{2,1,0:T(8,128)(2,1)S(1)}, bf16[3,24,256]{2,1,0:T(8,128)(2,1)S(1)}, bf16[3,24,256]{2,1,0:T(8,128)(2,1)S(1)}) custom-call(s32[3]{0:T(128)S(1)} %pad_add_fusion.scal, bf16[3,16384]{1,0:T(4,128)(2,1)S(1)} %bitcast.17, s32[192,128]{1,0:T(8,128)S(1)} %bitcast.18), custom_call_target="tpu_custom_call" | custom-call | tf_op jit(solution)/shard_map/send_pick/pallas_call | solution.py:604
  10.6 3.1 %collective-permute-start = (bf16[3,24,256]{2,1,0:T(8,128)(2,1)S(1)}, bf16[3,24,256]{2,1,0:T(8,128)(2,1)S(1)}, u32[]{:S(2)}, u32[]{:S(2)}) collective-permute-start(bf16[3,24,256]{2,1,0:T(8,128)(2,1)S(1)} %get-tuple-element.39), channel_id=1, source_target_pairs={{0,4},{4,8},{8,12},{12,0},{1,5},{5,9},{9,13},{13,1},{2,6},{6,10},{... | collective-permute-start | bytes 110600 | tf_op jit(solution)/shard_map/ppermute | solution.py:590
  13.7 2.6 %collective-permute-start.1 = (bf16[3,24,256]{2,1,0:T(8,128)(2,1)S(1)}, bf16[3,24,256]{2,1,0:T(8,128)(2,1)S(1)}, u32[]{:S(2)}, u32[]{:S(2)}) collective-permute-start(bf16[3,24,256]{2,1,0:T(8,128)(2,1)S(1)} %get-tuple-element.40), channel_id=1, source_target_pairs={{0,8},{4,12},{8,0},{12,4},{1,9},{5,13},{9,1},{13,5},{2,10},{6,14},... | collective-permute-start | bytes 110600 | tf_op jit(solution)/shard_map/ppermute | solution.py:590
  17.6 1.6 %copy-done = bf16[1,64,16384]{2,1,0:T(8,128)(2,1)S(1)} copy-done((bf16[1,64,16384]{2,1,0:T(8,128)(2,1)S(1)}, bf16[1,64,16384]{2,1,0:T(8,128)(2,1)}, u32[]{:S(2)}) %copy-start) | copy-done | bytes 2097176
  20.1 6.0 %frame.1 = (f32[64,16384]{1,0:T(8,128)S(1)}, bf16[4,64,128]{2,1,0:T(8,128)(2,1)S(1)}, bf16[2,192,128]{2,1,0:T(8,128)(2,1)S(1)}, bf16[192,192]{1,0:T(8,128)(2,1)S(1)}) custom-call(bf16[64,16384]{1,0:T(8,128)(2,1)S(1)} %bitcast.9, bf16[64,16384]{1,0:T(8,128)(2,1)S(1)} %bitcast.10, bf16[64,16384]{1,0:T(8,128)(2,1)S(1)} %bitcast.11, bf16[9,64,64]{2,1,0:T(8,128)(2,1)S(1)} %copy-done.4), custom_call_target="tpu_custom_call" | custom-call | flops 1207959552 | bytes 6291456 | tf_op jit(solution)/shard_map/frame/pallas_call | solution.py:622
  26.1 2.0 %copy-done.2 = f32[64,16384]{1,0:T(8,128)} copy-done((f32[64,16384]{1,0:T(8,128)}, f32[64,16384]{1,0:T(8,128)S(1)}, u32[]{:S(2)}) %copy-start.2) | copy-done | bytes 4194328
  30.4 2.8 %collective-permute-start.5 = (bf16[80,128]{1,0:T(8,128)(2,1)S(1)}, bf16[80,128]{1,0:T(8,128)(2,1)S(1)}, u32[]{:S(2)}, u32[]{:S(2)}) collective-permute-start(bf16[80,128]{1,0:T(8,128)(2,1)S(1)} %get-tuple-element.47), channel_id=1, source_target_pairs={{0,12},{4,0},{8,4},{12,8},{1,13},{5,1},{9,5},{13,9},{2,14},{6,2},{... | collective-permute-start | bytes 61448 | tf_op jit(solution)/shard_map/ppermute | solution.py:590
  33.2 5.6 %recv_pick.1.tiles = f32[8,16384]{1,0:T(8,128)S(1)} custom-call(s32[128,128]{1,0:T(8,128)S(1)} %bitcast.20, bf16[288,256]{1,0:T(8,128)(2,1)S(1)} %get-tuple-element.42.source), custom_call_target="tpu_custom_call" | custom-call | flops 2415919104 | bytes 262144 | tf_op jit(solution)/shard_map/recv_pick/pallas_call | solution.py:652
  40.6 1.5 %collective-permute-start.7 = (bf16[64,128]{1,0:T(8,128)(2,1)S(1)}, bf16[64,128]{1,0:T(8,128)(2,1)S(1)}, u32[]{:S(2)}, u32[]{:S(2)}) collective-permute-start(bf16[64,128]{1,0:T(8,128)(2,1)S(1)} %get-tuple-element.59), channel_id=1, source_target_pairs={{0,8},{4,12},{8,0},{12,4},{1,9},{5,13},{9,1},{13,5},{2,10},{6,14},... | collective-permute-start | bytes 49160 | tf_op jit(solution)/shard_map/ppermute | solution.py:590
  42.1 2.8 %collective-permute-start.8 = (bf16[64,128]{1,0:T(8,128)(2,1)S(1)}, bf16[64,128]{1,0:T(8,128)(2,1)S(1)}, u32[]{:S(2)}, u32[]{:S(2)}) collective-permute-start(bf16[64,128]{1,0:T(8,128)(2,1)S(1)} %get-tuple-element.60), channel_id=1, source_target_pairs={{0,12},{4,0},{8,4},{12,8},{1,13},{5,1},{9,5},{13,9},{2,14},{6,2},{... | collective-permute-start | bytes 49160 | tf_op jit(solution)/shard_map/ppermute | solution.py:590
  45.0 11.6 %middle.1 = (bf16[64,16384]{1,0:T(8,128)(2,1)S(1)}, bf16[64,16384]{1,0:T(8,128)(2,1)}, f32[64,96]{1,0:T(8,128)S(1)}, f32[192,192]{1,0:T(8,128)S(1)}) custom-call(f32[8,16384]{1,0:T(8,128)S(1)} %recv_pick.1.tiles, f32[4,8,128]{2,1,0:T(8,128)S(1)} %get-tuple-element.48.pads, f32[4,64,128]{2,1,0:T(8,128)S(1)} %get-tuple-element.49.rims_in, ...), custom_call_target="tpu_custom_call" | custom-call | flops 1207959552 | bytes 12582912 | tf_op jit(solution)/shard_map/middle/pallas_call | solution.py:683
  60.4 1.6 %pair.1 = (f32[48,256]{1,0:T(8,128)}, f32[48,256]{1,0:T(8,128)}) custom-call(s32[3]{0:T(128)} %copy-done.9, f32[96,256]{1,0:T(8,128)} %copy-done.7, f32[96,256]{1,0:T(8,128)} %copy-done.14), custom_call_target="tpu_custom_call" | custom-call | tf_op jit(solution)/shard_map/pair/pallas_call | solution.py:761
  61.9 1.5 %collective-permute-start.10 = (f32[48,256]{1,0:T(8,128)}, f32[48,256]{1,0:T(8,128)S(1)}, u32[]{:S(2)}, u32[]{:S(2)}) collective-permute-start(f32[48,256]{1,0:T(8,128)} %get-tuple-element.67), channel_id=1, source_target_pairs={{0,2},{2,0},{1,3},{3,1},{4,6},{6,4},{5,7},{7,5},{8,10},{10,8},{9,1... | collective-permute-start | bytes 147464 | tf_op jit(solution)/shard_map/ppermute | solution.py:757
  63.4 2.8 %collective-permute-done.10 = f32[48,256]{1,0:T(8,128)S(1)} collective-permute-done((f32[48,256]{1,0:T(8,128)}, f32[48,256]{1,0:T(8,128)S(1)}, u32[]{:S(2)}, u32[]{:S(2)}) %collective-permute-start.10) | collective-permute-done | bytes 49184 | tf_op jit(solution)/shard_map/ppermute | solution.py:757
  68.1 1.9 %collective-permute-start.11 = (f32[48,256]{1,0:T(8,128)S(1)}, f32[48,256]{1,0:T(8,128)S(1)}, u32[]{:S(2)}, u32[]{:S(2)}) collective-permute-start(f32[48,256]{1,0:T(8,128)S(1)} %add.3.mine), channel_id=1, source_target_pairs={{0,4},{4,8},{8,12},{12,0},{1,5},{5,9},{9,13},{13,1},{2,6},{6,10},{... | collective-permute-start | bytes 147464 | tf_op jit(solution)/shard_map/ppermute | solution.py:590
  71.2 1.5 %collective-permute-done.12.rest_1_ = f32[48,256]{1,0:T(8,128)S(1)} collective-permute-done((f32[48,256]{1,0:T(8,128)S(1)}, f32[48,256]{1,0:T(8,128)S(1)}, u32[]{:S(2)}, u32[]{:S(2)}) %collective-permute-start.12) | collective-permute-done | bytes 49184 | tf_op jit(solution)/shard_map/ppermute | solution.py:590
  74.7 1.5 %ring.1.mine = f32[48,256]{1,0:T(8,128)} custom-call(s32[3]{0:T(128)} %copy-done.9, f32[48,256]{1,0:T(8,128)} %copy-done.12, f32[48,256]{1,0:T(8,128)} %copy-done.18, f32[48,256]{1,0:T(8,128)} %copy-done.17, f32[48,256]{1,0:T(8,128)} %copy-done.16), custom_call_target="tpu_custom_call" | custom-call | tf_op jit(solution)/shard_map/ring/pallas_call | solution.py:774
  76.2 1.5 %collective-permute-start.14 = (f32[48,256]{1,0:T(8,128)}, f32[48,256]{1,0:T(8,128)S(1)}, u32[]{:S(2)}, u32[]{:S(2)}) collective-permute-start(f32[48,256]{1,0:T(8,128)} %ring.1.mine), channel_id=1, source_target_pairs={{0,2},{2,0},{1,3},{3,1},{4,6},{6,4},{5,7},{7,5},{8,10},{10,8},{9,1... | collective-permute-start | bytes 147464 | tf_op jit(solution)/shard_map/ppermute | solution.py:757
  77.7 2.8 %collective-permute-done.14.got = f32[48,256]{1,0:T(8,128)S(1)} collective-permute-done((f32[48,256]{1,0:T(8,128)}, f32[48,256]{1,0:T(8,128)S(1)}, u32[]{:S(2)}, u32[]{:S(2)}) %collective-permute-start.14) | collective-permute-done | bytes 49184 | tf_op jit(solution)/shard_map/ppermute | solution.py:757
  82.6 1.9 %output.3.rest_0_ = bf16[64,16384]{1,0:T(8,128)(2,1)} custom-call(bf16[64,16384]{1,0:T(8,128)(2,1)S(1)} %get-tuple-element.52.hid.prev.nxt, bf16[64,16384]{1,0:T(8,128)(2,1)S(1)} %get-tuple-element.52.hid.prev.nxt, bf16[64,16384]{1,0:T(8,128)(2,1)S(1)} %get-tuple-element.52.hid.prev.nxt, bf16[2,64,128]{2,1,0:T(8,128)(2,1)S(1)} %get-tuple-element.61.pads, ...), custom_call_target="tpu_custom_call" | custom-call | flops 301989888 | bytes 1048576 | tf_op jit(solution)/shard_map/output/pallas_call | solution.py:735
  84.6 2.0 %output.4.rest_0_ = bf16[64,16384]{1,0:T(8,128)(2,1)} custom-call(bf16[64,16384]{1,0:T(8,128)(2,1)S(1)} %get-tuple-element.52.hid.prev.nxt, bf16[64,16384]{1,0:T(8,128)(2,1)S(1)} %get-tuple-element.52.hid.prev.nxt, bf16[64,16384]{1,0:T(8,128)(2,1)S(1)} %get-tuple-element.52.hid.prev.nxt, ...), custom_call_target="tpu_custom_call", output_to_operand_aliasing={{}: (6, {})} | custom-call | flops 301989888 | bytes 1048576 | tf_op jit(solution)/shard_map/output/pallas_call | solution.py:735
  86.5 3.3 %output.5 = bf16[64,16384]{1,0:T(8,128)(2,1)} custom-call(bf16[64,16384]{1,0:T(8,128)(2,1)S(1)} %get-tuple-element.52.hid.prev.nxt, bf16[64,16384]{1,0:T(8,128)(2,1)S(1)} %get-tuple-element.52.hid.prev.nxt, bf16[64,16384]{1,0:T(8,128)(2,1)S(1)} %get-tuple-element.52.hid.prev.nxt, ...), custom_call_target="tpu_custom_call", output_to_operand_aliasing={{}: (6, {})} | custom-call | flops 603979776 | bytes 2097152 | tf_op jit(solution)/shard_map/output/pallas_call | solution.py:735
  90.4 1.9 %last.1 = (f32[9,64,3]{2,1,0:T(8,128)}, f32[9,64,64]{2,1,0:T(8,128)}) custom-call(s32[3]{0:T(128)} %copy-done.9, f32[96,256]{1,0:T(8,128)} %join.1.mine, f32[96,256]{1,0:T(8,128)} %copy-done.13), custom_call_target="tpu_custom_call" | custom-call | tf_op jit(solution)/shard_map/last/pallas_call | solution.py:791
  92.4 1.7 %copy.15 = f32[9,64,3]{1,2,0:T(4,128)} copy(f32[9,64,3]{2,1,0:T(8,128)} %get-tuple-element.72) | data formatting | bytes 13824
  (66 shorter events, 19.6 us)
Async XLA Ops:
  0.7 55.9 %copy-start.9 = (s32[3]{0:T(128)}, s32[3]{0:T(128)S(1)}, u32[]{:S(2)}) copy-start(s32[3]{0:T(128)S(1)} %pad_add_fusion.scal) | copy-start | bytes 40
  10.6 17.7 %collective-permute-start = (bf16[3,24,256]{2,1,0:T(8,128)(2,1)S(1)}, bf16[3,24,256]{2,1,0:T(8,128)(2,1)S(1)}, u32[]{:S(2)}, u32[]{:S(2)}) collective-permute-start(bf16[3,24,256]{2,1,0:T(8,128)(2,1)S(1)} %get-tuple-element.39), channel_id=1, source_target_pairs={{0,4},{4,8},{8,12},{12,0},{1,5},{5,9},{9,13},{13,1},{2,6},{6,10},{... | collective-permute-start | bytes 110600 | tf_op jit(solution)/shard_map/ppermute | solution.py:590
  13.7 14.6 %collective-permute-start.1 = (bf16[3,24,256]{2,1,0:T(8,128)(2,1)S(1)}, bf16[3,24,256]{2,1,0:T(8,128)(2,1)S(1)}, u32[]{:S(2)}, u32[]{:S(2)}) collective-permute-start(bf16[3,24,256]{2,1,0:T(8,128)(2,1)S(1)} %get-tuple-element.40), channel_id=1, source_target_pairs={{0,8},{4,12},{8,0},{12,4},{1,9},{5,13},{9,1},{13,5},{2,10},{6,14},... | collective-permute-start | bytes 110600 | tf_op jit(solution)/shard_map/ppermute | solution.py:590
  16.3 12.0 %collective-permute-start.2 = (bf16[3,24,256]{2,1,0:T(8,128)(2,1)S(1)}, bf16[3,24,256]{2,1,0:T(8,128)(2,1)S(1)}, u32[]{:S(2)}, u32[]{:S(2)}) collective-permute-start(bf16[3,24,256]{2,1,0:T(8,128)(2,1)S(1)} %get-tuple-element.41), channel_id=1, source_target_pairs={{0,12},{4,0},{8,4},{12,8},{1,13},{5,1},{9,5},{13,9},{2,14},{6,2},{... | collective-permute-start | bytes 110600 | tf_op jit(solution)/shard_map/ppermute | solution.py:590
  20.1 8.0 %copy-start.19 = (bf16[9,64,3]{1,2,0:T(4,128)(2,1)S(1)}, bf16[9,64,3]{1,2,0:T(4,128)(2,1)}, u32[]{:S(2)}) copy-start(bf16[9,64,3]{1,2,0:T(4,128)(2,1)} %param.13) | copy-start | bytes 10372
  20.1 8.2 %copy-start.8 = (s32[16384]{0:T(1024)S(1)}, s32[16384]{0:T(1024)}, u32[]{:S(2)}) copy-start(s32[16384]{0:T(1024)} %param.10) | copy-start | bytes 196612
  20.1 8.2 %copy-start.10 = (s32[4,4]{1,0:T(4,128)S(1)}, s32[4,4]{1,0:T(4,128)}, u32[]{:S(2)}) copy-start(s32[4,4]{1,0:T(4,128)} %nbr.5) | copy-start | bytes 196
  29.4 9.4 %collective-permute-start.3 = (bf16[80,128]{1,0:T(8,128)(2,1)S(1)}, bf16[80,128]{1,0:T(8,128)(2,1)S(1)}, u32[]{:S(2)}, u32[]{:S(2)}) collective-permute-start(bf16[80,128]{1,0:T(8,128)(2,1)S(1)} %get-tuple-element.45), channel_id=1, source_target_pairs={{0,4},{4,8},{8,12},{12,0},{1,5},{5,9},{9,13},{13,1},{2,6},{6,10},{... | collective-permute-start | bytes 61448 | tf_op jit(solution)/shard_map/ppermute | solution.py:590
  30.1 8.8 %collective-permute-start.4 = (bf16[80,128]{1,0:T(8,128)(2,1)S(1)}, bf16[80,128]{1,0:T(8,128)(2,1)S(1)}, u32[]{:S(2)}, u32[]{:S(2)}) collective-permute-start(bf16[80,128]{1,0:T(8,128)(2,1)S(1)} %get-tuple-element.46), channel_id=1, source_target_pairs={{0,8},{4,12},{8,0},{12,4},{1,9},{5,13},{9,1},{13,5},{2,10},{6,14},... | collective-permute-start | bytes 61448 | tf_op jit(solution)/shard_map/ppermute | solution.py:590
  30.4 8.4 %collective-permute-start.5 = (bf16[80,128]{1,0:T(8,128)(2,1)S(1)}, bf16[80,128]{1,0:T(8,128)(2,1)S(1)}, u32[]{:S(2)}, u32[]{:S(2)}) collective-permute-start(bf16[80,128]{1,0:T(8,128)(2,1)S(1)} %get-tuple-element.47), channel_id=1, source_target_pairs={{0,12},{4,0},{8,4},{12,8},{1,13},{5,1},{9,5},{13,9},{2,14},{6,2},{... | collective-permute-start | bytes 61448 | tf_op jit(solution)/shard_map/ppermute | solution.py:590
  33.2 5.6 %copy-start.11 = (s32[4,4]{1,0:T(4,128)S(1)}, s32[4,4]{1,0:T(4,128)}, u32[]{:S(2)}) copy-start(s32[4,4]{1,0:T(4,128)} %fac.3) | copy-start | bytes 196
  33.2 11.8 %copy-start.1 = (bf16[1,64,16384]{2,1,0:T(8,128)(2,1)S(1)}, bf16[1,64,16384]{2,1,0:T(8,128)(2,1)}, u32[]{:S(2)}) copy-start(bf16[1,64,16384]{2,1,0:T(8,128)(2,1)} %param.15) | copy-start | bytes 6291460
  33.2 11.8 %copy-start.3 = (f32[64,16384]{1,0:T(8,128)S(1)}, f32[64,16384]{1,0:T(8,128)}, u32[]{:S(2)}) copy-start(f32[64,16384]{1,0:T(8,128)} %copy-done.2) | copy-start | bytes 12582916
  40.0 16.6 %collective-permute-start.6 = (bf16[64,128]{1,0:T(8,128)(2,1)S(1)}, bf16[64,128]{1,0:T(8,128)(2,1)S(1)}, u32[]{:S(2)}, u32[]{:S(2)}) collective-permute-start(bf16[64,128]{1,0:T(8,128)(2,1)S(1)} %get-tuple-element.58), channel_id=1, source_target_pairs={{0,4},{4,8},{8,12},{12,0},{1,5},{5,9},{9,13},{13,1},{2,6},{6,10},{... | collective-permute-start | bytes 49160 | tf_op jit(solution)/shard_map/ppermute | solution.py:590
  40.6 16.0 %collective-permute-start.7 = (bf16[64,128]{1,0:T(8,128)(2,1)S(1)}, bf16[64,128]{1,0:T(8,128)(2,1)S(1)}, u32[]{:S(2)}, u32[]{:S(2)}) collective-permute-start(bf16[64,128]{1,0:T(8,128)(2,1)S(1)} %get-tuple-element.59), channel_id=1, source_target_pairs={{0,8},{4,12},{8,0},{12,4},{1,9},{5,13},{9,1},{13,5},{2,10},{6,14},... | collective-permute-start | bytes 49160 | tf_op jit(solution)/shard_map/ppermute | solution.py:590
  42.1 14.5 %collective-permute-start.8 = (bf16[64,128]{1,0:T(8,128)(2,1)S(1)}, bf16[64,128]{1,0:T(8,128)(2,1)S(1)}, u32[]{:S(2)}, u32[]{:S(2)}) collective-permute-start(bf16[64,128]{1,0:T(8,128)(2,1)S(1)} %get-tuple-element.60), channel_id=1, source_target_pairs={{0,12},{4,0},{8,4},{12,8},{1,13},{5,1},{9,5},{13,9},{2,14},{6,2},{... | collective-permute-start | bytes 49160 | tf_op jit(solution)/shard_map/ppermute | solution.py:590
  58.4 1.3 %collective-permute-start.9 = (f32[96,256]{1,0:T(8,128)S(1)}, f32[96,256]{1,0:T(8,128)S(1)}, u32[]{:S(2)}, u32[]{:S(2)}) collective-permute-start(f32[96,256]{1,0:T(8,128)S(1)} %get-tuple-element.65), channel_id=1, source_target_pairs={{0,1},{1,0},{2,3},{3,2},{4,5},{5,4},{6,7},{7,6},{8,9},{9,8},{10,11... | collective-permute-start | bytes 294920 | tf_op jit(solution)/shard_map/ppermute | solution.py:757
  61.9 4.3 %collective-permute-start.10 = (f32[48,256]{1,0:T(8,128)}, f32[48,256]{1,0:T(8,128)S(1)}, u32[]{:S(2)}, u32[]{:S(2)}) collective-permute-start(f32[48,256]{1,0:T(8,128)} %get-tuple-element.67), channel_id=1, source_target_pairs={{0,2},{2,0},{1,3},{3,1},{4,6},{6,4},{5,7},{7,5},{8,10},{10,8},{9,1... | collective-permute-start | bytes 147464 | tf_op jit(solution)/shard_map/ppermute | solution.py:757
  67.1 7.0 %copy-start.12 = (f32[48,256]{1,0:T(8,128)}, f32[48,256]{1,0:T(8,128)S(1)}, u32[]{:S(2)}) copy-start(f32[48,256]{1,0:T(8,128)S(1)} %add.3.mine) | copy-start | bytes 147460
  67.1 4.1 %collective-permute-start.13 = (f32[48,256]{1,0:T(8,128)S(1)}, f32[48,256]{1,0:T(8,128)S(1)}, u32[]{:S(2)}, u32[]{:S(2)}) collective-permute-start(f32[48,256]{1,0:T(8,128)S(1)} %add.3.mine), channel_id=1, source_target_pairs={{0,12},{4,0},{8,4},{12,8},{1,13},{5,1},{9,5},{13,9},{2,14},{6,2},{... | collective-permute-start | bytes 147464 | tf_op jit(solution)/shard_map/ppermute | solution.py:590
  67.1 5.5 %collective-permute-start.12 = (f32[48,256]{1,0:T(8,128)S(1)}, f32[48,256]{1,0:T(8,128)S(1)}, u32[]{:S(2)}, u32[]{:S(2)}) collective-permute-start(f32[48,256]{1,0:T(8,128)S(1)} %add.3.mine), channel_id=1, source_target_pairs={{0,8},{4,12},{8,0},{12,4},{1,9},{5,13},{9,1},{13,5},{2,10},{6,14},... | collective-permute-start | bytes 147464 | tf_op jit(solution)/shard_map/ppermute | solution.py:590
  68.1 6.0 %collective-permute-start.11 = (f32[48,256]{1,0:T(8,128)S(1)}, f32[48,256]{1,0:T(8,128)S(1)}, u32[]{:S(2)}, u32[]{:S(2)}) collective-permute-start(f32[48,256]{1,0:T(8,128)S(1)} %add.3.mine), channel_id=1, source_target_pairs={{0,4},{4,8},{8,12},{12,0},{1,5},{5,9},{9,13},{13,1},{2,6},{6,10},{... | collective-permute-start | bytes 147464 | tf_op jit(solution)/shard_map/ppermute | solution.py:590
  76.2 4.3 %collective-permute-start.14 = (f32[48,256]{1,0:T(8,128)}, f32[48,256]{1,0:T(8,128)S(1)}, u32[]{:S(2)}, u32[]{:S(2)}) collective-permute-start(f32[48,256]{1,0:T(8,128)} %ring.1.mine), channel_id=1, source_target_pairs={{0,2},{2,0},{1,3},{3,1},{4,6},{6,4},{5,7},{7,5},{8,10},{10,8},{9,1... | collective-permute-start | bytes 147464 | tf_op jit(solution)/shard_map/ppermute | solution.py:757
  82.6 7.2 %collective-permute-start.15 = (f32[96,256]{1,0:T(8,128)}, f32[96,256]{1,0:T(8,128)S(1)}, u32[]{:S(2)}, u32[]{:S(2)}) collective-permute-start(f32[96,256]{1,0:T(8,128)} %join.1.mine), channel_id=1, source_target_pairs={{0,1},{1,0},{2,3},{3,2},{4,5},{5,4},{6,7},{7,6},{8,9},{9,8},{10,11... | collective-permute-start | bytes 294920 | tf_op jit(solution)/shard_map/ppermute | solution.py:757
  (12 other events, 13.7 us)

commit v2 on v1

v2 whole, which is shorter than its diff:
```python
import functools
import math

import jax
import jax.numpy as jnp
from jax import lax
from jax.experimental import pallas as pl
from jax.experimental.pallas import tpu as pltpu
from jax.sharding import PartitionSpec as P

SIDE = 128
PIX = SIDE * SIDE
CH = 64
CIN = 3
LOW = 256
COMB = 96
ROWS = 16
STEPS = SIDE // ROWS
F32 = jnp.float32
BF16 = jnp.bfloat16
SMEM = pl.BlockSpec(memory_space=pltpu.SMEM)
VMEM = pl.BlockSpec(memory_space=pltpu.VMEM)


def iota(shape, dim):
    return lax.broadcasted_iota(jnp.int32, shape, dim)


def hot(a, b):
    return jnp.where(a == b, 1.0, 0.0).astype(BF16)


def dot(a, b):
    return jnp.dot(a, b, preferred_element_type=F32)


def dot_nt(a, b):
    return lax.dot_general(a, b, (((1,), (1,)), ((), ())), preferred_element_type=F32)


def reverse(strip):
    swap = hot(iota((SIDE, SIDE), 0) + iota((SIDE, SIDE), 1), SIDE - 1)
    return dot(strip.astype(BF16), swap)


def from_left(x):
    return jnp.where(iota(x.shape, 1) == 0, 0.0, pltpu.roll(x, 1, 1))


def from_right(x):
    return jnp.where(iota(x.shape, 1) == SIDE - 1, 0.0, pltpu.roll(x, SIDE - 1, 1))


def ends_table(shift, east):
    src = iota((SIDE, 2 * SIDE), 0)
    lane = iota((SIDE, 2 * SIDE), 1)
    return hot(lane, 2 * (src - shift) + (0 if east else 1))


def row_ends(pairs, row):
    half = row // (SIDE // 2)
    back = lax.rem(4 * SIDE - 2 * row - 1, SIDE)
    return pltpu.roll(pairs[half], back, 1)


def is_end(shape):
    lane = iota(shape, 1)
    return (lane == 0) | (lane == SIDE - 1)


def pick_rows(low_rows, high_rows, groups, source):
    found = dot(source, hot(iota((LOW, LOW), 0), low_rows))
    lines = iota((8, LOW), 0)
    accs = [jnp.zeros((8, LOW), F32)] * CIN
    for g in range(groups // 8):
        here = lines == high_rows - 8 * g
        for c in range(CIN):
            at = c * groups + 8 * g
            accs[c] = jnp.where(here, found[at : at + 8], accs[c])
    return [jnp.sum(x, axis=0, keepdims=True) for x in accs]


def split_index(index):
    return index & (LOW - 1), index >> 8


def tile_params(limit_mib):
    return pltpu.CompilerParams(vmem_limit_bytes=limit_mib << 20)


def send_kernel(tile_count, direct, scal, cyc, index, *rest):
    outs, (stage, source, found) = rest[:-3], rest[-3:]
    groups = PIX // LOW
    per_dest = index.shape[0] // 2 // tile_count
    whole = cyc[...].astype(F32)
    for h in range(groups):
        piece = whole[:, h * LOW : (h + 1) * LOW]
        for c in range(CIN):
            stage[pl.ds(c * groups + h, 1), :] = piece[c : c + 1]
    source[...] = stage[...].astype(BF16)
    data = source[...]
    me = scal[0]

    def chunk(m, carry):
        if direct:
            dest = me ^ (m // per_dest)
            at = dest * per_dest + lax.rem(m, per_dest)
        else:
            at = m
        row = jnp.concatenate([index[pl.ds(2 * at, 1), :], index[pl.ds(2 * at + 1, 1), :]], axis=1)
        low, high = split_index(row)
        picked = pick_rows(low, high, groups, data)
        for c in range(CIN):
            found[c, pl.ds(m, 1), :] = picked[c]
        return carry

    lax.fori_loop(0, tile_count * per_dest, chunk, 0, unroll=4)
    for d in range(tile_count):
        for c in range(CIN):
            block = found[c, d * per_dest : (d + 1) * per_dest, :].astype(BF16)
            if direct:
                outs[d][c] = block
            else:
                outs[0][d, c] = block


def side_towards(nbr, me, dest):
    side = jnp.int32(0)
    for k in range(4):
        side = jnp.where(nbr[me, k] == dest, k, side)
    return side


def send_strips(tile_count, direct, nbr, me, strips, outs):
    if direct:
        for s in range(1, tile_count):
            dest = me ^ s
            outs[s - 1][...] = strips[side_towards(nbr, me, dest)]
    else:
        for dest in range(tile_count):
            outs[0][dest] = strips[side_towards(nbr, me, dest)]


def take_strips(tile_count, direct, nbr, fac, me, own, arrived, table):
    for k in range(4):
        table[k] = own[k]
    if direct:
        for s in range(1, tile_count):
            table[4 + (me ^ s)] = arrived[s - 1][...]
    else:
        for d in range(tile_count):
            table[4 + d] = arrived[0][d]
    table[4 + tile_count] = jnp.zeros(table.shape[1:], table.dtype)
    got = []
    for k in range(4):
        other = nbr[me, k]
        at = jnp.where(other == me, fac[me, k], 4 + other)
        at = jnp.where(other < 0, 4 + tile_count, at)
        got.append(table[at])
    return got


def side_ends(north, east, south, west):
    at = lambda x, i: x[:, i : i + 1]
    last = SIDE - 1
    fours = [
        (at(west, 0), at(east, 0), at(west, 1), at(east, 1)),
        (at(north, last), at(south, last), at(north, last - 1), at(south, last - 1)),
        (at(east, last), at(west, last), at(east, last - 1), at(west, last - 1)),
        (at(south, 0), at(north, 0), at(south, 1), at(north, 1)),
    ]
    lane = iota((8, SIDE), 1)
    lines = []
    for four in fours:
        line = jnp.zeros((8, SIDE), F32)
        for n, value in enumerate(four):
            line = jnp.where(lane == n, value, line)
        lines.append(line)
    return lines


def strip_kernel(tile_count, direct, scal, nbr, fac, index, rims, *rest):
    n_in = tile_count if direct else 1
    n_out = tile_count - 1 if direct else 1
    blocks, rest = rest[:n_in], rest[n_in:]
    sends, rest = rest[:n_out], rest[n_out:]
    source, strips, comb, stage = rest
    me = scal[0]
    per_src = blocks[0].shape[-2]
    groups = tile_count * per_src
    for s in range(tile_count):
        for c in range(CIN):
            if direct:
                src = me ^ s
                at = c * groups + src * per_src
                if per_src % 8 == 0:
                    at = pl.multiple_of(at, 8)
                stage[pl.ds(at, per_src), :] = blocks[s][c].astype(F32)
            else:
                at = c * groups + s * per_src
                stage[at : at + per_src, :] = blocks[0][s, c].astype(F32)
    source[...] = stage[...].astype(BF16)
    data = source[...]
    flipped = index[...].astype(F32).T
    col = lambda j: flipped[j : j + 1, :].astype(jnp.int32)
    row = lambda i: index[i : i + 1, :]
    pairs = [(row(0), row(1)), (row(126), row(127)), (col(0), col(1)), (col(126), col(127))]
    for n, pair in enumerate(pairs):
        low, high = split_index(jnp.concatenate(pair, axis=1))
        picked = pick_rows(low, high, groups, data)
        for c in range(CIN):
            strips[2 * n, c : c + 1, :] = picked[c][:, :SIDE]
            strips[2 * n + 1, c : c + 1, :] = picked[c][:, SIDE:]
    for n in range(8):
        strips[n, CIN:, :] = jnp.zeros((8 - CIN, SIDE), F32)
    edge = [strips[0], strips[7], reverse(strips[3]), reverse(strips[4])]
    inner = [strips[1], strips[6], reverse(strips[2]), reverse(strips[5])]
    blank = jnp.zeros((COMB - CH - 16, SIDE), F32)
    for k in range(4):
        comb[k, :CH, :] = rims[k]
        comb[k, CH:, :] = jnp.concatenate([edge[k], inner[k], blank], axis=0).astype(BF16)
    if direct:
        pads = []
        for k in range(4):
            mine = comb[jnp.where(nbr[me, k] == me, fac[me, k], 0), CH : CH + 16, :].astype(F32)[:8]
            mine = jnp.where(nbr[me, k] == me, mine, 0.0)
            pads.append(reverse(mine) if k < 2 else mine)
        blank = jnp.zeros((8, SIDE), F32)
        for k, line in enumerate(side_ends(*pads)):
            comb[k, CH + 16 :, :] = jnp.concatenate([line, blank], axis=0).astype(BF16)
    send_strips(tile_count, direct, nbr, me, comb, sends)


def main_pick_kernel(groups, index, source, out):
    data = source[...]

    def chunk(m, carry):
        row = jnp.concatenate([index[pl.ds(2 * m, 1), :], index[pl.ds(2 * m + 1, 1), :]], axis=1)
        low, high = split_index(row)
        picked = pick_rows(low, high, groups, data)
        lanes = pl.ds(pl.multiple_of(m * LOW, LOW), LOW)
        for c in range(CIN):
            out[c : c + 1, lanes] = picked[c]
        return carry

    lax.fori_loop(0, PIX // LOW, chunk, 0, unroll=4)
    out[CIN:, :] = jnp.zeros((8 - CIN, PIX), F32)


def edge_kernel(cot, conv_second, conv_first, rims, columns, fwd_w, back_w, w1, side_w, acc, table):
    step = pl.program_id(0)

    @pl.when(step == 0)
    def _():
        for a in range(3):
            for b in range(3):
                w = conv_second[3 * a + b]
                fwd_w[b * CH : (b + 1) * CH, a * CH : (a + 1) * CH] = w
                back_w[a * CH : (a + 1) * CH, b * CH : (b + 1) * CH] = w.astype(F32).T.astype(BF16)
        table[...] = jnp.zeros_like(table)
        for side in range(4):
            for t in range(3):
                for u in range(3):
                    p = [3 * t + u, 3 * u + 2 - t, 3 * (2 - t) + 2 - u, 3 * (2 - u) + t][side]
                    table[32 * t + 8 * u : 32 * t + 8 * u + CIN, :CH] = conv_first[p].astype(F32)
            side_w[side] = table[...].T[:CH, : 3 * 32].astype(BF16)
        w1[...] = side_w[0]
        acc[...] = jnp.zeros_like(acc)

    half = step // (STEPS // 2)
    got = acc[half]
    pair = iota((CH, SIDE), 1) // 2
    for t in range(ROWS):
        r = step * ROWS + t
        line = cot[:, t * SIDE : (t + 1) * SIDE].astype(F32)
        turned = pltpu.roll(line, lax.rem(2 * r + 1, SIDE), 1)
        got = jnp.where(pair == lax.rem(r, SIDE // 2), turned, got)
    acc[half] = got

    def rim_row(line, a):
        line = line.astype(F32)
        three = jnp.concatenate([from_right(line), line, from_left(line)], axis=0).astype(BF16)
        return dot(back_w[a * CH : (a + 1) * CH, :], three)

    @pl.when(step == 0)
    def _():
        rims[0] = rim_row(cot[:, :SIDE], 0).astype(BF16)

    @pl.when(step == STEPS - 1)
    def _():
        rims[2] = reverse(rim_row(cot[:, (ROWS - 1) * SIDE :], 2)).astype(BF16)
        k = iota((2 * SIDE, 2 * SIDE), 0)
        n = iota((2 * SIDE, 2 * SIDE), 1)
        sort = hot(k, jnp.where(n < SIDE, 2 * n + 1, 2 * (n - SIDE)))
        both = jnp.concatenate([acc[0], acc[1]], axis=1).astype(BF16)
        both = dot(both, sort)
        for e in range(2):
            line = both[:, e * SIDE : (e + 1) * SIDE]
            columns[e] = line.astype(BF16)
            rim = jnp.zeros((CH, SIDE), F32)
            for a, near in enumerate((from_right(line), line, from_left(line))):
                w = back_w[a * CH : (a + 1) * CH, 2 * e * CH : (2 * e + 1) * CH]
                rim = rim + dot(w, near.astype(BF16))
            if e == 0:
                rims[3] = reverse(rim).astype(BF16)
            else:
                rims[1] = rim.astype(BF16)


def shifted(line, first, last):
    lane = iota(line.shape, 1)
    left = jnp.where(lane == 0, first, pltpu.roll(line, 1, 1))
    right = jnp.where(lane == SIDE - 1, last, pltpu.roll(line, SIDE - 1, 1))
    return [left, line, right]


def deliver(got, pads, rims_in):
    north = [reverse(got[0]), reverse(got[1]), got[2].astype(F32), got[3].astype(F32)]
    pad = [x[CH : CH + 8] for x in north]
    rims_in[0] = north[0][:CH]
    rims_in[1] = north[2][:CH]
    cols = dot(north[3][:CH].astype(BF16), ends_table(0, False))
    cols = cols + dot(north[1][:CH].astype(BF16), ends_table(0, True))
    rims_in[2] = cols[:, :SIDE]
    rims_in[3] = cols[:, SIDE:]
    pads[0] = pad[0]
    pads[1] = pad[2]
    cols = dot(pad[3].astype(BF16), ends_table(0, False)) + dot(pad[1].astype(BF16), ends_table(0, True))
    pads[2] = cols[:, :SIDE]
    pads[3] = cols[:, SIDE:]
    return pad


def near_kernel(tile_count, scal, nbr, fac, strips, comb, side_w, *rest):
    n = tile_count - 1
    arrived, (pads, rims_in, incoming, table, ends, lines) = rest[:n], rest[n:]
    me = scal[0]
    got = take_strips(tile_count, True, nbr, fac, me, comb, arrived, table)
    pad = deliver(got, pads, rims_in)
    for k, line in enumerate(side_ends(*pad)):
        ends[k] = line
    lines[...] = jnp.zeros_like(lines)
    zero = jnp.zeros((8, 1), F32)
    for k in range(4):
        other, face = nbr[me, k], fac[me, k]
        there = got[k][CH:].astype(F32)
        end = jnp.where(other == me, ends[face], there[16:24])
        at = lambda i: end[:, i : i + 1]
        outer = reverse(comb[k, CH : CH + 16, :])[:8]
        three = [(outer, zero, zero), (there[:8], at(0), at(1)), (there[8:16], at(2), at(3))]
        for t, line in enumerate(three):
            for u, value in enumerate(shifted(*line)):
                lines[32 * t + 8 * u : 32 * t + 8 * u + 8, :] = value
        pre = dot(side_w[face], lines[...].astype(BF16))
        hid = jnp.where(other < 0, 0.0, pre * jax.nn.sigmoid(pre))
        incoming[k] = (reverse(hid) if k < 2 else hid).astype(BF16)


def border_kernel(tile_count, scal, nbr, fac, strips, comb, w1_ref, arrived, *rest):
    pads, rims_in, own, sends, table, lines = rest
    me = scal[0]
    w1 = w1_ref[...]
    got = take_strips(tile_count, False, nbr, fac, me, comb, [arrived], table)
    pad = deliver(got, pads, rims_in)
    zero = jnp.zeros((8, 1), F32)
    at = lambda x, i: x[:, i : i + 1]
    n0, e0, s0, w0 = pad
    st = [strips[i] for i in range(8)]
    across = [
        (0, [(n0, zero, zero), (st[0], at(w0, 0), at(e0, 0)), (st[1], at(w0, 1), at(e0, 1))]),
        (2, [(st[2], at(w0, 126), at(e0, 126)), (st[3], at(w0, 127), at(e0, 127)), (s0, zero, zero)]),
    ]
    along = [
        (3, [(w0, zero, zero), (st[4], at(n0, 0), at(s0, 0)), (st[5], at(n0, 1), at(s0, 1))]),
        (1, [(st[6], at(n0, 126), at(s0, 126)), (st[7], at(n0, 127), at(s0, 127)), (e0, zero, zero)]),
    ]
    lines[...] = jnp.zeros_like(lines)
    for side, three in across:
        for a, line in enumerate(three):
            for b, value in enumerate(shifted(*line)):
                lines[32 * a + 8 * b : 32 * a + 8 * b + 8, side * SIDE : (side + 1) * SIDE] = value
    for side, three in along:
        for b, line in enumerate(three):
            for a, value in enumerate(shifted(*line)):
                lines[32 * a + 8 * b : 32 * a + 8 * b + 8, side * SIDE : (side + 1) * SIDE] = value
    pre = dot(w1, lines[...].astype(BF16))
    hid = (pre * jax.nn.sigmoid(pre)).astype(BF16)
    side = lambda k: hid[:, k * SIDE : (k + 1) * SIDE]
    own[0] = side(0)
    own[1] = side(1)
    own[2] = reverse(side(2)).astype(BF16)
    own[3] = reverse(side(3)).astype(BF16)
    send_strips(tile_count, False, nbr, me, own, [sends])


def middle_kernel(tiles, pads, rims_in, w1_ref, back_w, cot, prev, nxt, hidden, grad, g1, g2, planes, near, spread, kept):
    step = pl.program_id(0)

    @pl.when(step == 0)
    def _():
        g1[...] = jnp.zeros_like(g1)
        g2[...] = jnp.zeros_like(g2)
        kept[:, : 2 * SIDE] = jnp.zeros((CH, 2 * SIDE), BF16)
        rest = jnp.zeros((8, SIDE), F32)

        def put(row, line, ends):
            three = shifted(line, ends, ends)
            planes[:, row * SIDE : (row + 1) * SIDE] = jnp.concatenate(three + [rest], axis=0).astype(BF16)

        put(0, pads[0], rest)
        put(SIDE + 1, pads[1], rest)
        for i in range(SIDE):
            back = (4 * SIDE - 2 * i - 1) % SIDE
            ends = pltpu.roll(pads[2 + i // (SIDE // 2)], back, 1)
            put(i + 1, tiles[:, i * SIDE : (i + 1) * SIDE], ends)

    w1 = w1_ref[...]
    weights = back_w[...]
    for t in range(ROWS + 2):
        if t == 0:
            line = jnp.where(step > 0, prev[...], jnp.zeros_like(prev))
        elif t == ROWS + 1:
            line = jnp.where(step < STEPS - 1, nxt[...], jnp.zeros_like(nxt))
        else:
            line = cot[:, (t - 1) * SIDE : t * SIDE]
        lanes = slice(t * SIDE, (t + 1) * SIDE)
        wide = line.astype(F32)
        near[:CH, lanes] = from_right(wide).astype(BF16)
        near[CH : 2 * CH, lanes] = line
        near[2 * CH :, lanes] = from_left(wide).astype(BF16)
    for p in range((ROWS + 2) // 2):
        lanes = slice(2 * p * SIDE, (2 * p + 2) * SIDE)
        spread[:, lanes] = dot(weights, near[:, lanes])
    end = is_end((CH, SIDE))
    n_rows = 4
    acc1 = g1[...]
    for p in range(ROWS // n_rows):
        base = step * ROWS + p * n_rows
        cols = []
        for a in range(3):
            lanes = pl.ds(pl.multiple_of((base + a) * SIDE, SIDE), n_rows * SIDE)
            cols.append(planes[:, lanes])
        cols = jnp.concatenate(cols, axis=0)
        pre = dot(w1, cols)
        sigma = jax.nn.sigmoid(pre)
        hid = pre * sigma
        slope = sigma * (1.0 + pre * (1.0 - sigma))
        slopes = []
        for r in range(n_rows):
            t = p * n_rows + r
            here = lambda a: slice((t + 2 - a) * SIDE, (t + 3 - a) * SIDE)
            line = spread[:CH, here(0)] + spread[CH : 2 * CH, here(1)] + spread[2 * CH :, here(2)]
            line = line + jnp.where(end, row_ends(rims_in.at[2:4], base + r), 0.0)
            if t == 0:
                line = line + jnp.where(step == 0, rims_in[0], 0.0)
            if t == ROWS - 1:
                line = line + jnp.where(step == STEPS - 1, rims_in[1], 0.0)
            grad[:, t * SIDE : (t + 1) * SIDE] = line.astype(BF16)
            slopes.append((line * slope[:, r * SIDE : (r + 1) * SIDE]).astype(BF16))
        lanes = slice(p * n_rows * SIDE, (p + 1) * n_rows * SIDE)
        hid = hid.astype(BF16)
        hidden[:, lanes] = hid
        kept[:, (p * n_rows + 2) * SIDE : ((p + 1) * n_rows + 2) * SIDE] = hid
        acc1 = acc1 + dot_nt(cols, jnp.concatenate(slopes, axis=1))
    g1[...] = acc1

    def weigh(first, count):
        three = [kept[:, (first + a) * SIDE : (first + a + count) * SIDE] for a in range(3)]
        return dot_nt(near[:, first * SIDE : (first + count) * SIDE], jnp.concatenate(three, axis=0))

    g2[...] += weigh(0, ROWS)

    @pl.when(step == STEPS - 1)
    def _():
        kept[:, (ROWS + 2) * SIDE :] = jnp.zeros((CH, SIDE), BF16)
        g2[...] += weigh(ROWS, 1)

    kept[:, : 2 * SIDE] = kept[:, ROWS * SIDE : (ROWS + 2) * SIDE]


def close_kernel(tile_count, direct, scale, scal, nbr, fac, columns, top, bottom, g1, g2, fwd_w, *rest):
    if direct:
        incoming, pads, fringe, keep, send, total = rest
        north, east, south, west = [incoming[k] for k in range(4)]
    else:
        own, arrived, pads, fringe, keep, send, total, table = rest
        got = take_strips(tile_count, direct, nbr, fac, scal[0], own, [arrived], table)
        north, east = reverse(got[0]).astype(BF16), reverse(got[1]).astype(BF16)
        south, west = got[2], got[3]
    pads[0] = north
    pads[1] = south
    side = jnp.zeros((CH, 2 * SIDE), F32)
    for e, strip in ((0, west), (1, east)):
        three = [dot(strip, ends_table(a - 1, e == 1)) for a in range(3)]
        three = jnp.concatenate(three, axis=0).astype(BF16)
        side = side + dot(fwd_w[2 * CH * e : 2 * CH * e + CH, :], three)
    fringe[0] = side[:, :SIDE]
    fringe[1] = side[:, SIDE:]
    total[:, : 3 * CH] = g2[...] * scale
    total[:, 3 * CH :] = jnp.zeros((3 * CH, CH), F32)
    total[: 3 * 32, 3 * CH :] = g1[...] * scale

    def three_ways(line, turned):
        line = line.astype(F32)
        ways = [from_right(line), line, from_left(line)]
        return jnp.concatenate(ways[::-1] if turned else ways, axis=0).astype(BF16)

    total[:, :CH] += dot_nt(three_ways(top[...], False), north) * scale
    total[:, 2 * CH : 3 * CH] += dot_nt(three_ways(bottom[...], False), south) * scale
    total[:CH, : 3 * CH] += dot_nt(columns[0], three_ways(west, True)) * scale
    total[2 * CH :, : 3 * CH] += dot_nt(columns[1], three_ways(east, True)) * scale
    core = scal[2]
    half = keep.shape[0]
    if half == 3 * CH:
        keep[...] = total[...]
        send[...] = jnp.zeros_like(send)
    else:
        keep[...] = total[pl.ds(pl.multiple_of(core * half, 8), half), :]
        send[...] = total[pl.ds(pl.multiple_of((1 - core) * half, 8), half), :]


def pair_kernel(scal, kept, got, after, keep, send, total):
    total[...] = kept[...] + got[...]
    half = keep.shape[0]
    here = scal[1]
    keep[...] = total[pl.ds(pl.multiple_of(here * half, 8), half), :]
    send[...] = total[pl.ds(pl.multiple_of((1 - here) * half, 8), half), :]


def ring_kernel(tile_count, scal, mine, *rest):
    got, (after, out, table) = rest[:-3], rest[-3:]
    me = scal[0]
    table[me] = mine[...]
    for s in range(1, tile_count):
        table[me ^ s] = got[s - 1][...]
    total = table[0]
    for t in range(1, tile_count):
        total = total + table[t]
    out[...] = total


def join_kernel(scal, mine, got, after, out):
    half = mine.shape[0]
    here = scal[1]
    out[pl.ds(pl.multiple_of(here * half, 8), half), :] = mine[...]
    out[pl.ds(pl.multiple_of((1 - here) * half, 8), half), :] = got[...]


def unpack(total, first, second):
    for a in range(3):
        for b in range(3):
            second[3 * a + b] = total[b * CH : (b + 1) * CH, a * CH : (a + 1) * CH]
            row = 32 * a + 8 * b
            first[3 * a + b] = total[row : row + CIN, 3 * CH :]


def last_kernel(scal, mine, got, first, second, total):
    half = mine.shape[0]
    here = scal[2]
    total[pl.ds(pl.multiple_of(here * half, 8), half), :] = mine[...]
    total[pl.ds(pl.multiple_of((1 - here) * half, 8), half), :] = got[...]
    unpack(total, first, second)


def output_kernel(start, hid, prev, nxt, pads, fringe, fwd_w, *rest):
    out, token = rest[-2:]
    token[...] = jnp.zeros_like(token)
    step = pl.program_id(0) + start
    weights = fwd_w[...]
    here = hid[...]
    before = jnp.where(step > 0, prev[...], pads[0])
    after = jnp.where(step < STEPS - 1, nxt[...], pads[1])
    up = jnp.concatenate([here[:, SIDE:], after], axis=1)
    down = jnp.concatenate([before, here[:, :-SIDE]], axis=1)
    stacked = jnp.concatenate([down, here, up], axis=0)
    end = is_end((CH, SIDE))
    for p in range(ROWS // 2):
        z = dot(weights, stacked[:, 2 * p * SIDE : (2 * p + 2) * SIDE])
        for r in range(2):
            zr = z[:, r * SIDE : (r + 1) * SIDE]
            line = zr[CH : 2 * CH] + from_left(zr[:CH]) + from_right(zr[2 * CH :])
            line = line + jnp.where(end, row_ends(fringe, step * ROWS + 2 * p + r), 0.0)
            lanes = slice((2 * p + r) * SIDE, (2 * p + r + 1) * SIDE)
            out[:, lanes] = line.astype(BF16)


def shape(dims, kind):
    return jax.ShapeDtypeStruct(dims, kind)


def row_block(offset=0):
    return pl.BlockSpec((CH, ROWS * SIDE), lambda i: (0, i + offset))


def row_before(offset=0):
    return pl.BlockSpec((CH, SIDE), lambda i: (0, jnp.maximum((i + offset) * ROWS - 1, 0)))


def row_after(offset=0):
    return pl.BlockSpec((CH, SIDE), lambda i: (0, jnp.minimum((i + offset + 1) * ROWS, SIDE - 1)))


def cost(flops, moved):
    return pl.CostEstimate(flops=int(flops), bytes_accessed=int(moved), transcendentals=0)


def whole(dims):
    return pl.BlockSpec(dims, lambda i: (0,) * len(dims))


def body(cycle_maps, send_pick, recv_pick, neighbour, facing, conv_first, conv_second, cotangent):
    map_count, _, pixel_count = cycle_maps.shape
    tile_count = lax.axis_size("tile")
    chans = lax.axis_size("chan")
    cores = lax.axis_size("sub")
    direct = tile_count == 4
    assert map_count == 1 and pixel_count == PIX and tile_count != 8
    slots = send_pick.shape[0]
    per_pair = slots // tile_count // LOW
    groups = slots // LOW
    scal = jnp.stack([lax.axis_index(n).astype(jnp.int32) for n in ("tile", "chan", "sub")])
    cyc = cycle_maps.reshape(CIN, PIX)
    cot = cotangent.reshape(CH, PIX)
    n_send = tile_count - 1 if direct else 1

    def exchange(sends):
        if direct:
            return [
                lax.ppermute(x, "tile", [(i, i ^ s) for i in range(tile_count)])
                for s, x in zip(range(1, tile_count), sends)
            ]
        return [lax.all_to_all(sends[0], "tile", 0, 0, tiled=True)]

    def sent(dims, kind):
        if direct:
            return [shape(dims, kind)] * n_send
        return [shape((tile_count,) + dims, kind)]

    if direct:
        block_shapes = [shape((CIN, per_pair, LOW), BF16)] * tile_count
    else:
        block_shapes = [shape((tile_count, CIN, per_pair, LOW), BF16)]
    call = lambda kernel, name, flops, moved, limit, **kw: pl.pallas_call(
        kernel, name=name, cost_estimate=cost(flops, moved), compiler_params=tile_params(limit), **kw
    )
    conv_flops = 2 * 9 * CH * CH * PIX
    blocks = call(
        functools.partial(send_kernel, tile_count, direct),
        "send_pick",
        2 * CIN * PIX * slots,
        12 * PIX,
        8,
        in_specs=[SMEM, VMEM, VMEM],
        out_specs=[VMEM] * len(block_shapes),
        out_shape=block_shapes,
        scratch_shapes=[
            pltpu.VMEM((CIN * PIX // LOW, LOW), F32),
            pltpu.VMEM((CIN * PIX // LOW, LOW), BF16),
            pltpu.VMEM((CIN, groups, LOW), F32),
        ],
    )(scal, cyc, send_pick.reshape(slots // SIDE, SIDE))
    if direct:
        blocks = [blocks[0]] + exchange(blocks[1:])
    else:
        blocks = exchange(blocks)

    square = (3 * CH, 3 * CH)
    rims, columns, fwd_w, back_w, w1, side_w = call(
        edge_kernel,
        "edges",
        conv_flops // 8,
        2 * CH * PIX,
        16,
        grid=(STEPS,),
        in_specs=[row_block(), whole((9, CH, CH)), whole((9, CIN, CH))],
        out_specs=[
            whole((4, CH, SIDE)),
            whole((2, CH, SIDE)),
            whole(square),
            whole(square),
            whole((CH, 96)),
            whole((4, CH, 96)),
        ],
        out_shape=[
            shape((4, CH, SIDE), BF16),
            shape((2, CH, SIDE), BF16),
            shape(square, BF16),
            shape(square, BF16),
            shape((CH, 96), BF16),
            shape((4, CH, 96), BF16),
        ],
        scratch_shapes=[pltpu.VMEM((2, CH, SIDE), F32), pltpu.VMEM((SIDE, SIDE), F32)],
    )(cot, conv_second, jnp.swapaxes(conv_first, 1, 2))

    index = recv_pick.reshape(SIDE, SIDE)
    *sends, source, strips, comb = call(
        functools.partial(strip_kernel, tile_count, direct),
        "strips",
        2 * CIN * groups * LOW * 8 * SIDE,
        10 * PIX,
        8,
        in_specs=[SMEM, SMEM, SMEM] + [VMEM] * (2 + len(blocks)),
        out_specs=[VMEM] * (n_send + 3),
        out_shape=sent((COMB, SIDE), BF16)
        + [shape((CIN * groups, LOW), BF16), shape((8, 8, SIDE), F32), shape((4, COMB, SIDE), BF16)],
        scratch_shapes=[pltpu.VMEM((CIN * groups, LOW), F32)],
    )(scal, neighbour, facing, index, rims, *blocks)
    arrived = exchange(sends)

    tiles = call(
        functools.partial(main_pick_kernel, groups),
        "recv_pick",
        2 * CIN * groups * LOW * PIX,
        2 * 8 * PIX,
        8,
        in_specs=[VMEM] * 2,
        out_specs=VMEM,
        out_shape=shape((8, PIX), F32),
    )(index, source)

    pads_shapes = [shape((4, 8, SIDE), F32), shape((4, CH, SIDE), F32), shape((4, CH, SIDE), BF16)]
    table = pltpu.VMEM((5 + tile_count, COMB, SIDE), BF16)
    if direct:
        pads, rims_in, incoming = call(
            functools.partial(near_kernel, tile_count),
            "near",
            conv_flops // 128,
            PIX,
            8,
            in_specs=[SMEM] * 3 + [VMEM] * (3 + n_send),
            out_specs=[VMEM] * 3,
            out_shape=pads_shapes,
            scratch_shapes=[table, pltpu.VMEM((4, 8, SIDE), F32), pltpu.VMEM((96, SIDE), F32)],
        )(scal, neighbour, facing, strips, comb, side_w, *arrived)
        edges_in = [incoming]
    else:
        pads, rims_in, own, sends = call(
            functools.partial(border_kernel, tile_count),
            "border",
            conv_flops // 128,
            PIX,
            8,
            in_specs=[SMEM] * 3 + [VMEM] * 4,
            out_specs=[VMEM] * 4,
            out_shape=pads_shapes + sent((CH, SIDE), BF16),
            scratch_shapes=[table, pltpu.VMEM((96, 4 * SIDE), F32)],
        )(scal, neighbour, facing, strips, comb, w1, *arrived)
        edges_in = [own] + exchange([sends])

    hidden, grad, g1, g2 = call(
        middle_kernel,
        "middle",
        2 * conv_flops,
        8 * CH * PIX,
        24,
        grid=(STEPS,),
        in_specs=[
            whole((8, PIX)),
            whole((4, 8, SIDE)),
            whole((4, CH, SIDE)),
            whole((CH, 96)),
            whole(square),
            row_block(),
            row_before(),
            row_after(),
        ],
        out_specs=[row_block(), row_block(), whole((96, CH)), whole(square)],
        out_shape=[shape((CH, PIX), BF16), shape((CH, PIX), BF16), shape((96, CH), F32), shape(square, F32)],
        scratch_shapes=[
            pltpu.VMEM((32, (SIDE + 2) * SIDE), BF16),
            pltpu.VMEM((3 * CH, (ROWS + 2) * SIDE), BF16),
            pltpu.VMEM((3 * CH, (ROWS + 2) * SIDE), F32),
            pltpu.VMEM((CH, (ROWS + 3) * SIDE), BF16),
        ],
    )(tiles, pads, rims_in, w1, back_w, cot, cot, cot)

    scale = 1.0 / math.sqrt(map_count * chans * cores * tile_count * PIX)
    fast_sum = direct and chans == 2 and cores == 2
    half = 3 * CH // 2 if fast_sum else 3 * CH
    top = pl.BlockSpec((CH, SIDE), lambda i: (0, 0))
    bottom = pl.BlockSpec((CH, SIDE), lambda i: (0, SIDE - 1))
    pads2, fringe, keep, send = call(
        functools.partial(close_kernel, tile_count, direct, scale),
        "close",
        conv_flops // 128,
        PIX,
        8,
        grid=(1,),
        in_specs=[SMEM, SMEM, SMEM, whole((2, CH, SIDE)), top, bottom]
        + [whole((96, CH)), whole(square), whole(square)]
        + [whole(x.shape) for x in edges_in],
        out_specs=[whole((2, CH, SIDE)), whole((2, CH, SIDE)), whole((half, LOW)), whole((half, LOW))],
        out_shape=[
            shape((2, CH, SIDE), BF16),
            shape((2, CH, SIDE), F32),
            shape((half, LOW), F32),
            shape((half, LOW), F32),
        ],
        scratch_shapes=[pltpu.VMEM((3 * CH, LOW), F32)]
        + ([] if direct else [pltpu.VMEM((5 + tile_count, CH, SIDE), BF16)]),
    )(scal, neighbour, facing, columns, cot, cot, g1, g2, fwd_w, *edges_in)

    anywhere = pl.BlockSpec(memory_space=pl.ANY)

    def convolve(start, count, out, after):
        more = [after] if out is None else [after, out]
        return call(
            functools.partial(output_kernel, start),
            "output",
            conv_flops * count // STEPS,
            4 * CH * PIX * count // STEPS,
            12,
            grid=(count,),
            in_specs=[
                row_block(start),
                row_before(start),
                row_after(start),
                whole((2, CH, SIDE)),
                whole((2, CH, SIDE)),
                whole(square),
            ]
            + [anywhere] * len(more),
            out_specs=[row_block(start), whole((8, SIDE))],
            out_shape=[shape((CH, PIX), BF16), shape((8, SIDE), F32)],
            input_output_aliases={} if out is None else {7: 0},
        )(hidden, hidden, hidden, pads2, fringe, fwd_w, *more)

    finals = [shape((9, CIN, CH), F32), shape((9, CH, CH), F32)]
    if fast_sum:
        swap = lambda x, name: lax.ppermute(x, name, [(0, 1), (1, 0)])
        quarter = half // 2
        small = lambda kernel, name, **kw: call(kernel, name, 1000, half * LOW * 16, 4, **kw)
        got = swap(send, "sub")
        out, token = convolve(0, 1, None, send)
        keep2, send2 = small(
            pair_kernel,
            "pair",
            in_specs=[SMEM, VMEM, VMEM, anywhere],
            out_specs=[VMEM, VMEM],
            out_shape=[shape((quarter, LOW), F32)] * 2,
            scratch_shapes=[pltpu.VMEM((half, LOW), F32)],
        )(scal, keep, got, token)
        got = swap(send2, "chan")
        out, token = convolve(1, 2, out, send2)
        got, _ = lax.optimization_barrier((got, token))
        mine = keep2 + got
        got = exchange([mine] * n_send)
        out, token = convolve(3, 3, out, mine)
        mine = small(
            functools.partial(ring_kernel, tile_count),
            "ring",
            in_specs=[SMEM] + [VMEM] * tile_count + [anywhere],
            out_specs=VMEM,
            out_shape=shape((quarter, LOW), F32),
            scratch_shapes=[pltpu.VMEM((tile_count, quarter, LOW), F32)],
        )(scal, mine, *got, token)
        got = swap(mine, "chan")
        out, token = convolve(6, 2, out, mine)
        mine = small(
            join_kernel,
            "join",
            in_specs=[SMEM, VMEM, VMEM, anywhere],
            out_specs=VMEM,
            out_shape=shape((half, LOW), F32),
        )(scal, mine, got, token)
        got = swap(mine, "sub")
        first, second = small(
            last_kernel,
            "last",
            in_specs=[SMEM, VMEM, VMEM],
            out_specs=[VMEM, VMEM],
            out_shape=finals,
            scratch_shapes=[pltpu.VMEM((3 * CH, LOW), F32)],
        )(scal, mine, got)
    else:
        out, _ = convolve(0, STEPS, None, send)
        total = lax.psum(keep, ("tile", "chan", "sub"))
        first, second = pl.pallas_call(
            unpack, in_specs=[VMEM], out_specs=[VMEM, VMEM], out_shape=finals, name="unpack"
        )(total)
    return (out.reshape(1, CH, PIX), grad.reshape(1, CH, PIX), jnp.swapaxes(first, 1, 2), second)


def solution(mesh):
    in_specs = (
        P(("groups", "chan", "sub"), None, "tile"),
        P("tile"),
        P("tile"),
        P(),
        P(),
        P(),
        P(),
        P(("groups", "chan", "sub"), None, "tile"),
    )
    out_specs = (
        P(("groups", "chan", "sub"), None, "tile"),
        P(("groups", "chan", "sub"), None, "tile"),
        P("groups", None, None),
        P("groups", None, None),
    )
    return jax.shard_map(body, mesh=mesh, in_specs=in_specs, out_specs=out_specs, check_vma=False)
```

time: 94.6 us -> 71.1 us (0.75)
  local copies, waits for them, and re-layouts: 11.3 us -> 1.83 us
  Pallas kernels: 48.2 us -> 42.7 us
  starting transfers between devices: 21.8 us -> 17.9 us
  waiting for transfers between devices: 11 us -> 7.63 us
    unnamed x42 -> x16, local copies, waits for them, and re-layouts: 11.3 us -> 1.83 us
    pallas_call x14 -> x15, Pallas kernels: 48.2 us -> 42.7 us  [the longest x1 11.9 us: body(): call(middle_kernel, 'middle', 2 * conv_flops, 8 * CH * PIX, 24, grid=(STE...]
    ppermute x12 -> x9, starting transfers between devices: 18.8 us -> 14.6 us  [exchange(): lax.ppermute(x, 'tile', [(i, i ^ s) for i in range(tile_count)])]
    ppermute x4, waiting for transfers between devices: 6.92 us -> 4.59 us  [body(): swap = lambda x, name: lax.ppermute(x, name, [(0, 1), (1, 0)])]
    ppermute x12 -> x9, waiting for transfers between devices: 4.07 us -> 3.04 us  [exchange(): lax.ppermute(x, 'tile', [(i, i ^ s) for i in range(tile_count)])]
  transfers between devices with their start and end apart: 16 -> 13, of which waited for: 6 -> 5; matrix products, arithmetic and copies ran while one was open for 0% -> 0% of each run, Pallas kernels for 32% -> 22%
where the time goes in v2:
time: 71.1 us; the launch traced here: 71 us
  Pallas kernels  42.7 us (60%)
  starting transfers between devices  17.9 us (25%)
  waiting for transfers between devices  7.63 us (11%)
  local copies, waits for them, and re-layouts  1.83 us (3%)
  between operations  0.82 us (1%)
    ppermute x9, starting transfers between devices, exchange(): lax.ppermute(x, 'tile', [(i, i ^ s) for i in range(tile_count)])  14.6 us
    pallas_call x1, Pallas kernels, body(): call(middle_kernel, 'middle', 2 * conv_flops, 8 * CH * PIX, 24, grid=(STE...  11.9 us
    pallas_call x1, Pallas kernels, body(): call(functools.partial(send_kernel, tile_count, direct), 'send_pick', 2 *...  8.01 us
    pallas_call x4, Pallas kernels, convolve(): call(functools.partial(output_kernel, start), 'output', conv_flops * coun...  7.77 us
    pallas_call x1, Pallas kernels, body(): call(functools.partial(main_pick_kernel, groups), 'recv_pick', 2 * CIN *...  5.49 us
    ppermute x4, waiting for transfers between devices, body(): swap = lambda x, name: lax.ppermute(x, name, [(0, 1), (1, 0)])  4.59 us
    ppermute x4, starting transfers between devices, body(): swap = lambda x, name: lax.ppermute(x, name, [(0, 1), (1, 0)])  3.27 us
    ppermute x9, waiting for transfers between devices, exchange(): lax.ppermute(x, 'tile', [(i, i ^ s) for i in range(tile_count)])  3.04 us
  transfers between devices with their start and end apart: 13, of which 5 were waited for; matrix products, arithmetic and copies ran while one was open for 0% of the time, Pallas kernels for 22%

profile of v2, /device:TPU:0, one launch (start us, length us, event | category | flops | bytes accessed | tf_op | source)
XLA Modules:
  0.0 71.0 jit_solution(9610242397639240982)
XLA Ops:
  0.7 0.9 %copy-done.5 = bf16[1,3,16384]{2,1,0:T(4,128)(2,1)S(1)} copy-done((bf16[1,3,16384]{2,1,0:T(4,128)(2,1)S(1)}, bf16[1,3,16384]{2,1,0:T(4,128)(2,1)}, u32[]{:S(2)}) %copy-start.5) | copy-done | bytes 98328
  2.5 8.0 %send_pick.1 = (bf16[3,24,256]{2,1,0:T(8,128)(2,1)S(1)}, bf16[3,24,256]{2,1,0:T(8,128)(2,1)S(1)}, bf16[3,24,256]{2,1,0:T(8,128)(2,1)S(1)}, bf16[3,24,256]{2,1,0:T(8,128)(2,1)S(1)}) custom-call(s32[3]{0:T(128)S(1)} %pad_add_fusion.scal, bf16[3,16384]{1,0:T(4,128)(2,1)S(1)} %bitcast.18, s32[192,128]{1,0:T(8,128)S(1)} %bitcast.19), custom_call_target="tpu_custom_call" | custom-call | flops 2415919104 | bytes 196608 | tf_op jit(solution)/shard_map/send_pick/pallas_call | solution.py:647
  10.6 3.1 %collective-permute-start = (bf16[3,24,256]{2,1,0:T(8,128)(2,1)S(1)}, bf16[3,24,256]{2,1,0:T(8,128)(2,1)S(1)}, u32[]{:S(2)}, u32[]{:S(2)}) collective-permute-start(bf16[3,24,256]{2,1,0:T(8,128)(2,1)S(1)} %get-tuple-element.44), channel_id=1, source_target_pairs={{0,4},{4,0},{8,12},{12,8},{1,5},{5,1},{9,13},{13,9},{2,6},{6,2},{1... | collective-permute-start | bytes 110600 | tf_op jit(solution)/shard_map/ppermute | solution.py:629
  13.7 2.6 %collective-permute-start.1 = (bf16[3,24,256]{2,1,0:T(8,128)(2,1)S(1)}, bf16[3,24,256]{2,1,0:T(8,128)(2,1)S(1)}, u32[]{:S(2)}, u32[]{:S(2)}) collective-permute-start(bf16[3,24,256]{2,1,0:T(8,128)(2,1)S(1)} %get-tuple-element.45), channel_id=1, source_target_pairs={{0,8},{4,12},{8,0},{12,4},{1,9},{5,13},{9,1},{13,5},{2,10},{6,14},... | collective-permute-start | bytes 110600 | tf_op jit(solution)/shard_map/ppermute | solution.py:629
  16.3 2.7 %edges.1 = (bf16[4,64,128]{2,1,0:T(8,128)(2,1)S(1)}, bf16[2,64,128]{2,1,0:T(8,128)(2,1)S(1)}, bf16[192,192]{1,0:T(8,128)(2,1)S(1)}, bf16[192,192]{1,0:T(8,128)(2...) custom-call(bf16[64,16384]{1,0:T(8,128)(2,1)S(1)} %bitcast.11, bf16[9,64,64]{2,1,0:T(8,128)(2,1)S(1)} %copy-done.1, ...), custom_call_target="tpu_custom_call" | custom-call | flops 150994944 | bytes 2097152 | tf_op jit(solution)/shard_map/edges/pallas_call | solution.py:668
  19.2 2.8 %collective-permute-done.2.rest_3_ = bf16[3,24,256]{2,1,0:T(8,128)(2,1)S(1)} collective-permute-done((bf16[3,24,256]{2,1,0:T(8,128)(2,1)S(1)}, bf16[3,24,256]{2,1,0:T(8,128)(2,1)S(1)}, u32[]{:S(2)}, u32[]{:S(2)}) %collective-permute-start.2) | collective-permute-done | bytes 36896 | tf_op jit(solution)/shard_map/ppermute | solution.py:629
  22.0 1.3 %strips.1 = (bf16[96,128]{1,0:T(8,128)(2,1)S(1)}, bf16[96,128]{1,0:T(8,128)(2,1)S(1)}, bf16[96,128]{1,0:T(8,128)(2,1)S(1)}, bf16[288,256]{1,0:T(8,128)(2,1)S(1)}...) custom-call(s32[3]{0:T(128)S(1)} %pad_add_fusion.scal, s32[4,4]{1,0:T(4,128)S(1)} %copy-done.3, ...), custom_call_target="tpu_custom_call" | custom-call | flops 150994944 | bytes 163840 | tf_op jit(solution)/shard_map/strips/pallas_call | solution.py:696
  23.4 1.4 %collective-permute-start.4 = (bf16[96,128]{1,0:T(8,128)(2,1)S(1)}, bf16[96,128]{1,0:T(8,128)(2,1)S(1)}, u32[]{:S(2)}, u32[]{:S(2)}) collective-permute-start(bf16[96,128]{1,0:T(8,128)(2,1)S(1)} %get-tuple-element.52), channel_id=1, source_target_pairs={{0,8},{4,12},{8,0},{12,4},{1,9},{5,13},{9,1},{13,5},{2,10},{6,14},... | collective-permute-start | bytes 73736 | tf_op jit(solution)/shard_map/ppermute | solution.py:629
  24.8 3.0 %collective-permute-start.5 = (bf16[96,128]{1,0:T(8,128)(2,1)S(1)}, bf16[96,128]{1,0:T(8,128)(2,1)S(1)}, u32[]{:S(2)}, u32[]{:S(2)}) collective-permute-start(bf16[96,128]{1,0:T(8,128)(2,1)S(1)} %get-tuple-element.53), channel_id=1, source_target_pairs={{0,12},{4,8},{8,4},{12,0},{1,13},{5,9},{9,5},{13,1},{2,14},{6,10},... | collective-permute-start | bytes 73736 | tf_op jit(solution)/shard_map/ppermute | solution.py:629
  27.8 5.5 %recv_pick.1.tiles = f32[8,16384]{1,0:T(8,128)S(1)} custom-call(s32[128,128]{1,0:T(8,128)S(1)} %bitcast.21, bf16[288,256]{1,0:T(8,128)(2,1)S(1)} %get-tuple-element.47.source), custom_call_target="tpu_custom_call" | custom-call | flops 2415919104 | bytes 262144 | tf_op jit(solution)/shard_map/recv_pick/pallas_call | solution.py:710
  33.3 1.5 %near.1 = (f32[4,8,128]{2,1,0:T(8,128)S(1)}, f32[4,64,128]{2,1,0:T(8,128)S(1)}, bf16[4,64,128]{2,1,0:T(8,128)(2,1)S(1)}) custom-call(s32[3]{0:T(128)S(1)} %pad_add_fusion.scal, s32[4,4]{1,0:T(4,128)S(1)} %copy-done.3, s32[4,4]{1,0:T(4,128)S(1)} %copy-done.4, f32[8,8,128]{2,1,0:T(8,128)S(1)} %get-tuple-element.48.strips, ...), custom_call_target="tpu_custom_call" | custom-call | flops 9437184 | bytes 16384 | tf_op jit(solution)/shard_map/near/pallas_call | solution.py:724
  34.8 11.9 %middle.1 = (bf16[64,16384]{1,0:T(8,128)(2,1)S(1)}, bf16[64,16384]{1,0:T(8,128)(2,1)}, f32[96,64]{1,0:T(8,128)S(1)}, f32[192,192]{1,0:T(8,128)S(1)}) custom-call(f32[8,16384]{1,0:T(8,128)S(1)} %recv_pick.1.tiles, f32[4,8,128]{2,1,0:T(8,128)S(1)} %get-tuple-element.54.pads, f32[4,64,128]{2,1,0:T(8,128)S(1)} %get-tuple-element.55.rims_in, ...), custom_call_target="tpu_custom_call" | custom-call | flops 2415919104 | bytes 8388608 | tf_op jit(solution)/shard_map/middle/pallas_call | solution.py:750
  46.7 1.1 %close.1 = (bf16[2,64,128]{2,1,0:T(8,128)(2,1)S(1)}, f32[2,64,128]{2,1,0:T(8,128)S(1)}, f32[96,256]{1,0:T(8,128)S(1)}, f32[96,256]{1,0:T(8,128)S(1)}) custom-call(s32[3]{0:T(128)S(1)} %pad_add_fusion.scal, s32[4,4]{1,0:T(4,128)S(1)} %copy-done.3, s32[4,4]{1,0:T(4,128)S(1)} %copy-done.4, bf16[2,64,128]{2,1,0:T(8,128)(2,1)S(1)} %get-tuple-element.59.columns, ...), custom_call_target="tpu_custom_call" | custom-call | flops 9437184 | bytes 16384 | tf_op jit(solution)/shard_map/close/pallas_call | solution.py:782
  47.9 1.3 %output.4 = (bf16[64,16384]{1,0:T(8,128)(2,1)}, f32[8,128]{1,0:T(8,128)S(1)}) custom-call(bf16[64,16384]{1,0:T(8,128)(2,1)S(1)} %get-tuple-element.58.hid.prev.nxt, bf16[64,16384]{1,0:T(8,128)(2,1)S(1)} %get-tuple-element.58.hid.prev.nxt, bf16[64,16384]{1,0:T(8,128)(2,1)S(1)} %get-tuple-element.58.hid.prev.nxt, ...), custom_call_target="tpu_custom_call" | custom-call | flops 150994944 | bytes 524288 | tf_op jit(solution)/shard_map/output/pallas_call | solution.py:807
  49.7 1.6 %collective-permute-start.7 = (f32[48,256]{1,0:T(8,128)S(1)}, f32[48,256]{1,0:T(8,128)S(1)}, u32[]{:S(2)}, u32[]{:S(2)}) collective-permute-start(f32[48,256]{1,0:T(8,128)S(1)} %get-tuple-element.70.rest_0_), channel_id=1, source_target_pairs={{0,2},{2,0},{1,3},{3,1},{4,6},{6,4},{5,7},{7,5},{8,10},{10,8},{9,1... | collective-permute-start | bytes 147464 | tf_op jit(solution)/shard_map/ppermute | solution.py:830
  51.3 2.6 %collective-permute-done.7 = f32[48,256]{1,0:T(8,128)S(1)} collective-permute-done((f32[48,256]{1,0:T(8,128)S(1)}, f32[48,256]{1,0:T(8,128)S(1)}, u32[]{:S(2)}, u32[]{:S(2)}) %collective-permute-start.7) | collective-permute-done | bytes 49184 | tf_op jit(solution)/shard_map/ppermute | solution.py:830
  53.9 0.9 %collective-permute-start.10 = (f32[48,256]{1,0:T(8,128)S(1)}, f32[48,256]{1,0:T(8,128)S(1)}, u32[]{:S(2)}, u32[]{:S(2)}) collective-permute-start(f32[48,256]{1,0:T(8,128)S(1)} %add.3.rest_0_.mine), channel_id=1, source_target_pairs={{0,12},{4,8},{8,4},{12,0},{1,13},{5,9},{9,5},{13,1},{2,14},{6,10},... | collective-permute-start | bytes 147464 | tf_op jit(solution)/shard_map/ppermute | solution.py:629
  54.8 3.6 %collective-permute-start.8 = (f32[48,256]{1,0:T(8,128)S(1)}, f32[48,256]{1,0:T(8,128)S(1)}, u32[]{:S(2)}, u32[]{:S(2)}) collective-permute-start(f32[48,256]{1,0:T(8,128)S(1)} %add.3.rest_0_.mine), channel_id=1, source_target_pairs={{0,4},{4,0},{8,12},{12,8},{1,5},{5,1},{9,13},{13,9},{2,6},{6,2},{1... | collective-permute-start | bytes 147464 | tf_op jit(solution)/shard_map/ppermute | solution.py:629
  58.4 1.9 %output.5 = (bf16[64,16384]{1,0:T(8,128)(2,1)}, f32[8,128]{1,0:T(8,128)}) custom-call(bf16[64,16384]{1,0:T(8,128)(2,1)S(1)} %get-tuple-element.58.hid.prev.nxt, bf16[64,16384]{1,0:T(8,128)(2,1)S(1)} %get-tuple-element.58.hid.prev.nxt, bf16[64,16384]{1,0:T(8,128)(2,1)S(1)} %get-tuple-element.58.hid.prev.nxt, ...), custom_call_target="tpu_custom_call", output_to_operand_aliasing={{0}: (7, {})} | custom-call | flops 301989888 | bytes 1048576 | tf_op jit(solution)/shard_map/output/pallas_call | solution.py:807
  60.3 2.6 %output.6 = (bf16[64,16384]{1,0:T(8,128)(2,1)}, f32[8,128]{1,0:T(8,128)S(1)}) custom-call(bf16[64,16384]{1,0:T(8,128)(2,1)S(1)} %get-tuple-element.58.hid.prev.nxt, bf16[64,16384]{1,0:T(8,128)(2,1)S(1)} %get-tuple-element.58.hid.prev.nxt, bf16[64,16384]{1,0:T(8,128)(2,1)S(1)} %get-tuple-element.58.hid.prev.nxt, ...), custom_call_target="tpu_custom_call", output_to_operand_aliasing={{0}: (7, {})} | custom-call | flops 452984832 | bytes 1572864 | tf_op jit(solution)/shard_map/output/pallas_call | solution.py:807
  63.5 1.6 %collective-permute-start.11 = (f32[48,256]{1,0:T(8,128)S(1)}, f32[48,256]{1,0:T(8,128)S(1)}, u32[]{:S(2)}, u32[]{:S(2)}) collective-permute-start(f32[48,256]{1,0:T(8,128)S(1)} %ring.1.rest_0_.mine), channel_id=1, source_target_pairs={{0,2},{2,0},{1,3},{3,1},{4,6},{6,4},{5,7},{7,5},{8,10},{10,8},{9,1... | collective-permute-start | bytes 147464 | tf_op jit(solution)/shard_map/ppermute | solution.py:830
  65.1 1.9 %output.7 = (bf16[64,16384]{1,0:T(8,128)(2,1)}, f32[8,128]{1,0:T(8,128)S(1)}) custom-call(bf16[64,16384]{1,0:T(8,128)(2,1)S(1)} %get-tuple-element.58.hid.prev.nxt, bf16[64,16384]{1,0:T(8,128)(2,1)S(1)} %get-tuple-element.58.hid.prev.nxt, bf16[64,16384]{1,0:T(8,128)(2,1)S(1)} %get-tuple-element.58.hid.prev.nxt, ...), custom_call_target="tpu_custom_call", output_to_operand_aliasing={{0}: (7, {})} | custom-call | flops 301989888 | bytes 1048576 | tf_op jit(solution)/shard_map/output/pallas_call | solution.py:807
  68.3 1.3 %collective-permute-done.12.got = f32[96,256]{1,0:T(8,128)S(1)} collective-permute-done((f32[96,256]{1,0:T(8,128)S(1)}, f32[96,256]{1,0:T(8,128)S(1)}, u32[]{:S(2)}, u32[]{:S(2)}) %collective-permute-start.12) | collective-permute-done | bytes 98336 | tf_op jit(solution)/shard_map/ppermute | solution.py:830
  69.6 1.4 %last.1 = (f32[9,3,64]{2,1,0:T(4,128)}, f32[9,64,64]{2,1,0:T(8,128)}) custom-call(s32[3]{0:T(128)S(1)} %pad_add_fusion.scal, f32[96,256]{1,0:T(8,128)S(1)} %join.1.mine, f32[96,256]{1,0:T(8,128)S(1)} %collective-permute-done.12.got), custom_call_target="tpu_custom_call" | custom-call | flops 1000 | bytes 393216 | tf_op jit(solution)/shard_map/last/pallas_call | solution.py:867
  (35 shorter events, 3.8 us)
Async XLA Ops:
  0.7 0.9 %copy-start.5 = (bf16[1,3,16384]{2,1,0:T(4,128)(2,1)S(1)}, bf16[1,3,16384]{2,1,0:T(4,128)(2,1)}, u32[]{:S(2)}) copy-start(bf16[1,3,16384]{2,1,0:T(4,128)(2,1)} %param.8) | copy-start | bytes 294916
  1.6 0.9 %copy-start.6 = (s32[24576]{0:T(1024)S(1)}, s32[24576]{0:T(1024)}, u32[]{:S(2)}) copy-start(s32[24576]{0:T(1024)} %param.9) | copy-start | bytes 294916
  2.5 13.8 %copy-start = (bf16[1,64,16384]{2,1,0:T(8,128)(2,1)S(1)}, bf16[1,64,16384]{2,1,0:T(8,128)(2,1)}, u32[]{:S(2)}) copy-start(bf16[1,64,16384]{2,1,0:T(8,128)(2,1)} %param.15) | copy-start | bytes 6291460
  2.5 13.8 %copy-start.1 = (bf16[9,64,64]{2,1,0:T(8,128)(2,1)S(1)}, bf16[9,64,64]{2,1,0:T(8,128)(2,1)}, u32[]{:S(2)}) copy-start(bf16[9,64,64]{2,1,0:T(8,128)(2,1)} %conv_second.1) | copy-start | bytes 221188
  2.5 13.8 %copy-start.2 = (bf16[9,64,3]{1,2,0:T(4,128)(2,1)S(1)}, bf16[9,64,3]{1,2,0:T(4,128)(2,1)}, u32[]{:S(2)}) copy-start(bf16[9,64,3]{1,2,0:T(4,128)(2,1)} %param.13) | copy-start | bytes 10372
  10.5 11.5 %copy-start.3 = (s32[4,4]{1,0:T(4,128)S(1)}, s32[4,4]{1,0:T(4,128)}, u32[]{:S(2)}) copy-start(s32[4,4]{1,0:T(4,128)} %nbr.5) | copy-start | bytes 196
  10.5 11.5 %copy-start.4 = (s32[4,4]{1,0:T(4,128)S(1)}, s32[4,4]{1,0:T(4,128)}, u32[]{:S(2)}) copy-start(s32[4,4]{1,0:T(4,128)} %fac.5) | copy-start | bytes 196
  10.6 11.5 %copy-start.7 = (s32[16384]{0:T(1024)S(1)}, s32[16384]{0:T(1024)}, u32[]{:S(2)}) copy-start(s32[16384]{0:T(1024)} %param.10) | copy-start | bytes 196612
  10.6 8.4 %collective-permute-start = (bf16[3,24,256]{2,1,0:T(8,128)(2,1)S(1)}, bf16[3,24,256]{2,1,0:T(8,128)(2,1)S(1)}, u32[]{:S(2)}, u32[]{:S(2)}) collective-permute-start(bf16[3,24,256]{2,1,0:T(8,128)(2,1)S(1)} %get-tuple-element.44), channel_id=1, source_target_pairs={{0,4},{4,0},{8,12},{12,8},{1,5},{5,1},{9,13},{13,9},{2,6},{6,2},{1... | collective-permute-start | bytes 110600 | tf_op jit(solution)/shard_map/ppermute | solution.py:629
  13.7 5.5 %collective-permute-start.1 = (bf16[3,24,256]{2,1,0:T(8,128)(2,1)S(1)}, bf16[3,24,256]{2,1,0:T(8,128)(2,1)S(1)}, u32[]{:S(2)}, u32[]{:S(2)}) collective-permute-start(bf16[3,24,256]{2,1,0:T(8,128)(2,1)S(1)} %get-tuple-element.45), channel_id=1, source_target_pairs={{0,8},{4,12},{8,0},{12,4},{1,9},{5,13},{9,1},{13,5},{2,10},{6,14},... | collective-permute-start | bytes 110600 | tf_op jit(solution)/shard_map/ppermute | solution.py:629
  16.3 5.8 %collective-permute-start.2 = (bf16[3,24,256]{2,1,0:T(8,128)(2,1)S(1)}, bf16[3,24,256]{2,1,0:T(8,128)(2,1)S(1)}, u32[]{:S(2)}, u32[]{:S(2)}) collective-permute-start(bf16[3,24,256]{2,1,0:T(8,128)(2,1)S(1)} %get-tuple-element.46), channel_id=1, source_target_pairs={{0,12},{4,8},{8,4},{12,0},{1,13},{5,9},{9,5},{13,1},{2,14},{6,10},... | collective-permute-start | bytes 110600 | tf_op jit(solution)/shard_map/ppermute | solution.py:629
  23.3 10.0 %collective-permute-start.3 = (bf16[96,128]{1,0:T(8,128)(2,1)S(1)}, bf16[96,128]{1,0:T(8,128)(2,1)S(1)}, u32[]{:S(2)}, u32[]{:S(2)}) collective-permute-start(bf16[96,128]{1,0:T(8,128)(2,1)S(1)} %get-tuple-element.51), channel_id=1, source_target_pairs={{0,4},{4,0},{8,12},{12,8},{1,5},{5,1},{9,13},{13,9},{2,6},{6,2},{1... | collective-permute-start | bytes 73736 | tf_op jit(solution)/shard_map/ppermute | solution.py:629
  23.4 9.9 %collective-permute-start.4 = (bf16[96,128]{1,0:T(8,128)(2,1)S(1)}, bf16[96,128]{1,0:T(8,128)(2,1)S(1)}, u32[]{:S(2)}, u32[]{:S(2)}) collective-permute-start(bf16[96,128]{1,0:T(8,128)(2,1)S(1)} %get-tuple-element.52), channel_id=1, source_target_pairs={{0,8},{4,12},{8,0},{12,4},{1,9},{5,13},{9,1},{13,5},{2,10},{6,14},... | collective-permute-start | bytes 73736 | tf_op jit(solution)/shard_map/ppermute | solution.py:629
  24.8 8.5 %collective-permute-start.5 = (bf16[96,128]{1,0:T(8,128)(2,1)S(1)}, bf16[96,128]{1,0:T(8,128)(2,1)S(1)}, u32[]{:S(2)}, u32[]{:S(2)}) collective-permute-start(bf16[96,128]{1,0:T(8,128)(2,1)S(1)} %get-tuple-element.53), channel_id=1, source_target_pairs={{0,12},{4,8},{8,4},{12,0},{1,13},{5,9},{9,5},{13,1},{2,14},{6,10},... | collective-permute-start | bytes 73736 | tf_op jit(solution)/shard_map/ppermute | solution.py:629
  47.8 1.4 %collective-permute-start.6 = (f32[96,256]{1,0:T(8,128)S(1)}, f32[96,256]{1,0:T(8,128)S(1)}, u32[]{:S(2)}, u32[]{:S(2)}) collective-permute-start(f32[96,256]{1,0:T(8,128)S(1)} %get-tuple-element.67.rest_0_), channel_id=1, source_target_pairs={{0,1},{1,0},{2,3},{3,2},{4,5},{5,4},{6,7},{7,6},{8,9},{9,8},{10,11... | collective-permute-start | bytes 294920 | tf_op jit(solution)/shard_map/ppermute | solution.py:830
  49.7 4.2 %collective-permute-start.7 = (f32[48,256]{1,0:T(8,128)S(1)}, f32[48,256]{1,0:T(8,128)S(1)}, u32[]{:S(2)}, u32[]{:S(2)}) collective-permute-start(f32[48,256]{1,0:T(8,128)S(1)} %get-tuple-element.70.rest_0_), channel_id=1, source_target_pairs={{0,2},{2,0},{1,3},{3,1},{4,6},{6,4},{5,7},{7,5},{8,10},{10,8},{9,1... | collective-permute-start | bytes 147464 | tf_op jit(solution)/shard_map/ppermute | solution.py:830
  53.9 9.0 %collective-permute-start.10 = (f32[48,256]{1,0:T(8,128)S(1)}, f32[48,256]{1,0:T(8,128)S(1)}, u32[]{:S(2)}, u32[]{:S(2)}) collective-permute-start(f32[48,256]{1,0:T(8,128)S(1)} %add.3.rest_0_.mine), channel_id=1, source_target_pairs={{0,12},{4,8},{8,4},{12,0},{1,13},{5,9},{9,5},{13,1},{2,14},{6,10},... | collective-permute-start | bytes 147464 | tf_op jit(solution)/shard_map/ppermute | solution.py:629
  54.8 8.1 %collective-permute-start.9 = (f32[48,256]{1,0:T(8,128)S(1)}, f32[48,256]{1,0:T(8,128)S(1)}, u32[]{:S(2)}, u32[]{:S(2)}) collective-permute-start(f32[48,256]{1,0:T(8,128)S(1)} %add.3.rest_0_.mine), channel_id=1, source_target_pairs={{0,8},{4,12},{8,0},{12,4},{1,9},{5,13},{9,1},{13,5},{2,10},{6,14},... | collective-permute-start | bytes 147464 | tf_op jit(solution)/shard_map/ppermute | solution.py:629
  54.8 8.1 %collective-permute-start.8 = (f32[48,256]{1,0:T(8,128)S(1)}, f32[48,256]{1,0:T(8,128)S(1)}, u32[]{:S(2)}, u32[]{:S(2)}) collective-permute-start(f32[48,256]{1,0:T(8,128)S(1)} %add.3.rest_0_.mine), channel_id=1, source_target_pairs={{0,4},{4,0},{8,12},{12,8},{1,5},{5,1},{9,13},{13,9},{2,6},{6,2},{1... | collective-permute-start | bytes 147464 | tf_op jit(solution)/shard_map/ppermute | solution.py:629
  63.5 4.2 %collective-permute-start.11 = (f32[48,256]{1,0:T(8,128)S(1)}, f32[48,256]{1,0:T(8,128)S(1)}, u32[]{:S(2)}, u32[]{:S(2)}) collective-permute-start(f32[48,256]{1,0:T(8,128)S(1)} %ring.1.rest_0_.mine), channel_id=1, source_target_pairs={{0,2},{2,0},{1,3},{3,1},{4,6},{6,4},{5,7},{7,5},{8,10},{10,8},{9,1... | collective-permute-start | bytes 147464 | tf_op jit(solution)/shard_map/ppermute | solution.py:830
  68.2 1.4 %collective-permute-start.12 = (f32[96,256]{1,0:T(8,128)S(1)}, f32[96,256]{1,0:T(8,128)S(1)}, u32[]{:S(2)}, u32[]{:S(2)}) collective-permute-start(f32[96,256]{1,0:T(8,128)S(1)} %join.1.mine), channel_id=1, source_target_pairs={{0,1},{1,0},{2,3},{3,2},{4,5},{5,4},{6,7},{7,6},{8,9},{9,8},{10,11... | collective-permute-start | bytes 294920 | tf_op jit(solution)/shard_map/ppermute | solution.py:830

commit v3 on v2

--- a/solution.py
+++ b/solution.py
@@ -14,7 +14,7 @@
 CIN = 3
 LOW = 256
 COMB = 96
-ROWS = 16
+ROWS = 32
 STEPS = SIDE // ROWS
 F32 = jnp.float32
 BF16 = jnp.bfloat16
@@ -51,6 +51,10 @@
     return jnp.where(iota(x.shape, 1) == SIDE - 1, 0.0, pltpu.roll(x, SIDE - 1, 1))
 
 
+def keep_lane(lane):
+    return jnp.where(iota((CH, SIDE), 1) == lane, 0.0, 1.0).astype(BF16)
+
+
 def ends_table(shift, east):
     src = iota((SIDE, 2 * SIDE), 0)
     lane = iota((SIDE, 2 * SIDE), 1)
@@ -69,7 +73,9 @@
 
 
 def pick_rows(low_rows, high_rows, groups, source):
-    found = dot(source, hot(iota((LOW, LOW), 0), low_rows))
+    low = jnp.broadcast_to(low_rows, (LOW, LOW)).astype(jnp.int16)
+    rows = iota((LOW, LOW), 0).astype(jnp.int16)
+    found = dot(source, jnp.where(low == rows, jnp.bfloat16(1), jnp.bfloat16(0)))
     lines = iota((8, LOW), 0)
     accs = [jnp.zeros((8, LOW), F32)] * CIN
     for g in range(groups // 8):
@@ -114,7 +120,7 @@
             found[c, pl.ds(m, 1), :] = picked[c]
         return carry
 
-    lax.fori_loop(0, tile_count * per_dest, chunk, 0, unroll=4)
+    lax.fori_loop(0, tile_count * per_dest, chunk, 0, unroll=32)
     for d in range(tile_count):
         for c in range(CIN):
             block = found[c, d * per_dest : (d + 1) * per_dest, :].astype(BF16)
@@ -243,7 +249,7 @@
             out[c : c + 1, lanes] = picked[c]
         return carry
 
-    lax.fori_loop(0, PIX // LOW, chunk, 0, unroll=4)
+    lax.fori_loop(0, PIX // LOW, chunk, 0, unroll=32)
     out[CIN:, :] = jnp.zeros((8 - CIN, PIX), F32)
 
 
@@ -255,7 +261,7 @@
         for a in range(3):
             for b in range(3):
                 w = conv_second[3 * a + b]
-                fwd_w[b * CH : (b + 1) * CH, a * CH : (a + 1) * CH] = w
+                fwd_w[a * CH : (a + 1) * CH, b * CH : (b + 1) * CH] = w
                 back_w[a * CH : (a + 1) * CH, b * CH : (b + 1) * CH] = w.astype(F32).T.astype(BF16)
         table[...] = jnp.zeros_like(table)
         for side in range(4):
@@ -314,15 +320,15 @@
     return [left, line, right]
 
 
-def deliver(got, pads, rims_in):
+def deliver(got, pads, rims_in, rims_cols):
     north = [reverse(got[0]), reverse(got[1]), got[2].astype(F32), got[3].astype(F32)]
     pad = [x[CH : CH + 8] for x in north]
     rims_in[0] = north[0][:CH]
     rims_in[1] = north[2][:CH]
     cols = dot(north[3][:CH].astype(BF16), ends_table(0, False))
     cols = cols + dot(north[1][:CH].astype(BF16), ends_table(0, True))
-    rims_in[2] = cols[:, :SIDE]
-    rims_in[3] = cols[:, SIDE:]
+    rims_cols[0] = cols[:, :SIDE].astype(BF16)
+    rims_cols[1] = cols[:, SIDE:].astype(BF16)
     pads[0] = pad[0]
     pads[1] = pad[2]
     cols = dot(pad[3].astype(BF16), ends_table(0, False)) + dot(pad[1].astype(BF16), ends_table(0, True))
@@ -333,10 +339,10 @@
 
 def near_kernel(tile_count, scal, nbr, fac, strips, comb, side_w, *rest):
     n = tile_count - 1
-    arrived, (pads, rims_in, incoming, table, ends, lines) = rest[:n], rest[n:]
+    arrived, (pads, rims_in, rims_cols, incoming, table, ends, lines) = rest[:n], rest[n:]
     me = scal[0]
     got = take_strips(tile_count, True, nbr, fac, me, comb, arrived, table)
-    pad = deliver(got, pads, rims_in)
+    pad = deliver(got, pads, rims_in, rims_cols)
     for k, line in enumerate(side_ends(*pad)):
         ends[k] = line
     lines[...] = jnp.zeros_like(lines)
@@ -357,11 +363,11 @@
 
 
 def border_kernel(tile_count, scal, nbr, fac, strips, comb, w1_ref, arrived, *rest):
-    pads, rims_in, own, sends, table, lines = rest
+    pads, rims_in, rims_cols, own, sends, table, lines = rest
     me = scal[0]
     w1 = w1_ref[...]
     got = take_strips(tile_count, False, nbr, fac, me, comb, [arrived], table)
-    pad = deliver(got, pads, rims_in)
+    pad = deliver(got, pads, rims_in, rims_cols)
     zero = jnp.zeros((8, 1), F32)
     at = lambda x, i: x[:, i : i + 1]
     n0, e0, s0, w0 = pad
@@ -393,7 +399,9 @@
     send_strips(tile_count, False, nbr, me, own, [sends])
 
 
-def middle_kernel(tiles, pads, rims_in, w1_ref, back_w, cot, prev, nxt, hidden, grad, g1, g2, planes, near, spread, kept):
+def middle_kernel(
+    tiles, pads, rims_in, rims_cols, w1_ref, back_w, cot, prev, nxt, hidden, grad, g1, g2, planes, near, kept
+):
     step = pl.program_id(0)
 
     @pl.when(step == 0)
@@ -416,59 +424,65 @@
 
     w1 = w1_ref[...]
     weights = back_w[...]
-    for t in range(ROWS + 2):
-        if t == 0:
-            line = jnp.where(step > 0, prev[...], jnp.zeros_like(prev))
-        elif t == ROWS + 1:
-            line = jnp.where(step < STEPS - 1, nxt[...], jnp.zeros_like(nxt))
-        else:
-            line = cot[:, (t - 1) * SIDE : t * SIDE]
-        lanes = slice(t * SIDE, (t + 1) * SIDE)
-        wide = line.astype(F32)
-        near[:CH, lanes] = from_right(wide).astype(BF16)
-        near[CH : 2 * CH, lanes] = line
-        near[2 * CH :, lanes] = from_left(wide).astype(BF16)
-    for p in range((ROWS + 2) // 2):
-        lanes = slice(2 * p * SIDE, (2 * p + 2) * SIDE)
-        spread[:, lanes] = dot(weights, near[:, lanes])
+    no_first, no_last = keep_lane(0), keep_lane(SIDE - 1)
     end = is_end((CH, SIDE))
-    n_rows = 4
-    acc1 = g1[...]
-    for p in range(ROWS // n_rows):
-        base = step * ROWS + p * n_rows
-        cols = []
-        for a in range(3):
-            lanes = pl.ds(pl.multiple_of((base + a) * SIDE, SIDE), n_rows * SIDE)
-            cols.append(planes[:, lanes])
-        cols = jnp.concatenate(cols, axis=0)
-        pre = dot(w1, cols)
-        sigma = jax.nn.sigmoid(pre)
-        hid = pre * sigma
-        slope = sigma * (1.0 + pre * (1.0 - sigma))
-        slopes = []
-        for r in range(n_rows):
-            t = p * n_rows + r
-            here = lambda a: slice((t + 2 - a) * SIDE, (t + 3 - a) * SIDE)
-            line = spread[:CH, here(0)] + spread[CH : 2 * CH, here(1)] + spread[2 * CH :, here(2)]
-            line = line + jnp.where(end, row_ends(rims_in.at[2:4], base + r), 0.0)
-            if t == 0:
-                line = line + jnp.where(step == 0, rims_in[0], 0.0)
-            if t == ROWS - 1:
-                line = line + jnp.where(step == STEPS - 1, rims_in[1], 0.0)
-            grad[:, t * SIDE : (t + 1) * SIDE] = line.astype(BF16)
-            slopes.append((line * slope[:, r * SIDE : (r + 1) * SIDE]).astype(BF16))
-        lanes = slice(p * n_rows * SIDE, (p + 1) * n_rows * SIDE)
-        hid = hid.astype(BF16)
-        hidden[:, lanes] = hid
-        kept[:, (p * n_rows + 2) * SIDE : ((p + 1) * n_rows + 2) * SIDE] = hid
-        acc1 = acc1 + dot_nt(cols, jnp.concatenate(slopes, axis=1))
-    g1[...] = acc1
 
     def weigh(first, count):
         three = [kept[:, (first + a) * SIDE : (first + a + count) * SIDE] for a in range(3)]
         return dot_nt(near[:, first * SIDE : (first + count) * SIDE], jnp.concatenate(three, axis=0))
 
-    g2[...] += weigh(0, ROWS)
+    open_sum = open_last = None
+    slopes = []
+    for p in range(ROWS // 2 + 1):
+        for t in (2 * p, 2 * p + 1):
+            if t == 0:
+                line = jnp.where(step > 0, prev[...], jnp.zeros_like(prev))
+            elif t == ROWS + 1:
+                line = jnp.where(step < STEPS - 1, nxt[...], jnp.zeros_like(nxt))
+            else:
+                line = cot[:, (t - 1) * SIDE : t * SIDE]
+            lanes = slice(t * SIDE, (t + 1) * SIDE)
+            near[:CH, lanes] = pltpu.roll(line, SIDE - 1, 1) * no_last
+            near[CH : 2 * CH, lanes] = line
+            near[2 * CH :, lanes] = pltpu.roll(line, 1, 1) * no_first
+        z = dot(weights, near[:, 2 * p * SIDE : (2 * p + 2) * SIDE])
+        part = lambda a, r: z[a * CH : (a + 1) * CH, r * SIDE : (r + 1) * SIDE]
+        if p > 0:
+            pair = [open_sum + part(0, 0), part(0, 1) + part(1, 0) + open_last]
+            base = step * ROWS + 2 * p - 2
+            cols = []
+            for a in range(3):
+                lanes = pl.ds(pl.multiple_of((base + a) * SIDE, SIDE), 2 * SIDE)
+                cols.append(planes[:, lanes])
+            pre = dot(w1, jnp.concatenate(cols, axis=0))
+            sigma = jax.nn.sigmoid(pre)
+            hid = pre * sigma
+            slope = sigma + hid * (1.0 - sigma)
+            for r in range(2):
+                t = 2 * p - 2 + r
+                line = pair[r]
+                line = line + jnp.where(end, row_ends(rims_cols, base + r).astype(F32), 0.0)
+                if t == 0:
+                    line = line + jnp.where(step == 0, rims_in[0], 0.0)
+                if t == ROWS - 1:
+                    line = line + jnp.where(step == STEPS - 1, rims_in[1], 0.0)
+                grad[:, t * SIDE : (t + 1) * SIDE] = line.astype(BF16)
+                slopes.append((line * slope[:, r * SIDE : (r + 1) * SIDE]).astype(BF16))
+            hid = hid.astype(BF16)
+            hidden[:, (2 * p - 2) * SIDE : 2 * p * SIDE] = hid
+            kept[:, 2 * p * SIDE : (2 * p + 2) * SIDE] = hid
+        open_sum = part(1, 1) + part(2, 0)
+        open_last = part(2, 1)
+        if p > 0 and p % 4 == 0:
+            count = len(slopes)
+            cols = []
+            for a in range(3):
+                lanes = pl.ds(pl.multiple_of((step * ROWS + 2 * p - count + a) * SIDE, SIDE), count * SIDE)
+                cols.append(planes[:, lanes])
+            g1[...] += dot_nt(jnp.concatenate(cols, axis=0), jnp.concatenate(slopes, axis=1))
+            slopes = []
+        if p > 0 and p % 8 == 0:
+            g2[...] += weigh(2 * p - 16, 16)
 
     @pl.when(step == STEPS - 1)
     def _():
@@ -478,24 +492,20 @@
     kept[:, : 2 * SIDE] = kept[:, ROWS * SIDE : (ROWS + 2) * SIDE]
 
 
-def close_kernel(tile_count, direct, scale, scal, nbr, fac, columns, top, bottom, g1, g2, fwd_w, *rest):
+def close_kernel(tile_count, direct, scale, scal, nbr, fac, columns, top, bottom, g1, g2, *rest):
     if direct:
-        incoming, pads, fringe, keep, send, total = rest
+        incoming, pads, keep, send, total = rest
         north, east, south, west = [incoming[k] for k in range(4)]
     else:
-        own, arrived, pads, fringe, keep, send, total, table = rest
+        own, arrived, pads, keep, send, total, table = rest
         got = take_strips(tile_count, direct, nbr, fac, scal[0], own, [arrived], table)
         north, east = reverse(got[0]).astype(BF16), reverse(got[1]).astype(BF16)
         south, west = got[2], got[3]
     pads[0] = north
     pads[1] = south
-    side = jnp.zeros((CH, 2 * SIDE), F32)
-    for e, strip in ((0, west), (1, east)):
-        three = [dot(strip, ends_table(a - 1, e == 1)) for a in range(3)]
-        three = jnp.concatenate(three, axis=0).astype(BF16)
-        side = side + dot(fwd_w[2 * CH * e : 2 * CH * e + CH, :], three)
-    fringe[0] = side[:, :SIDE]
-    fringe[1] = side[:, SIDE:]
+    side = dot(west, ends_table(0, False)) + dot(east, ends_table(0, True))
+    pads[2] = side[:, :SIDE].astype(BF16)
+    pads[3] = side[:, SIDE:].astype(BF16)
     total[:, : 3 * CH] = g2[...] * scale
     total[:, 3 * CH :] = jnp.zeros((3 * CH, CH), F32)
     total[: 3 * 32, 3 * CH :] = g1[...] * scale
@@ -527,6 +537,10 @@
     send[...] = total[pl.ds(pl.multiple_of((1 - here) * half, 8), half), :]
 
 
+def add_kernel(mine, got, after, out):
+    out[...] = mine[...] + got[...]
+
+
 def ring_kernel(tile_count, scal, mine, *rest):
     got, (after, out, table) = rest[:-3], rest[-3:]
     me = scal[0]
@@ -562,26 +576,42 @@
     unpack(total, first, second)
 
 
-def output_kernel(start, hid, prev, nxt, pads, fringe, fwd_w, *rest):
-    out, token = rest[-2:]
+def output_kernel(start, hid, prev, nxt, pads, fwd_w, *rest):
+    out, token, near = rest[-3:]
     token[...] = jnp.zeros_like(token)
     step = pl.program_id(0) + start
     weights = fwd_w[...]
-    here = hid[...]
-    before = jnp.where(step > 0, prev[...], pads[0])
-    after = jnp.where(step < STEPS - 1, nxt[...], pads[1])
-    up = jnp.concatenate([here[:, SIDE:], after], axis=1)
-    down = jnp.concatenate([before, here[:, :-SIDE]], axis=1)
-    stacked = jnp.concatenate([down, here, up], axis=0)
-    end = is_end((CH, SIDE))
-    for p in range(ROWS // 2):
-        z = dot(weights, stacked[:, 2 * p * SIDE : (2 * p + 2) * SIDE])
-        for r in range(2):
-            zr = z[:, r * SIDE : (r + 1) * SIDE]
-            line = zr[CH : 2 * CH] + from_left(zr[:CH]) + from_right(zr[2 * CH :])
-            line = line + jnp.where(end, row_ends(fringe, step * ROWS + 2 * p + r), 0.0)
-            lanes = slice((2 * p + r) * SIDE, (2 * p + r + 1) * SIDE)
-            out[:, lanes] = line.astype(BF16)
+    lane = iota((CH, SIDE), 1)
+    first, last = lane == 0, lane == SIDE - 1
+    none = jnp.zeros((CH, SIDE), BF16)
+    open_sum = open_first = None
+    for p in range(ROWS // 2 + 1):
+        for t in (2 * p, 2 * p + 1):
+            row = step * ROWS + t - 1
+            if t == 0:
+                line = jnp.where(step > 0, prev[...], pads[0])
+                ends = row_ends(pads.at[2:4], jnp.maximum(row, 0))
+                ends = jnp.where(step > 0, ends, none)
+            elif t == ROWS + 1:
+                line = jnp.where(step < STEPS - 1, nxt[...], pads[1])
+                ends = row_ends(pads.at[2:4], jnp.minimum(row, SIDE - 1))
+                ends = jnp.where(step < STEPS - 1, ends, none)
+            else:
+                line = hid[:, (t - 1) * SIDE : t * SIDE]
+                ends = row_ends(pads.at[2:4], row)
+            lanes = slice(t * SIDE, (t + 1) * SIDE)
+            near[:CH, lanes] = jnp.where(first, ends, pltpu.roll(line, 1, 1))
+            near[CH : 2 * CH, lanes] = line
+            near[2 * CH :, lanes] = jnp.where(last, ends, pltpu.roll(line, SIDE - 1, 1))
+        z = dot(weights, near[:, 2 * p * SIDE : (2 * p + 2) * SIDE])
+        part = lambda a, r: z[a * CH : (a + 1) * CH, r * SIDE : (r + 1) * SIDE]
+        if p > 0:
+            lanes = slice((2 * p - 2) * SIDE, (2 * p - 1) * SIDE)
+            out[:, lanes] = (open_sum + part(2, 0)).astype(BF16)
+            lanes = slice((2 * p - 1) * SIDE, 2 * p * SIDE)
+            out[:, lanes] = (open_first + part(1, 0) + part(2, 1)).astype(BF16)
+        open_sum = part(0, 0) + part(1, 1)
+        open_first = part(0, 1)
 
 
 def shape(dims, kind):
@@ -718,30 +748,35 @@
         out_shape=shape((8, PIX), F32),
     )(index, source)
 
-    pads_shapes = [shape((4, 8, SIDE), F32), shape((4, CH, SIDE), F32), shape((4, CH, SIDE), BF16)]
+    pads_shapes = [
+        shape((4, 8, SIDE), F32),
+        shape((2, CH, SIDE), F32),
+        shape((2, CH, SIDE), BF16),
+        shape((4, CH, SIDE), BF16),
+    ]
     table = pltpu.VMEM((5 + tile_count, COMB, SIDE), BF16)
     if direct:
-        pads, rims_in, incoming = call(
+        pads, rims_in, rims_cols, incoming = call(
             functools.partial(near_kernel, tile_count),
             "near",
             conv_flops // 128,
             PIX,
             8,
             in_specs=[SMEM] * 3 + [VMEM] * (3 + n_send),
-            out_specs=[VMEM] * 3,
+            out_specs=[VMEM] * 4,
             out_shape=pads_shapes,
             scratch_shapes=[table, pltpu.VMEM((4, 8, SIDE), F32), pltpu.VMEM((96, SIDE), F32)],
         )(scal, neighbour, facing, strips, comb, side_w, *arrived)
         edges_in = [incoming]
     else:
-        pads, rims_in, own, sends = call(
+        pads, rims_in, rims_cols, own, sends = call(
             functools.partial(border_kernel, tile_count),
             "border",
             conv_flops // 128,
             PIX,
             8,
             in_specs=[SMEM] * 3 + [VMEM] * 4,
-            out_specs=[VMEM] * 4,
+            out_specs=[VMEM] * 5,
             out_shape=pads_shapes + sent((CH, SIDE), BF16),
             scratch_shapes=[table, pltpu.VMEM((96, 4 * SIDE), F32)],
         )(scal, neighbour, facing, strips, comb, w1, *arrived)
@@ -757,7 +792,8 @@
         in_specs=[
             whole((8, PIX)),
             whole((4, 8, SIDE)),
-            whole((4, CH, SIDE)),
+            whole((2, CH, SIDE)),
+            whole((2, CH, SIDE)),
             whole((CH, 96)),
             whole(square),
             row_block(),
@@ -769,17 +805,16 @@
         scratch_shapes=[
             pltpu.VMEM((32, (SIDE + 2) * SIDE), BF16),
             pltpu.VMEM((3 * CH, (ROWS + 2) * SIDE), BF16),
-            pltpu.VMEM((3 * CH, (ROWS + 2) * SIDE), F32),
             pltpu.VMEM((CH, (ROWS + 3) * SIDE), BF16),
         ],
-    )(tiles, pads, rims_in, w1, back_w, cot, cot, cot)
+    )(tiles, pads, rims_in, rims_cols, w1, back_w, cot, cot, cot)
 
     scale = 1.0 / math.sqrt(map_count * chans * cores * tile_count * PIX)
     fast_sum = direct and chans == 2 and cores == 2
     half = 3 * CH // 2 if fast_sum else 3 * CH
     top = pl.BlockSpec((CH, SIDE), lambda i: (0, 0))
     bottom = pl.BlockSpec((CH, SIDE), lambda i: (0, SIDE - 1))
-    pads2, fringe, keep, send = call(
+    pads2, keep, send = call(
         functools.partial(close_kernel, tile_count, direct, scale),
         "close",
         conv_flops // 128,
@@ -787,18 +822,17 @@
         8,
         grid=(1,),
         in_specs=[SMEM, SMEM, SMEM, whole((2, CH, SIDE)), top, bottom]
-        + [whole((96, CH)), whole(square), whole(square)]
+        + [whole((96, CH)), whole(square)]
         + [whole(x.shape) for x in edges_in],
-        out_specs=[whole((2, CH, SIDE)), whole((2, CH, SIDE)), whole((half, LOW)), whole((half, LOW))],
+        out_specs=[whole((4, CH, SIDE)), whole((half, LOW)), whole((half, LOW))],
         out_shape=[
-            shape((2, CH, SIDE), BF16),
-            shape((2, CH, SIDE), F32),
+            shape((4, CH, SIDE), BF16),
             shape((half, LOW), F32),
             shape((half, LOW), F32),
         ],
         scratch_shapes=[pltpu.VMEM((3 * CH, LOW), F32)]
         + ([] if direct else [pltpu.VMEM((5 + tile_count, CH, SIDE), BF16)]),
-    )(scal, neighbour, facing, columns, cot, cot, g1, g2, fwd_w, *edges_in)
+    )(scal, neighbour, facing, columns, cot, cot, g1, g2, *edges_in)
 
     anywhere = pl.BlockSpec(memory_space=pl.ANY)
 
@@ -811,19 +845,13 @@
             4 * CH * PIX * count // STEPS,
             12,
             grid=(count,),
-            in_specs=[
-                row_block(start),
-                row_before(start),
-                row_after(start),
-                whole((2, CH, SIDE)),
-                whole((2, CH, SIDE)),
-                whole(square),
-            ]
+            in_specs=[row_block(start), row_before(start), row_after(start), whole((4, CH, SIDE)), whole(square)]
             + [anywhere] * len(more),
             out_specs=[row_block(start), whole((8, SIDE))],
             out_shape=[shape((CH, PIX), BF16), shape((8, SIDE), F32)],
-            input_output_aliases={} if out is None else {7: 0},
-        )(hidden, hidden, hidden, pads2, fringe, fwd_w, *more)
+            input_output_aliases={} if out is None else {6: 0},
+            scratch_shapes=[pltpu.VMEM((3 * CH, (ROWS + 2) * SIDE), BF16)],
+        )(hidden, hidden, hidden, pads2, fwd_w, *more)
 
     finals = [shape((9, CIN, CH), F32), shape((9, CH, CH), F32)]
     if fast_sum:
@@ -841,11 +869,16 @@
             scratch_shapes=[pltpu.VMEM((half, LOW), F32)],
         )(scal, keep, got, token)
         got = swap(send2, "chan")
-        out, token = convolve(1, 2, out, send2)
-        got, _ = lax.optimization_barrier((got, token))
-        mine = keep2 + got
+        out, token = convolve(1, 1, out, send2)
+        mine = small(
+            add_kernel,
+            "add",
+            in_specs=[VMEM, VMEM, anywhere],
+            out_specs=VMEM,
+            out_shape=shape((quarter, LOW), F32),
+        )(keep2, got, token)
         got = exchange([mine] * n_send)
-        out, token = convolve(3, 3, out, mine)
+        out, token = convolve(2, 1, out, mine)
         mine = small(
             functools.partial(ring_kernel, tile_count),
             "ring",
@@ -855,7 +888,7 @@
             scratch_shapes=[pltpu.VMEM((tile_count, quarter, LOW), F32)],
         )(scal, mine, *got, token)
         got = swap(mine, "chan")
-        out, token = convolve(6, 2, out, mine)
+        out, token = convolve(3, 1, out, mine)
         mine = small(
             join_kernel,
             "join",

time: 71.1 us -> 62.5 us (0.88)
  Pallas kernels: 42.7 us -> 33.4 us
    pallas_call x1, Pallas kernels: 8.01 us -> 3.96 us  [body(): call(functools.partial(send_kernel, tile_count, direct), 'send_pick', 2 *...]
    pallas_call x1, Pallas kernels: 5.49 us -> 3.04 us  [body(): call(functools.partial(main_pick_kernel, groups), 'recv_pick', 2 * CIN *...]
    ppermute x9, waiting for transfers between devices: 3.04 us -> 5.06 us  [exchange(): lax.ppermute(x, 'tile', [(i, i ^ s) for i in range(tile_count)])]
    ppermute x4, waiting for transfers between devices: 4.59 us -> 3.23 us  [body(): swap = lambda x, name: lax.ppermute(x, name, [(0, 1), (1, 0)])]
    pallas_call x4, Pallas kernels: 7.77 us -> 6.6 us  [convolve(): call(functools.partial(output_kernel, start), 'output', conv_flops * coun...]
    pallas_call x1, Pallas kernels: 11.9 us -> 10.9 us  [body(): call(middle_kernel, 'middle', 2 * conv_flops, 8 * CH * PIX, 24, grid=(STE...]
  transfers between devices with their start and end apart: 13 -> 13, of which waited for: 5 -> 6; matrix products, arithmetic and copies ran while one was open for 0% -> 0% of each run, Pallas kernels for 22% -> 19%
where the time goes in v3:
time: 62.5 us; the launch traced here: 62.3 us
  Pallas kernels  33.4 us (53%)
  starting transfers between devices  17.9 us (29%)
  waiting for transfers between devices  8.28 us (13%)
  local copies, waits for them, and re-layouts  1.83 us (3%)
  between operations  0.82 us (1%)
    ppermute x9, starting transfers between devices, exchange(): lax.ppermute(x, 'tile', [(i, i ^ s) for i in range(tile_count)])  14.6 us
    pallas_call x1, Pallas kernels, body(): call(middle_kernel, 'middle', 2 * conv_flops, 8 * CH * PIX, 24, grid=(STE...  10.9 us
    pallas_call x4, Pallas kernels, convolve(): call(functools.partial(output_kernel, start), 'output', conv_flops * coun...  6.6 us
    ppermute x9, waiting for transfers between devices, exchange(): lax.ppermute(x, 'tile', [(i, i ^ s) for i in range(tile_count)])  5.06 us
    pallas_call x1, Pallas kernels, body(): call(functools.partial(send_kernel, tile_count, direct), 'send_pick', 2 *...  3.96 us
    ppermute x4, starting transfers between devices, body(): swap = lambda x, name: lax.ppermute(x, name, [(0, 1), (1, 0)])  3.27 us
    ppermute x4, waiting for transfers between devices, body(): swap = lambda x, name: lax.ppermute(x, name, [(0, 1), (1, 0)])  3.23 us
    pallas_call x1, Pallas kernels, body(): call(functools.partial(main_pick_kernel, groups), 'recv_pick', 2 * CIN *...  3.04 us
  transfers between devices with their start and end apart: 13, of which 6 were waited for; matrix products, arithmetic and copies ran while one was open for 0% of the time, Pallas kernels for 19%

profile of v3, /device:TPU:0, one launch (start us, length us, event | category | flops | bytes accessed | tf_op | source)
XLA Modules:
  0.0 62.3 jit_solution(3210946812741208093)
XLA Ops:
  2.5 4.0 %send_pick.1 = (bf16[3,24,256]{2,1,0:T(8,128)(2,1)S(1)}, bf16[3,24,256]{2,1,0:T(8,128)(2,1)S(1)}, bf16[3,24,256]{2,1,0:T(8,128)(2,1)S(1)}, bf16[3,24,256]{2,1,0:T(8,128)(2,1)S(1)}) custom-call(s32[3]{0:T(128)S(1)} %pad_add_fusion.scal, bf16[3,16384]{1,0:T(4,128)(2,1)S(1)} %bitcast.18, s32[192,128]{1,0:T(8,128)S(1)} %bitcast.19), custom_call_target="tpu_custom_call" | custom-call | flops 2415919104 | bytes 196608 | tf_op jit(solution)/shard_map/send_pick/pallas_call | solution.py:677
  6.5 3.1 %collective-permute-start = (bf16[3,24,256]{2,1,0:T(8,128)(2,1)S(1)}, bf16[3,24,256]{2,1,0:T(8,128)(2,1)S(1)}, u32[]{:S(2)}, u32[]{:S(2)}) collective-permute-start(bf16[3,24,256]{2,1,0:T(8,128)(2,1)S(1)} %get-tuple-element.45), channel_id=1, source_target_pairs={{0,4},{4,0},{8,12},{12,8},{1,5},{5,1},{9,13},{13,9},{2,6},{6,2},{1... | collective-permute-start | bytes 110600 | tf_op jit(solution)/shard_map/ppermute | solution.py:659
  9.6 2.6 %collective-permute-start.1 = (bf16[3,24,256]{2,1,0:T(8,128)(2,1)S(1)}, bf16[3,24,256]{2,1,0:T(8,128)(2,1)S(1)}, u32[]{:S(2)}, u32[]{:S(2)}) collective-permute-start(bf16[3,24,256]{2,1,0:T(8,128)(2,1)S(1)} %get-tuple-element.46), channel_id=1, source_target_pairs={{0,8},{4,12},{8,0},{12,4},{1,9},{5,13},{9,1},{13,5},{2,10},{6,14},... | collective-permute-start | bytes 110600 | tf_op jit(solution)/shard_map/ppermute | solution.py:659
  12.3 2.2 %edges.1 = (bf16[4,64,128]{2,1,0:T(8,128)(2,1)S(1)}, bf16[2,64,128]{2,1,0:T(8,128)(2,1)S(1)}, bf16[192,192]{1,0:T(8,128)(2,1)S(1)}, bf16[192,192]{1,0:T(8,128)(2...) custom-call(bf16[64,16384]{1,0:T(8,128)(2,1)S(1)} %bitcast.11, bf16[9,64,64]{2,1,0:T(8,128)(2,1)S(1)} %copy-done.1, ...), custom_call_target="tpu_custom_call" | custom-call | flops 150994944 | bytes 2097152 | tf_op jit(solution)/shard_map/edges/pallas_call | solution.py:698
  15.2 2.8 %collective-permute-done.2.rest_3_ = bf16[3,24,256]{2,1,0:T(8,128)(2,1)S(1)} collective-permute-done((bf16[3,24,256]{2,1,0:T(8,128)(2,1)S(1)}, bf16[3,24,256]{2,1,0:T(8,128)(2,1)S(1)}, u32[]{:S(2)}, u32[]{:S(2)}) %collective-permute-start.2) | collective-permute-done | bytes 36896 | tf_op jit(solution)/shard_map/ppermute | solution.py:659
  18.0 1.3 %strips.1 = (bf16[96,128]{1,0:T(8,128)(2,1)S(1)}, bf16[96,128]{1,0:T(8,128)(2,1)S(1)}, bf16[96,128]{1,0:T(8,128)(2,1)S(1)}, bf16[288,256]{1,0:T(8,128)(2,1)S(1)}...) custom-call(s32[3]{0:T(128)S(1)} %pad_add_fusion.scal, s32[4,4]{1,0:T(4,128)S(1)} %copy-done.3, ...), custom_call_target="tpu_custom_call" | custom-call | flops 150994944 | bytes 163840 | tf_op jit(solution)/shard_map/strips/pallas_call | solution.py:726
  19.3 1.0 %collective-permute-start.4 = (bf16[96,128]{1,0:T(8,128)(2,1)S(1)}, bf16[96,128]{1,0:T(8,128)(2,1)S(1)}, u32[]{:S(2)}, u32[]{:S(2)}) collective-permute-start(bf16[96,128]{1,0:T(8,128)(2,1)S(1)} %get-tuple-element.53), channel_id=1, source_target_pairs={{0,8},{4,12},{8,0},{12,4},{1,9},{5,13},{9,1},{13,5},{2,10},{6,14},... | collective-permute-start | bytes 73736 | tf_op jit(solution)/shard_map/ppermute | solution.py:659
  20.4 3.3 %collective-permute-start.5 = (bf16[96,128]{1,0:T(8,128)(2,1)S(1)}, bf16[96,128]{1,0:T(8,128)(2,1)S(1)}, u32[]{:S(2)}, u32[]{:S(2)}) collective-permute-start(bf16[96,128]{1,0:T(8,128)(2,1)S(1)} %get-tuple-element.54), channel_id=1, source_target_pairs={{0,12},{4,8},{8,4},{12,0},{1,13},{5,9},{9,5},{13,1},{2,14},{6,10},... | collective-permute-start | bytes 73736 | tf_op jit(solution)/shard_map/ppermute | solution.py:659
  23.7 3.0 %recv_pick.1.tiles = f32[8,16384]{1,0:T(8,128)S(1)} custom-call(s32[128,128]{1,0:T(8,128)S(1)} %bitcast.21, bf16[288,256]{1,0:T(8,128)(2,1)S(1)} %get-tuple-element.48.source), custom_call_target="tpu_custom_call" | custom-call | flops 2415919104 | bytes 262144 | tf_op jit(solution)/shard_map/recv_pick/pallas_call | solution.py:740
  26.8 1.5 %near.1 = (f32[4,8,128]{2,1,0:T(8,128)S(1)}, f32[2,64,128]{2,1,0:T(8,128)S(1)}, bf16[2,64,128]{2,1,0:T(8,128)(2,1)S(1)}, bf16[4,64,128]{2,1,0:T(8,128)(2,1)S(1)}) custom-call(s32[3]{0:T(128)S(1)} %pad_add_fusion.scal, s32[4,4]{1,0:T(4,128)S(1)} %copy-done.3, s32[4,4]{1,0:T(4,128)S(1)} %copy-done.4, f32[8,8,128]{2,1,0:T(8,128)S(1)} %get-tuple-element.49.strips, ...), custom_call_target="tpu_custom_call" | custom-call | flops 9437184 | bytes 16384 | tf_op jit(solution)/shard_map/near/pallas_call | solution.py:759
  28.3 10.9 %middle.1 = (bf16[64,16384]{1,0:T(8,128)(2,1)S(1)}, bf16[64,16384]{1,0:T(8,128)(2,1)}, f32[96,64]{1,0:T(8,128)S(1)}, f32[192,192]{1,0:T(8,128)S(1)}) custom-call(f32[8,16384]{1,0:T(8,128)S(1)} %recv_pick.1.tiles, f32[4,8,128]{2,1,0:T(8,128)S(1)} %get-tuple-element.55.pads, f32[2,64,128]{2,1,0:T(8,128)S(1)} %get-tuple-element.56.rims_in, ...), custom_call_target="tpu_custom_call" | custom-call | flops 2415919104 | bytes 8388608 | tf_op jit(solution)/shard_map/middle/pallas_call | solution.py:785
  40.2 1.7 %output.4 = (bf16[64,16384]{1,0:T(8,128)(2,1)}, f32[8,128]{1,0:T(8,128)S(1)}) custom-call(bf16[64,16384]{1,0:T(8,128)(2,1)S(1)} %get-tuple-element.60.hid.prev.nxt, bf16[64,16384]{1,0:T(8,128)(2,1)S(1)} %get-tuple-element.60.hid.prev.nxt, bf16[64,16384]{1,0:T(8,128)(2,1)S(1)} %get-tuple-element.60.hid.prev.nxt, ...), custom_call_target="tpu_custom_call" | custom-call | flops 301989888 | bytes 1048576 | tf_op jit(solution)/shard_map/output/pallas_call | solution.py:841
  42.4 1.6 %collective-permute-start.7 = (f32[48,256]{1,0:T(8,128)S(1)}, f32[48,256]{1,0:T(8,128)S(1)}, u32[]{:S(2)}, u32[]{:S(2)}) collective-permute-start(f32[48,256]{1,0:T(8,128)S(1)} %get-tuple-element.71.rest_0_), channel_id=1, source_target_pairs={{0,2},{2,0},{1,3},{3,1},{4,6},{6,4},{5,7},{7,5},{8,10},{10,8},{9,1... | collective-permute-start | bytes 147464 | tf_op jit(solution)/shard_map/ppermute | solution.py:858
  44.0 1.6 %output.5 = (bf16[64,16384]{1,0:T(8,128)(2,1)}, f32[8,128]{1,0:T(8,128)S(1)}) custom-call(bf16[64,16384]{1,0:T(8,128)(2,1)S(1)} %get-tuple-element.60.hid.prev.nxt, bf16[64,16384]{1,0:T(8,128)(2,1)S(1)} %get-tuple-element.60.hid.prev.nxt, bf16[64,16384]{1,0:T(8,128)(2,1)S(1)} %get-tuple-element.60.hid.prev.nxt, ...), custom_call_target="tpu_custom_call", output_to_operand_aliasing={{0}: (6, {})} | custom-call | flops 301989888 | bytes 1048576 | tf_op jit(solution)/shard_map/output/pallas_call | solution.py:841
  45.6 1.0 %collective-permute-done.7.got = f32[48,256]{1,0:T(8,128)S(1)} collective-permute-done((f32[48,256]{1,0:T(8,128)S(1)}, f32[48,256]{1,0:T(8,128)S(1)}, u32[]{:S(2)}, u32[]{:S(2)}) %collective-permute-start.7) | collective-permute-done | bytes 49184 | tf_op jit(solution)/shard_map/ppermute | solution.py:858
  46.6 2.6 %collective-permute-start.10 = (f32[48,256]{1,0:T(8,128)S(1)}, f32[48,256]{1,0:T(8,128)S(1)}, u32[]{:S(2)}, u32[]{:S(2)}) collective-permute-start(f32[48,256]{1,0:T(8,128)S(1)} %add.5.rest_0_.mine), channel_id=1, source_target_pairs={{0,12},{4,8},{8,4},{12,0},{1,13},{5,9},{9,5},{13,1},{2,14},{6,10},... | collective-permute-start | bytes 147464 | tf_op jit(solution)/shard_map/ppermute | solution.py:659
  49.2 1.8 %collective-permute-start.8 = (f32[48,256]{1,0:T(8,128)S(1)}, f32[48,256]{1,0:T(8,128)S(1)}, u32[]{:S(2)}, u32[]{:S(2)}) collective-permute-start(f32[48,256]{1,0:T(8,128)S(1)} %add.5.rest_0_.mine), channel_id=1, source_target_pairs={{0,4},{4,0},{8,12},{12,8},{1,5},{5,1},{9,13},{13,9},{2,6},{6,2},{1... | collective-permute-start | bytes 147464 | tf_op jit(solution)/shard_map/ppermute | solution.py:659
  51.1 1.6 %output.6 = (bf16[64,16384]{1,0:T(8,128)(2,1)}, f32[8,128]{1,0:T(8,128)S(1)}) custom-call(bf16[64,16384]{1,0:T(8,128)(2,1)S(1)} %get-tuple-element.60.hid.prev.nxt, bf16[64,16384]{1,0:T(8,128)(2,1)S(1)} %get-tuple-element.60.hid.prev.nxt, bf16[64,16384]{1,0:T(8,128)(2,1)S(1)} %get-tuple-element.60.hid.prev.nxt, ...), custom_call_target="tpu_custom_call", output_to_operand_aliasing={{0}: (6, {})} | custom-call | flops 301989888 | bytes 1048576 | tf_op jit(solution)/shard_map/output/pallas_call | solution.py:841
  52.7 1.5 %collective-permute-done.9.rest_1_ = f32[48,256]{1,0:T(8,128)S(1)} collective-permute-done((f32[48,256]{1,0:T(8,128)S(1)}, f32[48,256]{1,0:T(8,128)S(1)}, u32[]{:S(2)}, u32[]{:S(2)}) %collective-permute-start.9) | collective-permute-done | bytes 49184 | tf_op jit(solution)/shard_map/ppermute | solution.py:659
  54.9 1.6 %collective-permute-start.11 = (f32[48,256]{1,0:T(8,128)S(1)}, f32[48,256]{1,0:T(8,128)S(1)}, u32[]{:S(2)}, u32[]{:S(2)}) collective-permute-start(f32[48,256]{1,0:T(8,128)S(1)} %ring.1.rest_0_.mine), channel_id=1, source_target_pairs={{0,2},{2,0},{1,3},{3,1},{4,6},{6,4},{5,7},{7,5},{8,10},{10,8},{9,1... | collective-permute-start | bytes 147464 | tf_op jit(solution)/shard_map/ppermute | solution.py:858
  56.4 1.7 %output.7 = (bf16[64,16384]{1,0:T(8,128)(2,1)}, f32[8,128]{1,0:T(8,128)S(1)}) custom-call(bf16[64,16384]{1,0:T(8,128)(2,1)S(1)} %get-tuple-element.60.hid.prev.nxt, bf16[64,16384]{1,0:T(8,128)(2,1)S(1)} %get-tuple-element.60.hid.prev.nxt, bf16[64,16384]{1,0:T(8,128)(2,1)S(1)} %get-tuple-element.60.hid.prev.nxt, ...), custom_call_target="tpu_custom_call", output_to_operand_aliasing={{0}: (6, {})} | custom-call | flops 301989888 | bytes 1048576 | tf_op jit(solution)/shard_map/output/pallas_call | solution.py:841
  58.1 0.9 %collective-permute-done.11.got = f32[48,256]{1,0:T(8,128)S(1)} collective-permute-done((f32[48,256]{1,0:T(8,128)S(1)}, f32[48,256]{1,0:T(8,128)S(1)}, u32[]{:S(2)}, u32[]{:S(2)}) %collective-permute-start.11) | collective-permute-done | bytes 49184 | tf_op jit(solution)/shard_map/ppermute | solution.py:858
  59.7 1.3 %collective-permute-done.12.got = f32[96,256]{1,0:T(8,128)S(1)} collective-permute-done((f32[96,256]{1,0:T(8,128)S(1)}, f32[96,256]{1,0:T(8,128)S(1)}, u32[]{:S(2)}, u32[]{:S(2)}) %collective-permute-start.12) | collective-permute-done | bytes 98336 | tf_op jit(solution)/shard_map/ppermute | solution.py:858
  60.9 1.4 %last.1 = (f32[9,3,64]{2,1,0:T(4,128)}, f32[9,64,64]{2,1,0:T(8,128)}) custom-call(s32[3]{0:T(128)S(1)} %pad_add_fusion.scal, f32[96,256]{1,0:T(8,128)S(1)} %join.1.mine, f32[96,256]{1,0:T(8,128)S(1)} %collective-permute-done.12.got), custom_call_target="tpu_custom_call" | custom-call | flops 1000 | bytes 393216 | tf_op jit(solution)/shard_map/last/pallas_call | solution.py:900
  (35 shorter events, 5.4 us)
Async XLA Ops:
  0.7 0.9 %copy-start.5 = (bf16[1,3,16384]{2,1,0:T(4,128)(2,1)S(1)}, bf16[1,3,16384]{2,1,0:T(4,128)(2,1)}, u32[]{:S(2)}) copy-start(bf16[1,3,16384]{2,1,0:T(4,128)(2,1)} %param.8) | copy-start | bytes 294916
  1.6 0.9 %copy-start.6 = (s32[24576]{0:T(1024)S(1)}, s32[24576]{0:T(1024)}, u32[]{:S(2)}) copy-start(s32[24576]{0:T(1024)} %param.9) | copy-start | bytes 294916
  2.5 9.7 %copy-start = (bf16[1,64,16384]{2,1,0:T(8,128)(2,1)S(1)}, bf16[1,64,16384]{2,1,0:T(8,128)(2,1)}, u32[]{:S(2)}) copy-start(bf16[1,64,16384]{2,1,0:T(8,128)(2,1)} %param.15) | copy-start | bytes 6291460
  2.5 9.7 %copy-start.1 = (bf16[9,64,64]{2,1,0:T(8,128)(2,1)S(1)}, bf16[9,64,64]{2,1,0:T(8,128)(2,1)}, u32[]{:S(2)}) copy-start(bf16[9,64,64]{2,1,0:T(8,128)(2,1)} %conv_second.1) | copy-start | bytes 221188
  2.5 9.7 %copy-start.2 = (bf16[9,64,3]{1,2,0:T(4,128)(2,1)S(1)}, bf16[9,64,3]{1,2,0:T(4,128)(2,1)}, u32[]{:S(2)}) copy-start(bf16[9,64,3]{1,2,0:T(4,128)(2,1)} %param.13) | copy-start | bytes 10372
  6.5 11.5 %copy-start.3 = (s32[4,4]{1,0:T(4,128)S(1)}, s32[4,4]{1,0:T(4,128)}, u32[]{:S(2)}) copy-start(s32[4,4]{1,0:T(4,128)} %nbr.5) | copy-start | bytes 196
  6.5 11.5 %copy-start.4 = (s32[4,4]{1,0:T(4,128)S(1)}, s32[4,4]{1,0:T(4,128)}, u32[]{:S(2)}) copy-start(s32[4,4]{1,0:T(4,128)} %fac.5) | copy-start | bytes 196
  6.5 11.5 %copy-start.7 = (s32[16384]{0:T(1024)S(1)}, s32[16384]{0:T(1024)}, u32[]{:S(2)}) copy-start(s32[16384]{0:T(1024)} %param.10) | copy-start | bytes 196612
  6.5 8.0 %collective-permute-start = (bf16[3,24,256]{2,1,0:T(8,128)(2,1)S(1)}, bf16[3,24,256]{2,1,0:T(8,128)(2,1)S(1)}, u32[]{:S(2)}, u32[]{:S(2)}) collective-permute-start(bf16[3,24,256]{2,1,0:T(8,128)(2,1)S(1)} %get-tuple-element.45), channel_id=1, source_target_pairs={{0,4},{4,0},{8,12},{12,8},{1,5},{5,1},{9,13},{13,9},{2,6},{6,2},{1... | collective-permute-start | bytes 110600 | tf_op jit(solution)/shard_map/ppermute | solution.py:659
  9.6 5.5 %collective-permute-start.1 = (bf16[3,24,256]{2,1,0:T(8,128)(2,1)S(1)}, bf16[3,24,256]{2,1,0:T(8,128)(2,1)S(1)}, u32[]{:S(2)}, u32[]{:S(2)}) collective-permute-start(bf16[3,24,256]{2,1,0:T(8,128)(2,1)S(1)} %get-tuple-element.46), channel_id=1, source_target_pairs={{0,8},{4,12},{8,0},{12,4},{1,9},{5,13},{9,1},{13,5},{2,10},{6,14},... | collective-permute-start | bytes 110600 | tf_op jit(solution)/shard_map/ppermute | solution.py:659
  12.2 5.8 %collective-permute-start.2 = (bf16[3,24,256]{2,1,0:T(8,128)(2,1)S(1)}, bf16[3,24,256]{2,1,0:T(8,128)(2,1)S(1)}, u32[]{:S(2)}, u32[]{:S(2)}) collective-permute-start(bf16[3,24,256]{2,1,0:T(8,128)(2,1)S(1)} %get-tuple-element.47), channel_id=1, source_target_pairs={{0,12},{4,8},{8,4},{12,0},{1,13},{5,9},{9,5},{13,1},{2,14},{6,10},... | collective-permute-start | bytes 110600 | tf_op jit(solution)/shard_map/ppermute | solution.py:659
  19.3 7.5 %collective-permute-start.3 = (bf16[96,128]{1,0:T(8,128)(2,1)S(1)}, bf16[96,128]{1,0:T(8,128)(2,1)S(1)}, u32[]{:S(2)}, u32[]{:S(2)}) collective-permute-start(bf16[96,128]{1,0:T(8,128)(2,1)S(1)} %get-tuple-element.52), channel_id=1, source_target_pairs={{0,4},{4,0},{8,12},{12,8},{1,5},{5,1},{9,13},{13,9},{2,6},{6,2},{1... | collective-permute-start | bytes 73736 | tf_op jit(solution)/shard_map/ppermute | solution.py:659
  19.3 7.4 %collective-permute-start.4 = (bf16[96,128]{1,0:T(8,128)(2,1)S(1)}, bf16[96,128]{1,0:T(8,128)(2,1)S(1)}, u32[]{:S(2)}, u32[]{:S(2)}) collective-permute-start(bf16[96,128]{1,0:T(8,128)(2,1)S(1)} %get-tuple-element.53), channel_id=1, source_target_pairs={{0,8},{4,12},{8,0},{12,4},{1,9},{5,13},{9,1},{13,5},{2,10},{6,14},... | collective-permute-start | bytes 73736 | tf_op jit(solution)/shard_map/ppermute | solution.py:659
  20.4 6.4 %collective-permute-start.5 = (bf16[96,128]{1,0:T(8,128)(2,1)S(1)}, bf16[96,128]{1,0:T(8,128)(2,1)S(1)}, u32[]{:S(2)}, u32[]{:S(2)}) collective-permute-start(bf16[96,128]{1,0:T(8,128)(2,1)S(1)} %get-tuple-element.54), channel_id=1, source_target_pairs={{0,12},{4,8},{8,4},{12,0},{1,13},{5,9},{9,5},{13,1},{2,14},{6,10},... | collective-permute-start | bytes 73736 | tf_op jit(solution)/shard_map/ppermute | solution.py:659
  40.1 1.7 %collective-permute-start.6 = (f32[96,256]{1,0:T(8,128)S(1)}, f32[96,256]{1,0:T(8,128)S(1)}, u32[]{:S(2)}, u32[]{:S(2)}) collective-permute-start(f32[96,256]{1,0:T(8,128)S(1)} %get-tuple-element.68.rest_0_), channel_id=1, source_target_pairs={{0,1},{1,0},{2,3},{3,2},{4,5},{5,4},{6,7},{7,6},{8,9},{9,8},{10,11... | collective-permute-start | bytes 294920 | tf_op jit(solution)/shard_map/ppermute | solution.py:858
  42.4 4.2 %collective-permute-start.7 = (f32[48,256]{1,0:T(8,128)S(1)}, f32[48,256]{1,0:T(8,128)S(1)}, u32[]{:S(2)}, u32[]{:S(2)}) collective-permute-start(f32[48,256]{1,0:T(8,128)S(1)} %get-tuple-element.71.rest_0_), channel_id=1, source_target_pairs={{0,2},{2,0},{1,3},{3,1},{4,6},{6,4},{5,7},{7,5},{8,10},{10,8},{9,1... | collective-permute-start | bytes 147464 | tf_op jit(solution)/shard_map/ppermute | solution.py:858
  46.6 6.1 %collective-permute-start.10 = (f32[48,256]{1,0:T(8,128)S(1)}, f32[48,256]{1,0:T(8,128)S(1)}, u32[]{:S(2)}, u32[]{:S(2)}) collective-permute-start(f32[48,256]{1,0:T(8,128)S(1)} %add.5.rest_0_.mine), channel_id=1, source_target_pairs={{0,12},{4,8},{8,4},{12,0},{1,13},{5,9},{9,5},{13,1},{2,14},{6,10},... | collective-permute-start | bytes 147464 | tf_op jit(solution)/shard_map/ppermute | solution.py:659
  49.2 5.0 %collective-permute-start.9 = (f32[48,256]{1,0:T(8,128)S(1)}, f32[48,256]{1,0:T(8,128)S(1)}, u32[]{:S(2)}, u32[]{:S(2)}) collective-permute-start(f32[48,256]{1,0:T(8,128)S(1)} %add.5.rest_0_.mine), channel_id=1, source_target_pairs={{0,8},{4,12},{8,0},{12,4},{1,9},{5,13},{9,1},{13,5},{2,10},{6,14},... | collective-permute-start | bytes 147464 | tf_op jit(solution)/shard_map/ppermute | solution.py:659
  49.2 5.1 %collective-permute-start.8 = (f32[48,256]{1,0:T(8,128)S(1)}, f32[48,256]{1,0:T(8,128)S(1)}, u32[]{:S(2)}, u32[]{:S(2)}) collective-permute-start(f32[48,256]{1,0:T(8,128)S(1)} %add.5.rest_0_.mine), channel_id=1, source_target_pairs={{0,4},{4,0},{8,12},{12,8},{1,5},{5,1},{9,13},{13,9},{2,6},{6,2},{1... | collective-permute-start | bytes 147464 | tf_op jit(solution)/shard_map/ppermute | solution.py:659
  54.9 4.2 %collective-permute-start.11 = (f32[48,256]{1,0:T(8,128)S(1)}, f32[48,256]{1,0:T(8,128)S(1)}, u32[]{:S(2)}, u32[]{:S(2)}) collective-permute-start(f32[48,256]{1,0:T(8,128)S(1)} %ring.1.rest_0_.mine), channel_id=1, source_target_pairs={{0,2},{2,0},{1,3},{3,1},{4,6},{6,4},{5,7},{7,5},{8,10},{10,8},{9,1... | collective-permute-start | bytes 147464 | tf_op jit(solution)/shard_map/ppermute | solution.py:858
  59.6 1.4 %collective-permute-start.12 = (f32[96,256]{1,0:T(8,128)S(1)}, f32[96,256]{1,0:T(8,128)S(1)}, u32[]{:S(2)}, u32[]{:S(2)}) collective-permute-start(f32[96,256]{1,0:T(8,128)S(1)} %join.1.mine), channel_id=1, source_target_pairs={{0,1},{1,0},{2,3},{3,2},{4,5},{5,4},{6,7},{7,6},{8,9},{9,8},{10,11... | collective-permute-start | bytes 294920 | tf_op jit(solution)/shard_map/ppermute | solution.py:858

commit v4 on v3

--- a/solution.py
+++ b/solution.py
@@ -253,7 +253,24 @@
     out[CIN:, :] = jnp.zeros((8 - CIN, PIX), F32)
 
 
-def edge_kernel(cot, conv_second, conv_first, rims, columns, fwd_w, back_w, w1, side_w, acc, table):
+def shift_rows(near, step, cot, prev, nxt):
+    no_first, no_last = keep_lane(0), keep_lane(SIDE - 1)
+    for t in range(ROWS + 2):
+        if t == 0:
+            line = jnp.where(step > 0, prev[...], jnp.zeros_like(prev))
+        elif t == ROWS + 1:
+            line = jnp.where(step < STEPS - 1, nxt[...], jnp.zeros_like(nxt))
+        else:
+            line = cot[:, (t - 1) * SIDE : t * SIDE]
+        lanes = slice(t * SIDE, (t + 1) * SIDE)
+        near[:CH, lanes] = pltpu.roll(line, SIDE - 1, 1) * no_last
+        near[CH : 2 * CH, lanes] = line
+        near[2 * CH :, lanes] = pltpu.roll(line, 1, 1) * no_first
+
+
+def edge_kernel(
+    cot, prev, nxt, conv_second, conv_first, hg, rims, columns, fwd_w, w1, side_w, back_w, acc, table, near
+):
     step = pl.program_id(0)
 
     @pl.when(step == 0)
@@ -282,6 +299,18 @@
         turned = pltpu.roll(line, lax.rem(2 * r + 1, SIDE), 1)
         got = jnp.where(pair == lax.rem(r, SIDE // 2), turned, got)
     acc[half] = got
+
+    weights = back_w[...]
+    shift_rows(near, step, cot, prev, nxt)
+    open_sum = open_last = None
+    for p in range(ROWS // 2 + 1):
+        z = dot(weights, near[:, 2 * p * SIDE : (2 * p + 2) * SIDE])
+        part = lambda a, r: z[a * CH : (a + 1) * CH, r * SIDE : (r + 1) * SIDE]
+        if p > 0:
+            hg[:, (2 * p - 2) * SIDE : (2 * p - 1) * SIDE] = open_sum + part(0, 0)
+            hg[:, (2 * p - 1) * SIDE : 2 * p * SIDE] = part(0, 1) + part(1, 0) + open_last
+        open_sum = part(1, 1) + part(2, 0)
+        open_last = part(2, 1)
 
     def rim_row(line, a):
         line = line.astype(F32)
@@ -337,9 +366,9 @@
     return pad
 
 
-def near_kernel(tile_count, scal, nbr, fac, strips, comb, side_w, *rest):
-    n = tile_count - 1
-    arrived, (pads, rims_in, rims_cols, incoming, table, ends, lines) = rest[:n], rest[n:]
+def near_part(
+    tile_count, scal, nbr, fac, strips, comb, side_w, arrived, pads, rims_in, rims_cols, incoming, table, ends, lines
+):
     me = scal[0]
     got = take_strips(tile_count, True, nbr, fac, me, comb, arrived, table)
     pad = deliver(got, pads, rims_in, rims_cols)
@@ -399,9 +428,7 @@
     send_strips(tile_count, False, nbr, me, own, [sends])
 
 
-def middle_kernel(
-    tiles, pads, rims_in, rims_cols, w1_ref, back_w, cot, prev, nxt, hidden, grad, g1, g2, planes, near, kept
-):
+def middle_step(tiles, pads, rims_in, rims_cols, w1_ref, hg, cot, prev, nxt, hidden, grad, g1, g2, planes, near, kept):
     step = pl.program_id(0)
 
     @pl.when(step == 0)
@@ -423,66 +450,44 @@
             put(i + 1, tiles[:, i * SIDE : (i + 1) * SIDE], ends)
 
     w1 = w1_ref[...]
-    weights = back_w[...]
-    no_first, no_last = keep_lane(0), keep_lane(SIDE - 1)
     end = is_end((CH, SIDE))
 
     def weigh(first, count):
         three = [kept[:, (first + a) * SIDE : (first + a + count) * SIDE] for a in range(3)]
         return dot_nt(near[:, first * SIDE : (first + count) * SIDE], jnp.concatenate(three, axis=0))
 
-    open_sum = open_last = None
-    slopes = []
-    for p in range(ROWS // 2 + 1):
-        for t in (2 * p, 2 * p + 1):
+    shift_rows(near, step, cot, prev, nxt)
+    n_rows = 4
+    acc1 = g1[...]
+    for p in range(ROWS // n_rows):
+        base = step * ROWS + p * n_rows
+        cols = []
+        for a in range(3):
+            lanes = pl.ds(pl.multiple_of((base + a) * SIDE, SIDE), n_rows * SIDE)
+            cols.append(planes[:, lanes])
+        cols = jnp.concatenate(cols, axis=0)
+        pre = dot(w1, cols)
+        sigma = jax.nn.sigmoid(pre)
+        hid = pre * sigma
+        slope = sigma + hid * (1.0 - sigma)
+        slopes = []
+        for r in range(n_rows):
+            t = p * n_rows + r
+            line = hg[:, t * SIDE : (t + 1) * SIDE]
+            line = line + jnp.where(end, row_ends(rims_cols, base + r).astype(F32), 0.0)
             if t == 0:
-                line = jnp.where(step > 0, prev[...], jnp.zeros_like(prev))
-            elif t == ROWS + 1:
-                line = jnp.where(step < STEPS - 1, nxt[...], jnp.zeros_like(nxt))
-            else:
-                line = cot[:, (t - 1) * SIDE : t * SIDE]
-            lanes = slice(t * SIDE, (t + 1) * SIDE)
-            near[:CH, lanes] = pltpu.roll(line, SIDE - 1, 1) * no_last
-            near[CH : 2 * CH, lanes] = line
-            near[2 * CH :, lanes] = pltpu.roll(line, 1, 1) * no_first
-        z = dot(weights, near[:, 2 * p * SIDE : (2 * p + 2) * SIDE])
-        part = lambda a, r: z[a * CH : (a + 1) * CH, r * SIDE : (r + 1) * SIDE]
-        if p > 0:
-            pair = [open_sum + part(0, 0), part(0, 1) + part(1, 0) + open_last]
-            base = step * ROWS + 2 * p - 2
-            cols = []
-            for a in range(3):
-                lanes = pl.ds(pl.multiple_of((base + a) * SIDE, SIDE), 2 * SIDE)
-                cols.append(planes[:, lanes])
-            pre = dot(w1, jnp.concatenate(cols, axis=0))
-            sigma = jax.nn.sigmoid(pre)
-            hid = pre * sigma
-            slope = sigma + hid * (1.0 - sigma)
-            for r in range(2):
-                t = 2 * p - 2 + r
-                line = pair[r]
-                line = line + jnp.where(end, row_ends(rims_cols, base + r).astype(F32), 0.0)
-                if t == 0:
-                    line = line + jnp.where(step == 0, rims_in[0], 0.0)
-                if t == ROWS - 1:
-                    line = line + jnp.where(step == STEPS - 1, rims_in[1], 0.0)
-                grad[:, t * SIDE : (t + 1) * SIDE] = line.astype(BF16)
-                slopes.append((line * slope[:, r * SIDE : (r + 1) * SIDE]).astype(BF16))
-            hid = hid.astype(BF16)
-            hidden[:, (2 * p - 2) * SIDE : 2 * p * SIDE] = hid
-            kept[:, 2 * p * SIDE : (2 * p + 2) * SIDE] = hid
-        open_sum = part(1, 1) + part(2, 0)
-        open_last = part(2, 1)
-        if p > 0 and p % 4 == 0:
-            count = len(slopes)
-            cols = []
-            for a in range(3):
-                lanes = pl.ds(pl.multiple_of((step * ROWS + 2 * p - count + a) * SIDE, SIDE), count * SIDE)
-                cols.append(planes[:, lanes])
-            g1[...] += dot_nt(jnp.concatenate(cols, axis=0), jnp.concatenate(slopes, axis=1))
-            slopes = []
-        if p > 0 and p % 8 == 0:
-            g2[...] += weigh(2 * p - 16, 16)
+                line = line + jnp.where(step == 0, rims_in[0], 0.0)
+            if t == ROWS - 1:
+                line = line + jnp.where(step == STEPS - 1, rims_in[1], 0.0)
+            grad[:, t * SIDE : (t + 1) * SIDE] = line.astype(BF16)
+            slopes.append((line * slope[:, r * SIDE : (r + 1) * SIDE]).astype(BF16))
+        lanes = slice(p * n_rows * SIDE, (p + 1) * n_rows * SIDE)
+        hid = hid.astype(BF16)
+        hidden[:, lanes] = hid
+        kept[:, (p * n_rows + 2) * SIDE : ((p + 1) * n_rows + 2) * SIDE] = hid
+        acc1 = acc1 + dot_nt(cols, jnp.concatenate(slopes, axis=1))
+    g1[...] = acc1
+    g2[...] += weigh(0, ROWS)
 
     @pl.when(step == STEPS - 1)
     def _():
@@ -492,15 +497,36 @@
     kept[:, : 2 * SIDE] = kept[:, ROWS * SIDE : (ROWS + 2) * SIDE]
 
 
-def close_kernel(tile_count, direct, scale, scal, nbr, fac, columns, top, bottom, g1, g2, *rest):
-    if direct:
-        incoming, pads, keep, send, total = rest
-        north, east, south, west = [incoming[k] for k in range(4)]
-    else:
-        own, arrived, pads, keep, send, total, table = rest
-        got = take_strips(tile_count, direct, nbr, fac, scal[0], own, [arrived], table)
-        north, east = reverse(got[0]).astype(BF16), reverse(got[1]).astype(BF16)
-        south, west = got[2], got[3]
+def middle_kernel(tile_count, scale, quarters, *refs):
+    scal, nbr, fac, strips, comb, side_w, *refs = refs
+    arrived, refs = refs[: tile_count - 1], refs[tile_count - 1 :]
+    tiles, w1_ref, hg, cot, prev, nxt, columns, top, bottom, *refs = refs
+    hidden, grad, edge_pads, *refs = refs
+    parts, refs = refs[:quarters], refs[quarters:]
+    pads, rims_in, rims_cols, incoming, table, ends, lines, g1, g2, planes, near, kept, total = refs
+    step = pl.program_id(0)
+
+    @pl.when(step == 0)
+    def _():
+        near_part(
+            tile_count, scal, nbr, fac, strips, comb, side_w, arrived, pads, rims_in, rims_cols, incoming, table, ends, lines
+        )
+
+    middle_step(tiles, pads, rims_in, rims_cols, w1_ref, hg, cot, prev, nxt, hidden, grad, g1, g2, planes, near, kept)
+
+    @pl.when(step == STEPS - 1)
+    def _():
+        close_part(scale, scal, [incoming[k] for k in range(4)], columns, top, bottom, g1, g2, edge_pads, parts, total)
+
+
+def close_kernel(tile_count, scale, scal, nbr, fac, columns, top, bottom, g1, g2, own, arrived, pads, keep, total, table):
+    got = take_strips(tile_count, False, nbr, fac, scal[0], own, [arrived], table)
+    four = [reverse(got[0]).astype(BF16), reverse(got[1]).astype(BF16), got[2], got[3]]
+    close_part(scale, scal, four, columns, top, bottom, g1, g2, pads, [keep], total)
+
+
+def close_part(scale, scal, four, columns, top, bottom, g1, g2, pads, parts, total):
+    north, east, south, west = four
     pads[0] = north
     pads[1] = south
     side = dot(west, ends_table(0, False)) + dot(east, ends_table(0, True))
@@ -519,26 +545,17 @@
     total[:, 2 * CH : 3 * CH] += dot_nt(three_ways(bottom[...], False), south) * scale
     total[:CH, : 3 * CH] += dot_nt(columns[0], three_ways(west, True)) * scale
     total[2 * CH :, : 3 * CH] += dot_nt(columns[1], three_ways(east, True)) * scale
-    core = scal[2]
-    half = keep.shape[0]
-    if half == 3 * CH:
-        keep[...] = total[...]
-        send[...] = jnp.zeros_like(send)
+    if len(parts) == 1:
+        parts[0][...] = total[...]
     else:
-        keep[...] = total[pl.ds(pl.multiple_of(core * half, 8), half), :]
-        send[...] = total[pl.ds(pl.multiple_of((1 - core) * half, 8), half), :]
-
-
-def pair_kernel(scal, kept, got, after, keep, send, total):
-    total[...] = kept[...] + got[...]
-    half = keep.shape[0]
-    here = scal[1]
-    keep[...] = total[pl.ds(pl.multiple_of(here * half, 8), half), :]
-    send[...] = total[pl.ds(pl.multiple_of((1 - here) * half, 8), half), :]
-
-
-def add_kernel(mine, got, after, out):
-    out[...] = mine[...] + got[...]
+        mine = 2 * scal[1] + scal[2]
+        rows = parts[0].shape[0]
+        for r, part in enumerate(parts):
+            part[...] = total[pl.ds(pl.multiple_of((mine ^ r) * rows, 8), rows), :]
+
+
+def add_kernel(mine, one, two, three, after, out):
+    out[...] = (mine[...] + one[...]) + (two[...] + three[...])
 
 
 def ring_kernel(tile_count, scal, mine, *rest):
@@ -553,13 +570,6 @@
     out[...] = total
 
 
-def join_kernel(scal, mine, got, after, out):
-    half = mine.shape[0]
-    here = scal[1]
-    out[pl.ds(pl.multiple_of(here * half, 8), half), :] = mine[...]
-    out[pl.ds(pl.multiple_of((1 - here) * half, 8), half), :] = got[...]
-
-
 def unpack(total, first, second):
     for a in range(3):
         for b in range(3):
@@ -568,11 +578,11 @@
             first[3 * a + b] = total[row : row + CIN, 3 * CH :]
 
 
-def last_kernel(scal, mine, got, first, second, total):
-    half = mine.shape[0]
-    here = scal[2]
-    total[pl.ds(pl.multiple_of(here * half, 8), half), :] = mine[...]
-    total[pl.ds(pl.multiple_of((1 - here) * half, 8), half), :] = got[...]
+def last_kernel(scal, mine, one, two, three, first, second, total):
+    here = 2 * scal[1] + scal[2]
+    rows = mine.shape[0]
+    for r, part in enumerate((mine, one, two, three)):
+        total[pl.ds(pl.multiple_of((here ^ r) * rows, 8), rows), :] = part[...]
     unpack(total, first, second)
 
 
@@ -695,32 +705,37 @@
         blocks = exchange(blocks)
 
     square = (3 * CH, 3 * CH)
-    rims, columns, fwd_w, back_w, w1, side_w = call(
+    hg, rims, columns, fwd_w, w1, side_w = call(
         edge_kernel,
         "edges",
-        conv_flops // 8,
-        2 * CH * PIX,
+        conv_flops,
+        6 * CH * PIX,
         16,
         grid=(STEPS,),
-        in_specs=[row_block(), whole((9, CH, CH)), whole((9, CIN, CH))],
+        in_specs=[row_block(), row_before(), row_after(), whole((9, CH, CH)), whole((9, CIN, CH))],
         out_specs=[
+            row_block(),
             whole((4, CH, SIDE)),
             whole((2, CH, SIDE)),
-            whole(square),
             whole(square),
             whole((CH, 96)),
             whole((4, CH, 96)),
         ],
         out_shape=[
+            shape((CH, PIX), F32),
             shape((4, CH, SIDE), BF16),
             shape((2, CH, SIDE), BF16),
-            shape(square, BF16),
             shape(square, BF16),
             shape((CH, 96), BF16),
             shape((4, CH, 96), BF16),
         ],
-        scratch_shapes=[pltpu.VMEM((2, CH, SIDE), F32), pltpu.VMEM((SIDE, SIDE), F32)],
-    )(cot, conv_second, jnp.swapaxes(conv_first, 1, 2))
+        scratch_shapes=[
+            pltpu.VMEM(square, BF16),
+            pltpu.VMEM((2, CH, SIDE), F32),
+            pltpu.VMEM((SIDE, SIDE), F32),
+            pltpu.VMEM((3 * CH, (ROWS + 2) * SIDE), BF16),
+        ],
+    )(cot, cot, cot, conv_second, jnp.swapaxes(conv_first, 1, 2))
 
     index = recv_pick.reshape(SIDE, SIDE)
     *sends, source, strips, comb = call(
@@ -748,26 +763,45 @@
         out_shape=shape((8, PIX), F32),
     )(index, source)
 
-    pads_shapes = [
-        shape((4, 8, SIDE), F32),
-        shape((2, CH, SIDE), F32),
-        shape((2, CH, SIDE), BF16),
-        shape((4, CH, SIDE), BF16),
+    pad_buffers = [((4, 8, SIDE), F32), ((2, CH, SIDE), F32), ((2, CH, SIDE), BF16), ((4, CH, SIDE), BF16)]
+    table = pltpu.VMEM((5 + tile_count, COMB, SIDE), BF16)
+    scale = 1.0 / math.sqrt(map_count * chans * cores * tile_count * PIX)
+    fast_sum = direct and chans == 2 and cores == 2
+    quarters = 4 if fast_sum else 1
+    rows = 3 * CH // quarters
+    top = pl.BlockSpec((CH, SIDE), lambda i: (0, 0))
+    bottom = pl.BlockSpec((CH, SIDE), lambda i: (0, SIDE - 1))
+    gradients = [((96, CH), F32), (square, F32)]
+    work = [
+        pltpu.VMEM((32, (SIDE + 2) * SIDE), BF16),
+        pltpu.VMEM((3 * CH, (ROWS + 2) * SIDE), BF16),
+        pltpu.VMEM((CH, (ROWS + 3) * SIDE), BF16),
     ]
-    table = pltpu.VMEM((5 + tile_count, COMB, SIDE), BF16)
+    cot_blocks = [row_block(), row_block(), row_before(), row_after()]
     if direct:
-        pads, rims_in, rims_cols, incoming = call(
-            functools.partial(near_kernel, tile_count),
-            "near",
-            conv_flops // 128,
-            PIX,
-            8,
-            in_specs=[SMEM] * 3 + [VMEM] * (3 + n_send),
-            out_specs=[VMEM] * 4,
-            out_shape=pads_shapes,
-            scratch_shapes=[table, pltpu.VMEM((4, 8, SIDE), F32), pltpu.VMEM((96, SIDE), F32)],
-        )(scal, neighbour, facing, strips, comb, side_w, *arrived)
-        edges_in = [incoming]
+        hidden, grad, pads2, *parts = call(
+            functools.partial(middle_kernel, tile_count, scale, quarters),
+            "middle",
+            conv_flops,
+            12 * CH * PIX,
+            24,
+            grid=(STEPS,),
+            in_specs=[SMEM] * 3
+            + [whole(x.shape) for x in (strips, comb, side_w, *arrived, tiles, w1)]
+            + cot_blocks
+            + [whole((2, CH, SIDE)), top, bottom],
+            out_specs=[row_block(), row_block(), whole((4, CH, SIDE))] + [whole((rows, LOW))] * quarters,
+            out_shape=[shape((CH, PIX), BF16), shape((CH, PIX), BF16), shape((4, CH, SIDE), BF16)]
+            + [shape((rows, LOW), F32)] * quarters,
+            scratch_shapes=[pltpu.VMEM(*x) for x in pad_buffers]
+            + [table, pltpu.VMEM((4, 8, SIDE), F32), pltpu.VMEM((96, SIDE), F32)]
+            + [pltpu.VMEM(*x) for x in gradients]
+            + work
+            + [pltpu.VMEM((3 * CH, LOW), F32)],
+        )(
+            *(scal, neighbour, facing, strips, comb, side_w, *arrived),
+            *(tiles, w1, hg, cot, cot, cot, columns, cot, cot),
+        )
     else:
         pads, rims_in, rims_cols, own, sends = call(
             functools.partial(border_kernel, tile_count),
@@ -777,62 +811,35 @@
             8,
             in_specs=[SMEM] * 3 + [VMEM] * 4,
             out_specs=[VMEM] * 5,
-            out_shape=pads_shapes + sent((CH, SIDE), BF16),
+            out_shape=[shape(*x) for x in pad_buffers] + sent((CH, SIDE), BF16),
             scratch_shapes=[table, pltpu.VMEM((96, 4 * SIDE), F32)],
         )(scal, neighbour, facing, strips, comb, w1, *arrived)
-        edges_in = [own] + exchange([sends])
-
-    hidden, grad, g1, g2 = call(
-        middle_kernel,
-        "middle",
-        2 * conv_flops,
-        8 * CH * PIX,
-        24,
-        grid=(STEPS,),
-        in_specs=[
-            whole((8, PIX)),
-            whole((4, 8, SIDE)),
-            whole((2, CH, SIDE)),
-            whole((2, CH, SIDE)),
-            whole((CH, 96)),
-            whole(square),
-            row_block(),
-            row_before(),
-            row_after(),
-        ],
-        out_specs=[row_block(), row_block(), whole((96, CH)), whole(square)],
-        out_shape=[shape((CH, PIX), BF16), shape((CH, PIX), BF16), shape((96, CH), F32), shape(square, F32)],
-        scratch_shapes=[
-            pltpu.VMEM((32, (SIDE + 2) * SIDE), BF16),
-            pltpu.VMEM((3 * CH, (ROWS + 2) * SIDE), BF16),
-            pltpu.VMEM((CH, (ROWS + 3) * SIDE), BF16),
-        ],
-    )(tiles, pads, rims_in, rims_cols, w1, back_w, cot, cot, cot)
-
-    scale = 1.0 / math.sqrt(map_count * chans * cores * tile_count * PIX)
-    fast_sum = direct and chans == 2 and cores == 2
-    half = 3 * CH // 2 if fast_sum else 3 * CH
-    top = pl.BlockSpec((CH, SIDE), lambda i: (0, 0))
-    bottom = pl.BlockSpec((CH, SIDE), lambda i: (0, SIDE - 1))
-    pads2, keep, send = call(
-        functools.partial(close_kernel, tile_count, direct, scale),
-        "close",
-        conv_flops // 128,
-        PIX,
-        8,
-        grid=(1,),
-        in_specs=[SMEM, SMEM, SMEM, whole((2, CH, SIDE)), top, bottom]
-        + [whole((96, CH)), whole(square)]
-        + [whole(x.shape) for x in edges_in],
-        out_specs=[whole((4, CH, SIDE)), whole((half, LOW)), whole((half, LOW))],
-        out_shape=[
-            shape((4, CH, SIDE), BF16),
-            shape((half, LOW), F32),
-            shape((half, LOW), F32),
-        ],
-        scratch_shapes=[pltpu.VMEM((3 * CH, LOW), F32)]
-        + ([] if direct else [pltpu.VMEM((5 + tile_count, CH, SIDE), BF16)]),
-    )(scal, neighbour, facing, columns, cot, cot, g1, g2, *edges_in)
+        edges_in = exchange([sends])
+        hidden, grad, g1, g2 = call(
+            middle_step,
+            "middle",
+            conv_flops,
+            12 * CH * PIX,
+            24,
+            grid=(STEPS,),
+            in_specs=[whole(x.shape) for x in (tiles, pads, rims_in, rims_cols, w1)] + cot_blocks,
+            out_specs=[row_block(), row_block()] + [whole(x[0]) for x in gradients],
+            out_shape=[shape((CH, PIX), BF16), shape((CH, PIX), BF16)] + [shape(*x) for x in gradients],
+            scratch_shapes=work,
+        )(tiles, pads, rims_in, rims_cols, w1, hg, cot, cot, cot)
+        pads2, *parts = call(
+            functools.partial(close_kernel, tile_count, scale),
+            "close",
+            conv_flops // 128,
+            PIX,
+            8,
+            grid=(1,),
+            in_specs=[SMEM, SMEM, SMEM, whole((2, CH, SIDE)), top, bottom]
+            + [whole(x.shape) for x in (g1, g2, own, *edges_in)],
+            out_specs=[whole((4, CH, SIDE)), whole((rows, LOW))],
+            out_shape=[shape((4, CH, SIDE), BF16), shape((rows, LOW), F32)],
+            scratch_shapes=[pltpu.VMEM((3 * CH, LOW), F32), pltpu.VMEM((5 + tile_count, CH, SIDE), BF16)],
+        )(scal, neighbour, facing, columns, cot, cot, g1, g2, own, *edges_in)
 
     anywhere = pl.BlockSpec(memory_space=pl.ANY)
 
@@ -855,28 +862,21 @@
 
     finals = [shape((9, CIN, CH), F32), shape((9, CH, CH), F32)]
     if fast_sum:
-        swap = lambda x, name: lax.ppermute(x, name, [(0, 1), (1, 0)])
-        quarter = half // 2
-        small = lambda kernel, name, **kw: call(kernel, name, 1000, half * LOW * 16, 4, **kw)
-        got = swap(send, "sub")
-        out, token = convolve(0, 1, None, send)
-        keep2, send2 = small(
-            pair_kernel,
-            "pair",
-            in_specs=[SMEM, VMEM, VMEM, anywhere],
-            out_specs=[VMEM, VMEM],
-            out_shape=[shape((quarter, LOW), F32)] * 2,
-            scratch_shapes=[pltpu.VMEM((half, LOW), F32)],
-        )(scal, keep, got, token)
-        got = swap(send2, "chan")
-        out, token = convolve(1, 1, out, send2)
+        group = ("chan", "sub")
+
+        def swap(x, r):
+            return lax.ppermute(x, group, [(i, i ^ r) for i in range(4)])
+
+        small = lambda kernel, name, **kw: call(kernel, name, 1000, 4 * rows * LOW * 16, 4, **kw)
+        got = [swap(parts[r], r) for r in (1, 2, 3)]
+        out, token = convolve(0, 2, None, parts[1])
         mine = small(
             add_kernel,
             "add",
-            in_specs=[VMEM, VMEM, anywhere],
+            in_specs=[VMEM] * 4 + [anywhere],
             out_specs=VMEM,
-            out_shape=shape((quarter, LOW), F32),
-        )(keep2, got, token)
+            out_shape=shape((rows, LOW), F32),
+        )(parts[0], *got, token)
         got = exchange([mine] * n_send)
         out, token = convolve(2, 1, out, mine)
         mine = small(
@@ -884,30 +884,22 @@
             "ring",
             in_specs=[SMEM] + [VMEM] * tile_count + [anywhere],
             out_specs=VMEM,
-            out_shape=shape((quarter, LOW), F32),
-            scratch_shapes=[pltpu.VMEM((tile_count, quarter, LOW), F32)],
+            out_shape=shape((rows, LOW), F32),
+            scratch_shapes=[pltpu.VMEM((tile_count, rows, LOW), F32)],
         )(scal, mine, *got, token)
-        got = swap(mine, "chan")
+        got = [swap(mine, r) for r in (1, 2, 3)]
         out, token = convolve(3, 1, out, mine)
-        mine = small(
-            join_kernel,
-            "join",
-            in_specs=[SMEM, VMEM, VMEM, anywhere],
-            out_specs=VMEM,
-            out_shape=shape((half, LOW), F32),
-        )(scal, mine, got, token)
-        got = swap(mine, "sub")
         first, second = small(
             last_kernel,
             "last",
-            in_specs=[SMEM, VMEM, VMEM],
+            in_specs=[SMEM] + [VMEM] * 4,
             out_specs=[VMEM, VMEM],
             out_shape=finals,
             scratch_shapes=[pltpu.VMEM((3 * CH, LOW), F32)],
-        )(scal, mine, got)
+        )(scal, mine, *got)
     else:
-        out, _ = convolve(0, STEPS, None, send)
-        total = lax.psum(keep, ("tile", "chan", "sub"))
+        out, _ = convolve(0, STEPS, None, parts[0])
+        total = lax.psum(parts[0], ("tile", "chan", "sub"))
         first, second = pl.pallas_call(
             unpack, in_specs=[VMEM], out_specs=[VMEM, VMEM], out_shape=finals, name="unpack"
         )(total)

time: 62.5 us -> 57.5 us (0.920)
  Pallas kernels: 33.4 us -> 30 us
  waiting for transfers between devices: 8.28 us -> 5.93 us
  starting transfers between devices: 17.9 us -> 18.7 us
    pallas_call x8 -> x4, Pallas kernels: 18 us -> 15.2 us  [the longest x1 8.86 us: body(): call(functools.partial(middle_kernel, tile_count, scale, quarters), 'midd...]
    ppermute x9, waiting for transfers between devices: 5.06 us -> 3.78 us  [exchange(): lax.ppermute(x, 'tile', [(i, i ^ s) for i in range(tile_count)])]
    ppermute x4 -> x6, waiting for transfers between devices: 3.23 us -> 2.15 us  [swap(): return lax.ppermute(x, group, [(i, i ^ r) for i in range(4)])]
    ppermute x4 -> x6, starting transfers between devices: 3.27 us -> 4.07 us  [swap(): return lax.ppermute(x, group, [(i, i ^ r) for i in range(4)])]
    pallas_call x4 -> x3, Pallas kernels: 6.6 us -> 6 us  [convolve(): call(functools.partial(output_kernel, start), 'output', conv_flops * coun...]
  transfers between devices with their start and end apart: 13 -> 15, of which waited for: 6 -> 7; matrix products, arithmetic and copies ran while one was open for 0% -> 0% of each run, Pallas kernels for 19% -> 24%
where the time goes in v4:
time: 57.5 us; the launch traced here: 57.3 us
  Pallas kernels  30 us (52%)
  starting transfers between devices  18.7 us (33%)
  waiting for transfers between devices  5.93 us (10%)
  local copies, waits for them, and re-layouts  1.83 us (3%)
  between operations  0.77 us (1%)
    ppermute x9, starting transfers between devices, exchange(): lax.ppermute(x, 'tile', [(i, i ^ s) for i in range(tile_count)])  14.6 us
    pallas_call x1, Pallas kernels, body(): call(functools.partial(middle_kernel, tile_count, scale, quarters), 'midd...  8.86 us
    pallas_call x3, Pallas kernels, convolve(): call(functools.partial(output_kernel, start), 'output', conv_flops * coun...  6 us
    pallas_call x1, Pallas kernels, body(): call(edge_kernel, 'edges', conv_flops, 6 * CH * PIX, 16, grid=(STEPS,), i...  4.95 us
    ppermute x6, starting transfers between devices, swap(): return lax.ppermute(x, group, [(i, i ^ r) for i in range(4)])  4.07 us
    pallas_call x1, Pallas kernels, body(): call(functools.partial(send_kernel, tile_count, direct), 'send_pick', 2 *...  3.96 us
    ppermute x9, waiting for transfers between devices, exchange(): lax.ppermute(x, 'tile', [(i, i ^ s) for i in range(tile_count)])  3.78 us
    pallas_call x1, Pallas kernels, body(): call(functools.partial(main_pick_kernel, groups), 'recv_pick', 2 * CIN *...  3.04 us
  transfers between devices with their start and end apart: 15, of which 7 were waited for; matrix products, arithmetic and copies ran while one was open for 0% of the time, Pallas kernels for 24%

profile of v4, /device:TPU:0, one launch (start us, length us, event | category | flops | bytes accessed | tf_op | source)
XLA Modules:
  0.0 57.3 jit_solution(16397131407360263856)
XLA Ops:
  0.7 0.9 %copy-done.5 = bf16[1,3,16384]{2,1,0:T(4,128)(2,1)S(1)} copy-done((bf16[1,3,16384]{2,1,0:T(4,128)(2,1)S(1)}, bf16[1,3,16384]{2,1,0:T(4,128)(2,1)}, u32[]{:S(2)}) %copy-start.5) | copy-done | bytes 98328
  1.6 0.9 %copy-done.6 = s32[24576]{0:T(1024)S(1)} copy-done((s32[24576]{0:T(1024)S(1)}, s32[24576]{0:T(1024)}, u32[]{:S(2)}) %copy-start.6) | copy-done | bytes 98328
  2.5 4.0 %send_pick.1 = (bf16[3,24,256]{2,1,0:T(8,128)(2,1)S(1)}, bf16[3,24,256]{2,1,0:T(8,128)(2,1)S(1)}, bf16[3,24,256]{2,1,0:T(8,128)(2,1)S(1)}, bf16[3,24,256]{2,1,0:T(8,128)(2,1)S(1)}) custom-call(s32[3]{0:T(128)S(1)} %pad_add_fusion.scal.refs_0_, bf16[3,16384]{1,0:T(4,128)(2,1)S(1)} %bitcast.20, s32[192,128]{1,0:T(8,128)S(1)} %bitcast.21), custom_call_target="tpu_custom_call" | custom-call | flops 2415919104 | bytes 196608 | tf_op jit(solution)/shard_map/send_pick/pallas_call | solution.py:687
  6.5 3.1 %collective-permute-start = (bf16[3,24,256]{2,1,0:T(8,128)(2,1)S(1)}, bf16[3,24,256]{2,1,0:T(8,128)(2,1)S(1)}, u32[]{:S(2)}, u32[]{:S(2)}) collective-permute-start(bf16[3,24,256]{2,1,0:T(8,128)(2,1)S(1)} %get-tuple-element.36), channel_id=1, source_target_pairs={{0,4},{4,0},{8,12},{12,8},{1,5},{5,1},{9,13},{13,9},{2,6},{6,2},{1... | collective-permute-start | bytes 110600 | tf_op jit(solution)/shard_map/ppermute | solution.py:669
  9.6 2.6 %collective-permute-start.1 = (bf16[3,24,256]{2,1,0:T(8,128)(2,1)S(1)}, bf16[3,24,256]{2,1,0:T(8,128)(2,1)S(1)}, u32[]{:S(2)}, u32[]{:S(2)}) collective-permute-start(bf16[3,24,256]{2,1,0:T(8,128)(2,1)S(1)} %get-tuple-element.37), channel_id=1, source_target_pairs={{0,8},{4,12},{8,0},{12,4},{1,9},{5,13},{9,1},{13,5},{2,10},{6,14},... | collective-permute-start | bytes 110600 | tf_op jit(solution)/shard_map/ppermute | solution.py:669
  12.3 5.0 %edges.1 = (f32[64,16384]{1,0:T(8,128)S(1)}, bf16[4,64,128]{2,1,0:T(8,128)(2,1)S(1)}, bf16[2,64,128]{2,1,0:T(8,128)(2,1)S(1)}, bf16[192,192]{1,0:T(8,128)(2,1)S(...) custom-call(bf16[64,16384]{1,0:T(8,128)(2,1)S(1)} %bitcast.11, bf16[64,16384]{1,0:T(8,128)(2,1)S(1)} %bitcast.12, ...), custom_call_target="tpu_custom_call" | custom-call | flops 1207959552 | bytes 6291456 | tf_op jit(solution)/shard_map/edges/pallas_call | solution.py:708
  17.2 0.7 %collective-permute-done.2.rest_3_ = bf16[3,24,256]{2,1,0:T(8,128)(2,1)S(1)} collective-permute-done((bf16[3,24,256]{2,1,0:T(8,128)(2,1)S(1)}, bf16[3,24,256]{2,1,0:T(8,128)(2,1)S(1)}, u32[]{:S(2)}, u32[]{:S(2)}) %collective-permute-start.2) | collective-permute-done | bytes 36896 | tf_op jit(solution)/shard_map/ppermute | solution.py:669
  18.0 1.3 %strips.1 = (bf16[96,128]{1,0:T(8,128)(2,1)S(1)}, bf16[96,128]{1,0:T(8,128)(2,1)S(1)}, bf16[96,128]{1,0:T(8,128)(2,1)S(1)}, bf16[288,256]{1,0:T(8,128)(2,1)S(1)}...) custom-call(s32[3]{0:T(128)S(1)} %pad_add_fusion.scal.refs_0_, s32[4,4]{1,0:T(4,128)S(1)} %copy-done.3, ...), custom_call_target="tpu_custom_call" | custom-call | flops 150994944 | bytes 163840 | tf_op jit(solution)/shard_map/strips/pallas_call | solution.py:741
  19.5 3.5 %collective-permute-start.4 = (bf16[96,128]{1,0:T(8,128)(2,1)S(1)}, bf16[96,128]{1,0:T(8,128)(2,1)S(1)}, u32[]{:S(2)}, u32[]{:S(2)}) collective-permute-start(bf16[96,128]{1,0:T(8,128)(2,1)S(1)} %get-tuple-element.43), channel_id=1, source_target_pairs={{0,8},{4,12},{8,0},{12,4},{1,9},{5,13},{9,1},{13,5},{2,10},{6,14},... | collective-permute-start | bytes 73736 | tf_op jit(solution)/shard_map/ppermute | solution.py:669
  23.0 0.7 %collective-permute-start.5 = (bf16[96,128]{1,0:T(8,128)(2,1)S(1)}, bf16[96,128]{1,0:T(8,128)(2,1)S(1)}, u32[]{:S(2)}, u32[]{:S(2)}) collective-permute-start(bf16[96,128]{1,0:T(8,128)(2,1)S(1)} %get-tuple-element.44), channel_id=1, source_target_pairs={{0,12},{4,8},{8,4},{12,0},{1,13},{5,9},{9,5},{13,1},{2,14},{6,10},... | collective-permute-start | bytes 73736 | tf_op jit(solution)/shard_map/ppermute | solution.py:669
  23.7 3.0 %recv_pick.1.refs_9_ = f32[8,16384]{1,0:T(8,128)S(1)} custom-call(s32[128,128]{1,0:T(8,128)S(1)} %bitcast.23, bf16[288,256]{1,0:T(8,128)(2,1)S(1)} %get-tuple-element.45.source), custom_call_target="tpu_custom_call" | custom-call | flops 2415919104 | bytes 262144 | tf_op jit(solution)/shard_map/recv_pick/pallas_call | solution.py:755
  26.8 1.9 %collective-permute-done.5.refs_8_ = bf16[96,128]{1,0:T(8,128)(2,1)S(1)} collective-permute-done((bf16[96,128]{1,0:T(8,128)(2,1)S(1)}, bf16[96,128]{1,0:T(8,128)(2,1)S(1)}, u32[]{:S(2)}, u32[]{:S(2)}) %collective-permute-start.5) | collective-permute-done | bytes 24608 | tf_op jit(solution)/shard_map/ppermute | solution.py:669
  28.6 8.9 %middle.1 = (bf16[64,16384]{1,0:T(8,128)(2,1)S(1)}, bf16[64,16384]{1,0:T(8,128)(2,1)}, bf16[4,64,128]{2,1,0:T(8,128)(2,1)S(1)}, f32[48,256]{1,0:T(8,128)S(1)}, f...) custom-call(s32[3]{0:T(128)S(1)} %pad_add_fusion.scal.refs_0_, s32[4,4]{1,0:T(4,128)S(1)} %copy-done.3, ...), custom_call_target="tpu_custom_call" | custom-call | flops 1207959552 | bytes 12582912 | tf_op jit(solution)/shard_map/middle/pallas_call | solution.py:782
  37.5 1.5 %collective-permute-start.7 = (f32[48,256]{1,0:T(8,128)S(1)}, f32[48,256]{1,0:T(8,128)S(1)}, u32[]{:S(2)}, u32[]{:S(2)}) collective-permute-start(f32[48,256]{1,0:T(8,128)S(1)} %get-tuple-element.54), channel_id=1, source_target_pairs={{0,2},{1,3},{2,0},{3,1},{4,6},{5,7},{6,4},{7,5},{8,10},{9,11},{10,... | collective-permute-start | bytes 147464 | tf_op jit(solution)/shard_map/ppermute | solution.py:868
  39.0 0.6 %collective-permute-start.6 = (f32[48,256]{1,0:T(8,128)S(1)}, f32[48,256]{1,0:T(8,128)S(1)}, u32[]{:S(2)}, u32[]{:S(2)}) collective-permute-start(f32[48,256]{1,0:T(8,128)S(1)} %get-tuple-element.53.rest_0_), channel_id=1, source_target_pairs={{0,1},{1,0},{2,3},{3,2},{4,5},{5,4},{6,7},{7,6},{8,9},{9,8},{10,11... | collective-permute-start | bytes 147464 | tf_op jit(solution)/shard_map/ppermute | solution.py:868
  39.6 2.7 %output.3 = (bf16[64,16384]{1,0:T(8,128)(2,1)}, f32[8,128]{1,0:T(8,128)S(1)}) custom-call(bf16[64,16384]{1,0:T(8,128)(2,1)S(1)} %get-tuple-element.49.hid.prev.nxt, bf16[64,16384]{1,0:T(8,128)(2,1)S(1)} %get-tuple-element.49.hid.prev.nxt, bf16[64,16384]{1,0:T(8,128)(2,1)S(1)} %get-tuple-element.49.hid.prev.nxt, ...), custom_call_target="tpu_custom_call" | custom-call | flops 603979776 | bytes 2097152 | tf_op jit(solution)/shard_map/output/pallas_call | solution.py:848
  42.6 1.4 %collective-permute-start.11 = (f32[48,256]{1,0:T(8,128)S(1)}, f32[48,256]{1,0:T(8,128)S(1)}, u32[]{:S(2)}, u32[]{:S(2)}) collective-permute-start(f32[48,256]{1,0:T(8,128)S(1)} %add.5.rest_0_.mine), channel_id=1, source_target_pairs={{0,12},{4,8},{8,4},{12,0},{1,13},{5,9},{9,5},{13,1},{2,14},{6,10},... | collective-permute-start | bytes 147464 | tf_op jit(solution)/shard_map/ppermute | solution.py:669
  44.0 3.1 %collective-permute-start.9 = (f32[48,256]{1,0:T(8,128)S(1)}, f32[48,256]{1,0:T(8,128)S(1)}, u32[]{:S(2)}, u32[]{:S(2)}) collective-permute-start(f32[48,256]{1,0:T(8,128)S(1)} %add.5.rest_0_.mine), channel_id=1, source_target_pairs={{0,4},{4,0},{8,12},{12,8},{1,5},{5,1},{9,13},{13,9},{2,6},{6,2},{1... | collective-permute-start | bytes 147464 | tf_op jit(solution)/shard_map/ppermute | solution.py:669
  47.1 1.7 %output.4 = (bf16[64,16384]{1,0:T(8,128)(2,1)}, f32[8,128]{1,0:T(8,128)S(1)}) custom-call(bf16[64,16384]{1,0:T(8,128)(2,1)S(1)} %get-tuple-element.49.hid.prev.nxt, bf16[64,16384]{1,0:T(8,128)(2,1)S(1)} %get-tuple-element.49.hid.prev.nxt, bf16[64,16384]{1,0:T(8,128)(2,1)S(1)} %get-tuple-element.49.hid.prev.nxt, ...), custom_call_target="tpu_custom_call", output_to_operand_aliasing={{0}: (6, {})} | custom-call | flops 301989888 | bytes 1048576 | tf_op jit(solution)/shard_map/output/pallas_call | solution.py:848
  49.1 0.9 %collective-permute-done.10.rest_1_ = f32[48,256]{1,0:T(8,128)S(1)} collective-permute-done((f32[48,256]{1,0:T(8,128)S(1)}, f32[48,256]{1,0:T(8,128)S(1)}, u32[]{:S(2)}, u32[]{:S(2)}) %collective-permute-start.10) | collective-permute-done | bytes 49184 | tf_op jit(solution)/shard_map/ppermute | solution.py:669
  50.5 1.3 %collective-permute-start.14 = (f32[48,256]{1,0:T(8,128)S(1)}, f32[48,256]{1,0:T(8,128)S(1)}, u32[]{:S(2)}, u32[]{:S(2)}) collective-permute-start(f32[48,256]{1,0:T(8,128)S(1)} %ring.1.rest_0_.mine), channel_id=1, source_target_pairs={{0,3},{1,2},{2,1},{3,0},{4,7},{5,6},{6,5},{7,4},{8,11},{9,10},{10,... | collective-permute-start | bytes 147464 | tf_op jit(solution)/shard_map/ppermute | solution.py:868
  52.5 1.7 %output.5 = (bf16[64,16384]{1,0:T(8,128)(2,1)}, f32[8,128]{1,0:T(8,128)}) custom-call(bf16[64,16384]{1,0:T(8,128)(2,1)S(1)} %get-tuple-element.49.hid.prev.nxt, bf16[64,16384]{1,0:T(8,128)(2,1)S(1)} %get-tuple-element.49.hid.prev.nxt, bf16[64,16384]{1,0:T(8,128)(2,1)S(1)} %get-tuple-element.49.hid.prev.nxt, ...), custom_call_target="tpu_custom_call", output_to_operand_aliasing={{0}: (6, {})} | custom-call | flops 301989888 | bytes 1048576 | tf_op jit(solution)/shard_map/output/pallas_call | solution.py:848
  54.5 1.4 %collective-permute-done.13.two = f32[48,256]{1,0:T(8,128)S(1)} collective-permute-done((f32[48,256]{1,0:T(8,128)S(1)}, f32[48,256]{1,0:T(8,128)S(1)}, u32[]{:S(2)}, u32[]{:S(2)}) %collective-permute-start.13) | collective-permute-done | bytes 49184 | tf_op jit(solution)/shard_map/ppermute | solution.py:868
  55.9 1.4 %last.1 = (f32[9,3,64]{2,1,0:T(4,128)}, f32[9,64,64]{2,1,0:T(8,128)}) custom-call(s32[3]{0:T(128)S(1)} %pad_add_fusion.scal.refs_0_, f32[48,256]{1,0:T(8,128)S(1)} %ring.1.rest_0_.mine, f32[48,256]{1,0:T(8,128)S(1)} %collective-permute-done.12.one, f32[48,256]{1,0:T(8,128)S(1)} %collective-permute-done.13.two, f32[48,256]{1,0:T(8,128)S(1)} %collective-permute-done.14.three), custom_call_target="tpu_custom_call" | custom-call | flops 1000 | bytes 786432 | tf_op jit(solution)/shard_map/last/pallas_call | solution.py:892
  (34 shorter events, 2.7 us)
Async XLA Ops:
  0.7 0.9 %copy-start.5 = (bf16[1,3,16384]{2,1,0:T(4,128)(2,1)S(1)}, bf16[1,3,16384]{2,1,0:T(4,128)(2,1)}, u32[]{:S(2)}) copy-start(bf16[1,3,16384]{2,1,0:T(4,128)(2,1)} %param.8) | copy-start | bytes 294916
  1.6 0.9 %copy-start.6 = (s32[24576]{0:T(1024)S(1)}, s32[24576]{0:T(1024)}, u32[]{:S(2)}) copy-start(s32[24576]{0:T(1024)} %param.9) | copy-start | bytes 294916
  2.5 9.7 %copy-start = (bf16[1,64,16384]{2,1,0:T(8,128)(2,1)S(1)}, bf16[1,64,16384]{2,1,0:T(8,128)(2,1)}, u32[]{:S(2)}) copy-start(bf16[1,64,16384]{2,1,0:T(8,128)(2,1)} %param.15) | copy-start | bytes 6291460
  2.5 9.7 %copy-start.1 = (bf16[9,64,64]{2,1,0:T(8,128)(2,1)S(1)}, bf16[9,64,64]{2,1,0:T(8,128)(2,1)}, u32[]{:S(2)}) copy-start(bf16[9,64,64]{2,1,0:T(8,128)(2,1)} %conv_second.1) | copy-start | bytes 221188
  2.5 9.7 %copy-start.2 = (bf16[9,64,3]{1,2,0:T(4,128)(2,1)S(1)}, bf16[9,64,3]{1,2,0:T(4,128)(2,1)}, u32[]{:S(2)}) copy-start(bf16[9,64,3]{1,2,0:T(4,128)(2,1)} %param.13) | copy-start | bytes 10372
  6.5 10.7 %collective-permute-start = (bf16[3,24,256]{2,1,0:T(8,128)(2,1)S(1)}, bf16[3,24,256]{2,1,0:T(8,128)(2,1)S(1)}, u32[]{:S(2)}, u32[]{:S(2)}) collective-permute-start(bf16[3,24,256]{2,1,0:T(8,128)(2,1)S(1)} %get-tuple-element.36), channel_id=1, source_target_pairs={{0,4},{4,0},{8,12},{12,8},{1,5},{5,1},{9,13},{13,9},{2,6},{6,2},{1... | collective-permute-start | bytes 110600 | tf_op jit(solution)/shard_map/ppermute | solution.py:669
  9.6 7.6 %collective-permute-start.1 = (bf16[3,24,256]{2,1,0:T(8,128)(2,1)S(1)}, bf16[3,24,256]{2,1,0:T(8,128)(2,1)S(1)}, u32[]{:S(2)}, u32[]{:S(2)}) collective-permute-start(bf16[3,24,256]{2,1,0:T(8,128)(2,1)S(1)} %get-tuple-element.37), channel_id=1, source_target_pairs={{0,8},{4,12},{8,0},{12,4},{1,9},{5,13},{9,1},{13,5},{2,10},{6,14},... | collective-permute-start | bytes 110600 | tf_op jit(solution)/shard_map/ppermute | solution.py:669
  12.2 5.8 %collective-permute-start.2 = (bf16[3,24,256]{2,1,0:T(8,128)(2,1)S(1)}, bf16[3,24,256]{2,1,0:T(8,128)(2,1)S(1)}, u32[]{:S(2)}, u32[]{:S(2)}) collective-permute-start(bf16[3,24,256]{2,1,0:T(8,128)(2,1)S(1)} %get-tuple-element.38), channel_id=1, source_target_pairs={{0,12},{4,8},{8,4},{12,0},{1,13},{5,9},{9,5},{13,1},{2,14},{6,10},... | collective-permute-start | bytes 110600 | tf_op jit(solution)/shard_map/ppermute | solution.py:669
  12.2 5.7 %copy-start.3 = (s32[4,4]{1,0:T(4,128)S(1)}, s32[4,4]{1,0:T(4,128)}, u32[]{:S(2)}) copy-start(s32[4,4]{1,0:T(4,128)} %refs_1_.1) | copy-start | bytes 196
  12.2 5.7 %copy-start.4 = (s32[4,4]{1,0:T(4,128)S(1)}, s32[4,4]{1,0:T(4,128)}, u32[]{:S(2)}) copy-start(s32[4,4]{1,0:T(4,128)} %refs_2_.1) | copy-start | bytes 196
  12.2 5.7 %copy-start.7 = (s32[16384]{0:T(1024)S(1)}, s32[16384]{0:T(1024)}, u32[]{:S(2)}) copy-start(s32[16384]{0:T(1024)} %param.10) | copy-start | bytes 196612
  19.2 7.5 %collective-permute-start.3 = (bf16[96,128]{1,0:T(8,128)(2,1)S(1)}, bf16[96,128]{1,0:T(8,128)(2,1)S(1)}, u32[]{:S(2)}, u32[]{:S(2)}) collective-permute-start(bf16[96,128]{1,0:T(8,128)(2,1)S(1)} %get-tuple-element.42), channel_id=1, source_target_pairs={{0,4},{4,0},{8,12},{12,8},{1,5},{5,1},{9,13},{13,9},{2,6},{6,2},{1... | collective-permute-start | bytes 73736 | tf_op jit(solution)/shard_map/ppermute | solution.py:669
  19.5 7.2 %collective-permute-start.4 = (bf16[96,128]{1,0:T(8,128)(2,1)S(1)}, bf16[96,128]{1,0:T(8,128)(2,1)S(1)}, u32[]{:S(2)}, u32[]{:S(2)}) collective-permute-start(bf16[96,128]{1,0:T(8,128)(2,1)S(1)} %get-tuple-element.43), channel_id=1, source_target_pairs={{0,8},{4,12},{8,0},{12,4},{1,9},{5,13},{9,1},{13,5},{2,10},{6,14},... | collective-permute-start | bytes 73736 | tf_op jit(solution)/shard_map/ppermute | solution.py:669
  23.0 5.6 %collective-permute-start.5 = (bf16[96,128]{1,0:T(8,128)(2,1)S(1)}, bf16[96,128]{1,0:T(8,128)(2,1)S(1)}, u32[]{:S(2)}, u32[]{:S(2)}) collective-permute-start(bf16[96,128]{1,0:T(8,128)(2,1)S(1)} %get-tuple-element.44), channel_id=1, source_target_pairs={{0,12},{4,8},{8,4},{12,0},{1,13},{5,9},{9,5},{13,1},{2,14},{6,10},... | collective-permute-start | bytes 73736 | tf_op jit(solution)/shard_map/ppermute | solution.py:669
  37.5 4.8 %collective-permute-start.7 = (f32[48,256]{1,0:T(8,128)S(1)}, f32[48,256]{1,0:T(8,128)S(1)}, u32[]{:S(2)}, u32[]{:S(2)}) collective-permute-start(f32[48,256]{1,0:T(8,128)S(1)} %get-tuple-element.54), channel_id=1, source_target_pairs={{0,2},{1,3},{2,0},{3,1},{4,6},{5,7},{6,4},{7,5},{8,10},{9,11},{10,... | collective-permute-start | bytes 147464 | tf_op jit(solution)/shard_map/ppermute | solution.py:868
  39.0 3.6 %collective-permute-start.8 = (f32[48,256]{1,0:T(8,128)S(1)}, f32[48,256]{1,0:T(8,128)S(1)}, u32[]{:S(2)}, u32[]{:S(2)}) collective-permute-start(f32[48,256]{1,0:T(8,128)S(1)} %get-tuple-element.55), channel_id=1, source_target_pairs={{0,3},{1,2},{2,1},{3,0},{4,7},{5,6},{6,5},{7,4},{8,11},{9,10},{10,... | collective-permute-start | bytes 147464 | tf_op jit(solution)/shard_map/ppermute | solution.py:868
  39.0 3.6 %collective-permute-start.6 = (f32[48,256]{1,0:T(8,128)S(1)}, f32[48,256]{1,0:T(8,128)S(1)}, u32[]{:S(2)}, u32[]{:S(2)}) collective-permute-start(f32[48,256]{1,0:T(8,128)S(1)} %get-tuple-element.53.rest_0_), channel_id=1, source_target_pairs={{0,1},{1,0},{2,3},{3,2},{4,5},{5,4},{6,7},{7,6},{8,9},{9,8},{10,11... | collective-permute-start | bytes 147464 | tf_op jit(solution)/shard_map/ppermute | solution.py:868
  42.6 6.4 %collective-permute-start.11 = (f32[48,256]{1,0:T(8,128)S(1)}, f32[48,256]{1,0:T(8,128)S(1)}, u32[]{:S(2)}, u32[]{:S(2)}) collective-permute-start(f32[48,256]{1,0:T(8,128)S(1)} %add.5.rest_0_.mine), channel_id=1, source_target_pairs={{0,12},{4,8},{8,4},{12,0},{1,13},{5,9},{9,5},{13,1},{2,14},{6,10},... | collective-permute-start | bytes 147464 | tf_op jit(solution)/shard_map/ppermute | solution.py:669
  44.0 5.9 %collective-permute-start.10 = (f32[48,256]{1,0:T(8,128)S(1)}, f32[48,256]{1,0:T(8,128)S(1)}, u32[]{:S(2)}, u32[]{:S(2)}) collective-permute-start(f32[48,256]{1,0:T(8,128)S(1)} %add.5.rest_0_.mine), channel_id=1, source_target_pairs={{0,8},{4,12},{8,0},{12,4},{1,9},{5,13},{9,1},{13,5},{2,10},{6,14},... | collective-permute-start | bytes 147464 | tf_op jit(solution)/shard_map/ppermute | solution.py:669
  44.0 5.9 %collective-permute-start.9 = (f32[48,256]{1,0:T(8,128)S(1)}, f32[48,256]{1,0:T(8,128)S(1)}, u32[]{:S(2)}, u32[]{:S(2)}) collective-permute-start(f32[48,256]{1,0:T(8,128)S(1)} %add.5.rest_0_.mine), channel_id=1, source_target_pairs={{0,4},{4,0},{8,12},{12,8},{1,5},{5,1},{9,13},{13,9},{2,6},{6,2},{1... | collective-permute-start | bytes 147464 | tf_op jit(solution)/shard_map/ppermute | solution.py:669
  50.5 4.0 %collective-permute-start.14 = (f32[48,256]{1,0:T(8,128)S(1)}, f32[48,256]{1,0:T(8,128)S(1)}, u32[]{:S(2)}, u32[]{:S(2)}) collective-permute-start(f32[48,256]{1,0:T(8,128)S(1)} %ring.1.rest_0_.mine), channel_id=1, source_target_pairs={{0,3},{1,2},{2,1},{3,0},{4,7},{5,6},{6,5},{7,4},{8,11},{9,10},{10,... | collective-permute-start | bytes 147464 | tf_op jit(solution)/shard_map/ppermute | solution.py:868
  51.8 4.1 %collective-permute-start.13 = (f32[48,256]{1,0:T(8,128)S(1)}, f32[48,256]{1,0:T(8,128)S(1)}, u32[]{:S(2)}, u32[]{:S(2)}) collective-permute-start(f32[48,256]{1,0:T(8,128)S(1)} %ring.1.rest_0_.mine), channel_id=1, source_target_pairs={{0,2},{1,3},{2,0},{3,1},{4,6},{5,7},{6,4},{7,5},{8,10},{9,11},{10,... | collective-permute-start | bytes 147464 | tf_op jit(solution)/shard_map/ppermute | solution.py:868
  52.2 3.7 %collective-permute-start.12 = (f32[48,256]{1,0:T(8,128)S(1)}, f32[48,256]{1,0:T(8,128)S(1)}, u32[]{:S(2)}, u32[]{:S(2)}) collective-permute-start(f32[48,256]{1,0:T(8,128)S(1)} %ring.1.rest_0_.mine), channel_id=1, source_target_pairs={{0,1},{1,0},{2,3},{3,2},{4,5},{5,4},{6,7},{7,6},{8,9},{9,8},{10,11... | collective-permute-start | bytes 147464 | tf_op jit(solution)/shard_map/ppermute | solution.py:868
